TPU v7x, 32 devices: a whole 2x2x4 slice. The times are simulated.
32 devices in a mesh: dp: 2 (over y), ctx: 4 (over z), tp: 4 (over x, core).
Axes of the slice: x: 2, y: 2, z: 4, core: 2. Of those that a mesh axis runs over, the one named last changes fastest.
Arguments:
- tokens: bfloat16 [16, 1024, 768], P('dp', 'ctx'), may hold values from -6 to 6
- out_grad: bfloat16 [16, 1024, 768], P('dp', 'ctx'), may hold values from -6 to 6
- query_weight: bfloat16 [768, 768], P(('dp', 'ctx'), 'tp'), may hold values from -0.21875 to 0.21875
- key_weight: bfloat16 [768, 768], P(('dp', 'ctx'), 'tp'), may hold values from -0.21875 to 0.21875
- value_weight: bfloat16 [768, 768], P(('dp', 'ctx'), 'tp'), may hold values from -0.21875 to 0.21875
- output_weight: bfloat16 [768, 768], P(('dp', 'ctx'), 'tp'), may hold values from -4 to 4
- up_weight: bfloat16 [768, 3072], P(('dp', 'ctx'), 'tp'), may hold values from -0.21875 to 0.21875
- down_weight: bfloat16 [768, 3072], P(('dp', 'ctx'), 'tp'), may hold values from -0.109375 to 0.109375
- norm1_gain: bfloat16 [768], P(('dp', 'ctx')), may hold values from 0.5 to 1.5
- norm1_bias: bfloat16 [768], P(('dp', 'ctx')), may hold values from -4 to 4
- output_bias: bfloat16 [768], P(('dp', 'ctx')), may hold values from -4 to 4
- norm2_gain: bfloat16 [768], P(('dp', 'ctx')), may hold values from 0.5 to 1.5
- norm2_bias: bfloat16 [768], P(('dp', 'ctx')), may hold values from -4 to 4
- down_bias: bfloat16 [768], P(('dp', 'ctx')), may hold values from -4 to 4
- query_bias: bfloat16 [768], P('tp'), may hold values from -1.5 to 1.5
- value_bias: bfloat16 [768], P('tp'), may hold values from -0.75 to 0.75
- up_bias: bfloat16 [3072], P('tp'), may hold values from -6 to 6
Outputs:
- layer_out: bfloat16 [16, 1024, 768], P('dp', 'ctx')
- tokens_grad: float32 [16, 1024, 768], P('dp', 'ctx')
- query_weight_grad: float32 [768, 768], P(('dp', 'ctx'), 'tp')
- key_weight_grad: float32 [768, 768], P(('dp', 'ctx'), 'tp')
- value_weight_grad: float32 [768, 768], P(('dp', 'ctx'), 'tp')
- output_weight_grad: float32 [768, 768], P(('dp', 'ctx'), 'tp')
- up_weight_grad: float32 [768, 3072], P(('dp', 'ctx'), 'tp')
- down_weight_grad: float32 [768, 3072], P(('dp', 'ctx'), 'tp')
- norm1_gain_grad: float32 [768], P(('dp', 'ctx'))
- norm1_bias_grad: float32 [768], P(('dp', 'ctx'))
- output_bias_grad: float32 [768], P(('dp', 'ctx'))
- norm2_gain_grad: float32 [768], P(('dp', 'ctx'))
- norm2_bias_grad: float32 [768], P(('dp', 'ctx'))
- down_bias_grad: float32 [768], P(('dp', 'ctx'))
- query_bias_grad: float32 [768], P('tp')
- value_bias_grad: float32 [768], P('tp')
- up_bias_grad: float32 [3072], P('tp')
All inputs are finite; a program needn't handle non-finite values.
Results may differ from a plain program's by a relative error of at most 0.011.
Values may be sent and summed in bfloat16 or wider, within the bound.
A program may use at most 192 MiB of HBM per device.

v0:
```python
import jax
import jax.numpy as jnp
from jax import lax
from jax.sharding import PartitionSpec as P

HEAD_DIM = 64
MICRO = 2


epsilon = 1e-05
root_half = 0.7071067811865476
density_scale = 0.3989422804014327


def normalize(values):
    centred = values - jnp.mean(values, axis=-1, keepdims=True)
    spread = lax.rsqrt(jnp.mean(centred * centred, axis=-1, keepdims=True) + epsilon)
    return (centred * spread, spread)


def norm_back(grad_scaled, scaled, spread):
    inner_term = grad_scaled - jnp.mean(grad_scaled, axis=-1, keepdims=True)
    inner_term = inner_term - scaled * jnp.mean(grad_scaled * scaled, axis=-1, keepdims=True)
    return inner_term * spread


def gelu_slope(upward):
    return 0.5 * (1.0 + lax.erf(upward * root_half)) + upward * density_scale * jnp.exp(
        -0.5 * upward * upward
    )


def plain_product(left_side, right_side):
    return jnp.dot(left_side, right_side, preferred_element_type=jnp.float32)


def times_transposed(left_side, right_side):
    return jnp.einsum("tc,dc->td", left_side, right_side, preferred_element_type=jnp.float32)


def contract_rows(left_side, right_side):
    return jnp.einsum("ta,tb->ab", left_side, right_side, preferred_element_type=jnp.float32)


def project_heads(rows, weight_heads):
    return jnp.einsum("sqc,che->sheq", rows, weight_heads, preferred_element_type=jnp.float32)


def heads_to_rows(heads, weight_heads):
    return jnp.einsum("sheq,che->sqc", heads, weight_heads, preferred_element_type=jnp.float32)


def heads_weight_grad(rows, heads):
    grad = jnp.einsum("sqc,sheq->che", rows, heads, preferred_element_type=jnp.float32)
    return grad.reshape(grad.shape[0], grad.shape[1] * grad.shape[2])


def add_pairs(left_tuple, right_tuple):
    return tuple((former + latter for former, latter in zip(left_tuple, right_tuple)))


def gather_forward(shards):
    return (
        lax.all_gather(shards[0], ("dp", "ctx"), axis=0, tiled=True),
        lax.all_gather(shards[1], ("dp", "ctx"), axis=0, tiled=True),
        lax.all_gather(shards[2], ("dp", "ctx"), axis=0, tiled=True),
        lax.all_gather(shards[3], ("dp", "ctx"), axis=0, tiled=True),
        lax.all_gather(shards[4], ("dp", "ctx"), axis=0, tiled=True),
        lax.all_gather(shards[5], ("dp", "ctx"), axis=0, tiled=True),
        lax.all_gather(shards[6], ("dp", "ctx"), axis=0, tiled=True),
        lax.all_gather(shards[7], ("dp", "ctx"), axis=0, tiled=True),
        lax.all_gather(shards[8], ("dp", "ctx"), axis=0, tiled=True),
        lax.all_gather(shards[9], ("dp", "ctx"), axis=0, tiled=True),
        lax.all_gather(shards[10], ("dp", "ctx"), axis=0, tiled=True),
        lax.all_gather(shards[11], ("dp", "ctx"), axis=0, tiled=True),
    )


def gather_backward(shards):
    return (
        lax.all_gather(shards[0], ("dp", "ctx"), axis=0, tiled=True),
        lax.all_gather(shards[1], ("dp", "ctx"), axis=0, tiled=True),
        lax.all_gather(shards[2], ("dp", "ctx"), axis=0, tiled=True),
        lax.all_gather(shards[3], ("dp", "ctx"), axis=0, tiled=True),
        lax.all_gather(shards[4], ("dp", "ctx"), axis=0, tiled=True),
        lax.all_gather(shards[5], ("dp", "ctx"), axis=0, tiled=True),
        lax.all_gather(shards[6], ("dp", "ctx"), axis=0, tiled=True),
        lax.all_gather(shards[7], ("dp", "ctx"), axis=0, tiled=True),
        lax.all_gather(shards[8], ("dp", "ctx"), axis=0, tiled=True),
        lax.all_gather(shards[9], ("dp", "ctx"), axis=0, tiled=True),
        lax.all_gather(shards[10], ("dp", "ctx"), axis=0, tiled=True),
        lax.all_gather(shards[11], ("dp", "ctx"), axis=0, tiled=True),
    )


def reduce_grads(grads_local):
    return (
        lax.psum_scatter(grads_local[0], ("dp", "ctx"), scatter_dimension=0, tiled=True),
        lax.psum_scatter(grads_local[1], ("dp", "ctx"), scatter_dimension=0, tiled=True),
        lax.psum_scatter(grads_local[2], ("dp", "ctx"), scatter_dimension=0, tiled=True),
        lax.psum_scatter(grads_local[3], ("dp", "ctx"), scatter_dimension=0, tiled=True),
        lax.psum_scatter(grads_local[4], ("dp", "ctx"), scatter_dimension=0, tiled=True),
        lax.psum_scatter(grads_local[5], ("dp", "ctx"), scatter_dimension=0, tiled=True),
        lax.psum_scatter(grads_local[6], ("dp", "ctx"), scatter_dimension=0, tiled=True),
        lax.psum_scatter(grads_local[7], ("dp", "ctx"), scatter_dimension=0, tiled=True),
        lax.psum_scatter(grads_local[8], ("dp", "ctx"), scatter_dimension=0, tiled=True),
        lax.psum_scatter(grads_local[9], ("dp", "ctx"), scatter_dimension=0, tiled=True),
        lax.psum_scatter(grads_local[10], ("dp", "ctx"), scatter_dimension=0, tiled=True),
        lax.psum_scatter(grads_local[11], ("dp", "ctx"), scatter_dimension=0, tiled=True),
    )


def forward_pass(block_tokens, gathered, column_bias, allowed):
    (
        full_query,
        full_key,
        full_value,
        full_output,
        full_up,
        full_down,
        gain_one,
        shift_one,
        out_shift,
        gain_two,
        shift_two,
        down_shift,
    ) = gathered
    seq_micro, block_len, model_width = block_tokens.shape
    row_count = seq_micro * block_len
    local_width = full_query.shape[1]
    local_heads = local_width // HEAD_DIM
    score_scale = HEAD_DIM ** (-0.5)
    query_heads_w = full_query.reshape(model_width, local_heads, HEAD_DIM)
    key_heads_w = full_key.reshape(model_width, local_heads, HEAD_DIM)
    value_heads_w = full_value.reshape(model_width, local_heads, HEAD_DIM)
    output_heads_w = full_output.reshape(model_width, local_heads, HEAD_DIM)
    inputs = block_tokens.reshape(row_count, model_width).astype(jnp.float32)
    scaled_one, spread_one = normalize(inputs)
    normed_one = (scaled_one * gain_one.astype(jnp.float32) + shift_one.astype(jnp.float32)).astype(
        jnp.bfloat16
    )
    normed_seq = normed_one.reshape(seq_micro, block_len, model_width)
    query_shift = column_bias[0].reshape(1, local_heads, HEAD_DIM, 1)
    value_shift = column_bias[1].reshape(1, local_heads, HEAD_DIM, 1)
    query_heads = (project_heads(normed_seq, query_heads_w) + query_shift).astype(jnp.bfloat16)
    keys_local = project_heads(normed_seq, key_heads_w).astype(jnp.bfloat16)
    values_local = (project_heads(normed_seq, value_heads_w) + value_shift).astype(jnp.bfloat16)
    key_heads, value_heads = (
        lax.all_gather(keys_local, "ctx", axis=3, tiled=True),
        lax.all_gather(values_local, "ctx", axis=3, tiled=True),
    )
    scores = (
        jnp.einsum("sheq,shek->shqk", query_heads, key_heads, preferred_element_type=jnp.float32)
        * score_scale
    )
    scores = jnp.where(allowed, scores, -jnp.inf)
    largest = jnp.max(scores, axis=-1, keepdims=True)
    powers = jnp.exp(scores - largest)
    total_mass = jnp.sum(powers, axis=-1, keepdims=True)
    probabilities = (powers / total_mass).astype(jnp.bfloat16)
    log_mass = largest + jnp.log(total_mass)
    mixed_heads = jnp.einsum(
        "shqk,shek->sheq", probabilities, value_heads, preferred_element_type=jnp.float32
    ).astype(jnp.bfloat16)
    attn_total = lax.psum(
        heads_to_rows(mixed_heads, output_heads_w).reshape(row_count, model_width), "tp"
    )
    hidden = inputs + attn_total + out_shift.astype(jnp.float32)
    scaled_two, spread_two = normalize(hidden)
    normed_two = (scaled_two * gain_two.astype(jnp.float32) + shift_two.astype(jnp.float32)).astype(
        jnp.bfloat16
    )
    upward = plain_product(normed_two, full_up) + column_bias[2]
    activated = jax.nn.gelu(upward, approximate=False).astype(jnp.bfloat16)
    ffn_total = lax.psum(times_transposed(activated, full_down).astype(jnp.bfloat16), "tp").astype(
        jnp.float32
    )
    output = (hidden + ffn_total + down_shift.astype(jnp.float32)).astype(jnp.bfloat16)
    saved_state = (
        scaled_one,
        spread_one,
        normed_one,
        query_heads,
        key_heads,
        value_heads,
        log_mass,
        mixed_heads,
        scaled_two,
        spread_two,
        normed_two,
        upward,
        activated,
    )
    return (output.reshape(seq_micro, block_len, model_width), saved_state)


def backward_pass(block_grad, gathered, saved_state, allowed):
    (
        full_query,
        full_key,
        full_value,
        full_output,
        full_up,
        full_down,
        gain_one,
        shift_one,
        out_shift,
        gain_two,
        shift_two,
        down_shift,
    ) = gathered
    (
        scaled_one,
        spread_one,
        normed_one,
        query_heads,
        key_heads,
        value_heads,
        log_mass,
        mixed_heads,
        scaled_two,
        spread_two,
        normed_two,
        upward,
        activated,
    ) = saved_state
    seq_micro, block_len, model_width = block_grad.shape
    row_count = seq_micro * block_len
    local_width = full_query.shape[1]
    local_heads = local_width // HEAD_DIM
    score_scale = HEAD_DIM ** (-0.5)
    query_heads_w = full_query.reshape(model_width, local_heads, HEAD_DIM)
    key_heads_w = full_key.reshape(model_width, local_heads, HEAD_DIM)
    value_heads_w = full_value.reshape(model_width, local_heads, HEAD_DIM)
    output_heads_w = full_output.reshape(model_width, local_heads, HEAD_DIM)
    grad_rows = block_grad.reshape(row_count, model_width)
    grad_float = grad_rows.astype(jnp.float32)
    down_grad = contract_rows(grad_rows, activated)
    down_shift_grad = jnp.sum(grad_float, axis=0)
    slope_input = plain_product(grad_rows, full_down)
    up_grad_rows = (slope_input * gelu_slope(upward)).astype(jnp.bfloat16)
    up_bias_grad = jnp.sum(up_grad_rows.astype(jnp.float32), axis=0)
    up_grad = contract_rows(normed_two, up_grad_rows)
    normed_two_grad = lax.psum(times_transposed(up_grad_rows, full_up), "tp")
    gain_two_grad = jnp.sum(normed_two_grad * scaled_two, axis=0)
    shift_two_grad = jnp.sum(normed_two_grad, axis=0)
    hidden_grad = grad_float + norm_back(
        normed_two_grad * gain_two.astype(jnp.float32), scaled_two, spread_two
    )
    branch_grad = hidden_grad.astype(jnp.bfloat16)
    out_shift_grad = jnp.sum(branch_grad.astype(jnp.float32), axis=0)
    branch_seq = branch_grad.reshape(seq_micro, block_len, model_width)
    output_grad = heads_weight_grad(branch_seq, mixed_heads)
    mixed_grad = project_heads(branch_seq, output_heads_w).astype(jnp.bfloat16)
    scores = (
        jnp.einsum("sheq,shek->shqk", query_heads, key_heads, preferred_element_type=jnp.float32)
        * score_scale
    )
    scores = jnp.where(allowed, scores, -jnp.inf)
    softmax_out = jnp.exp(scores - log_mass)
    softmax_low = softmax_out.astype(jnp.bfloat16)
    prob_grad = jnp.einsum(
        "sheq,shek->shqk", mixed_grad, value_heads, preferred_element_type=jnp.float32
    )
    centre_term = jnp.sum(softmax_out * prob_grad, axis=-1, keepdims=True)
    score_grad = (softmax_out * (prob_grad - centre_term)).astype(jnp.bfloat16)
    query_grad = (
        jnp.einsum("shqk,shek->sheq", score_grad, key_heads, preferred_element_type=jnp.float32)
        * score_scale
    ).astype(jnp.bfloat16)
    key_terms = (
        jnp.einsum("shqk,sheq->shek", score_grad, query_heads, preferred_element_type=jnp.float32)
        * score_scale
    )
    value_terms = jnp.einsum(
        "shqk,sheq->shek", softmax_low, mixed_grad, preferred_element_type=jnp.float32
    )
    key_part, value_part = (
        lax.psum_scatter(key_terms, "ctx", scatter_dimension=3, tiled=True),
        lax.psum_scatter(value_terms, "ctx", scatter_dimension=3, tiled=True),
    )
    key_grad = key_part.astype(jnp.bfloat16)
    value_grad = value_part.astype(jnp.bfloat16)
    query_bias_grad = jnp.sum(query_grad.astype(jnp.float32), axis=(0, 3)).reshape(local_width)
    value_bias_grad = jnp.sum(value_grad.astype(jnp.float32), axis=(0, 3)).reshape(local_width)
    normed_seq = normed_one.reshape(seq_micro, block_len, model_width)
    query_w_grad = heads_weight_grad(normed_seq, query_grad)
    key_w_grad = heads_weight_grad(normed_seq, key_grad)
    value_w_grad = heads_weight_grad(normed_seq, value_grad)
    normed_part = (
        heads_to_rows(query_grad, query_heads_w)
        + heads_to_rows(key_grad, key_heads_w)
        + heads_to_rows(value_grad, value_heads_w)
    )
    normed_one_grad = lax.psum(normed_part.reshape(row_count, model_width), "tp")
    gain_one_grad = jnp.sum(normed_one_grad * scaled_one, axis=0)
    shift_one_grad = jnp.sum(normed_one_grad, axis=0)
    input_grad = hidden_grad + norm_back(
        normed_one_grad * gain_one.astype(jnp.float32), scaled_one, spread_one
    )
    micro_grads = (
        query_w_grad,
        key_w_grad,
        value_w_grad,
        output_grad,
        up_grad,
        down_grad,
        gain_one_grad,
        shift_one_grad,
        out_shift_grad,
        gain_two_grad,
        shift_two_grad,
        down_shift_grad,
    )
    bias_terms = (query_bias_grad, value_bias_grad, up_bias_grad)
    return (input_grad.reshape(seq_micro, block_len, model_width), micro_grads, bias_terms)


def per_device(
    tokens,
    out_grad,
    query_weight,
    key_weight,
    value_weight,
    output_weight,
    up_weight,
    down_weight,
    norm1_gain,
    norm1_bias,
    output_bias,
    norm2_gain,
    norm2_bias,
    down_bias,
    query_bias,
    value_bias,
    up_bias,
):
    shards = (
        query_weight,
        key_weight,
        value_weight,
        output_weight,
        up_weight,
        down_weight,
        norm1_gain,
        norm1_bias,
        output_bias,
        norm2_gain,
        norm2_bias,
        down_bias,
    )
    seq_count = tokens.shape[0]
    block_len = tokens.shape[1]
    seq_micro = seq_count // MICRO
    full_len = block_len * lax.axis_size("ctx")
    key_blocks = jnp.arange(full_len, dtype=jnp.int32) // block_len
    allowed = (key_blocks <= lax.axis_index("ctx"))[None, None, None, :]
    column_bias = (
        query_bias.astype(jnp.float32),
        value_bias.astype(jnp.float32),
        up_bias.astype(jnp.float32),
    )
    outputs = []
    input_grads = []
    for batch_index in range(MICRO):
        first_seq = batch_index * seq_micro
        forward_weights = gather_forward(shards)
        output, saved_state = forward_pass(
            tokens[first_seq : first_seq + seq_micro], forward_weights, column_bias, allowed
        )
        backward_weights = gather_backward(shards)
        input_grad, micro_grads, bias_terms = backward_pass(
            out_grad[first_seq : first_seq + seq_micro], backward_weights, saved_state, allowed
        )
        outputs.append(output)
        input_grads.append(input_grad)
        bias_sums = bias_terms if batch_index == 0 else add_pairs(bias_sums, bias_terms)
        reduced = reduce_grads(micro_grads)
        owned_sums = reduced if batch_index == 0 else add_pairs(owned_sums, reduced)
    bias_total = lax.psum((bias_sums[0], bias_sums[1], bias_sums[2]), ("dp", "ctx"))
    layer_out = jnp.concatenate(outputs, axis=0)
    tokens_grad = jnp.concatenate(input_grads, axis=0)
    return (
        layer_out,
        tokens_grad,
        owned_sums[0],
        owned_sums[1],
        owned_sums[2],
        owned_sums[3],
        owned_sums[4],
        owned_sums[5],
        owned_sums[6],
        owned_sums[7],
        owned_sums[8],
        owned_sums[9],
        owned_sums[10],
        owned_sums[11],
        bias_total[0],
        bias_total[1],
        bias_total[2],
    )


def solution(mesh):
    return jax.shard_map(
        per_device,
        mesh=mesh,
        in_specs=(
            P("dp", "ctx", None),
            P("dp", "ctx", None),
            P(("dp", "ctx"), "tp"),
            P(("dp", "ctx"), "tp"),
            P(("dp", "ctx"), "tp"),
            P(("dp", "ctx"), "tp"),
            P(("dp", "ctx"), "tp"),
            P(("dp", "ctx"), "tp"),
            P(("dp", "ctx")),
            P(("dp", "ctx")),
            P(("dp", "ctx")),
            P(("dp", "ctx")),
            P(("dp", "ctx")),
            P(("dp", "ctx")),
            P("tp"),
            P("tp"),
            P("tp"),
        ),
        out_specs=(
            P("dp", "ctx", None),
            P("dp", "ctx", None),
            P(("dp", "ctx"), "tp"),
            P(("dp", "ctx"), "tp"),
            P(("dp", "ctx"), "tp"),
            P(("dp", "ctx"), "tp"),
            P(("dp", "ctx"), "tp"),
            P(("dp", "ctx"), "tp"),
            P(("dp", "ctx")),
            P(("dp", "ctx")),
            P(("dp", "ctx")),
            P(("dp", "ctx")),
            P(("dp", "ctx")),
            P(("dp", "ctx")),
            P("tp"),
            P("tp"),
            P("tp"),
        ),
        check_vma=False,
    )
```

profile of v0, /device:TPU:25, one launch (start us, length us, event | category | flops | bytes accessed | tf_op | source)
XLA Modules:
  0.0 1377.4 jit_solution(13121506097369573926)
XLA Ops:
  15.2 25.9 %all-reduce.14 = (bf16[768]{0:T(1024)(128)(2,1)S(1)}, bf16[768]{0:T(1024)(128)(2,1)S(1)}, bf16[768]{0:T(1024)(128)(2,1)S(1)}, bf16[768]{0:T(1024)(128)(2,1)}, bf...) all-reduce(bf16[768]{0:T(1024)(128)(2,1)S(1)} %dynamic-update-slice, ...), channel_id=1, replica_groups=mesh['dp'=2,'ctx'=4,'tp'=4] {'dp','ctx'}, use_global_device_ids=true, to_apply=%add.1 | all-reduce | flops 4608 | bytes 18432
  45.9 29.0 %all_gather.37 = bf16[768,192]{1,0:T(8,128)(2,1)} all-gather(bf16[96,192]{1,0:T(8,128)(2,1)S(1)} %copy-done.44), channel_id=1, replica_groups=mesh['dp'=2,'ctx'=4,'tp'=4] {'dp','ctx'}, dimensions={0}, use_global_device_ids=true | all-gather | bytes 331776 | tf_op jit(solution)/shard_map/all_gather | solution.py:65
  80.3 32.4 %all_gather.34 = bf16[768,192]{1,0:T(8,128)(2,1)} all-gather(bf16[96,192]{1,0:T(8,128)(2,1)S(1)} %copy-done.45), channel_id=1, replica_groups=mesh['dp'=2,'ctx'=4,'tp'=4] {'dp','ctx'}, dimensions={0}, use_global_device_ids=true | all-gather | bytes 331776 | tf_op jit(solution)/shard_map/all_gather | solution.py:66
  115.8 31.7 %all_gather.36 = bf16[768,192]{1,0:T(8,128)(2,1)} all-gather(bf16[96,192]{1,0:T(8,128)(2,1)S(1)} %copy-done.46), channel_id=1, replica_groups=mesh['dp'=2,'ctx'=4,'tp'=4] {'dp','ctx'}, dimensions={0}, use_global_device_ids=true | all-gather | bytes 331776 | tf_op jit(solution)/shard_map/all_gather | solution.py:64
  152.0 31.8 %all_gather.39 = bf16[768,192]{1,0:T(8,128)(2,1)} all-gather(bf16[96,192]{1,0:T(8,128)(2,1)S(1)} %copy-done.47), channel_id=1, replica_groups=mesh['dp'=2,'ctx'=4,'tp'=4] {'dp','ctx'}, dimensions={0}, use_global_device_ids=true | all-gather | bytes 331776 | tf_op jit(solution)/shard_map/all_gather | solution.py:67
  188.3 8.0 fusion.12
  196.3 10.7 fusion
  207.1 11.1 all-gather.7.cloned.1.call-done
  218.1 6.8 fusion.125
  231.5 88.0 %all-reduce.23.cloned.1.call-done = f32[1024,768]{1,0:T(8,128)} async-done(((f32[1024,768]{1,0:T(8,128)}), f32[1024,768]{1,0:T(8,128)}) %all-reduce.23.cloned.1.call-update) | async-done | bytes 3145744 | tf_op jit(solution)/shard_map/psum | solution.py:165
  347.0 65.9 %all-reduce.27.cloned.1.call-done = f32[1024,768]{1,0:T(8,128)} async-done(((f32[1024,768]{1,0:T(8,128)}), f32[1024,768]{1,0:T(8,128)}) %all-reduce.27.cloned.1.call-update) | async-done | bytes 3145744 | tf_op jit(solution)/shard_map/psum | solution.py:244
  422.8 16.5 %multiply_reduce_fusion.1 = (f32[4,3,256]{2,1,0:T(4,128)S(1)}, f32[4,3,256]{2,1,0:T(4,128)S(1)}, f32[4,3,256,1024]{3,2,1,0:T(8,128)}) fusion(f32[4,3,256]{2,1,0:T(4,128)S(1)} %log_add_fusion.1, f32[4,3,256,1024]{3,2,1,0:T(8,128)} %get-tuple-element.150, pred[1024]{0:T(1024)(128)(4,1)S(1)} %fusion.146, f32[4,3,256]{2,1,0:T(4,128)S(1)} %get-tuple-element.95, ...), kind=kOutput, calls=%fused_computation.4 | convolution fusion | flops 430958592 | bytes 39764992 | tf_op jit(solution)/shard_map/sheq,shek->shqk/dot_general | solution.py:262
  439.2 11.5 all-gather.15.cloned.1.call-done
  450.7 6.8 fusion.124
  460.7 68.2 %all-reduce.25.cloned.1.call-done = f32[1024,768]{1,0:T(8,128)} async-done(((f32[1024,768]{1,0:T(8,128)}), f32[1024,768]{1,0:T(8,128)}) %all-reduce.25.cloned.1.call-update) | async-done | bytes 3145744 | tf_op jit(solution)/shard_map/psum | solution.py:165
  534.2 16.6 %fusion.16 = (bf16[1024,768]{1,0:T(8,128)(2,1)}, bf16[1024,768]{1,0:T(8,128)(2,1)}, f32[1024,768]{1,0:T(8,128)S(1)}) fusion(f32[1024,768]{1,0:T(8,128)S(1)} %copy-done.111, f32[768]{0:T(1024)S(1)} %copy-done.94, bf16[768,768]{1,0:T(8,128)(2,1)S(1)} %copy-done.107, f32[1024,768]{1,0:T(8,128)S(1)} %get-tuple-element.126, f32[1024]{0:T(1024)S(1)} %add_rsqrt_fusion, ...), kind=kOutput, calls=%fused_computation.31 | convolution fusion | flops 1315700736 | bytes 13779968 | tf_op jit(solution)/shard_map/dot_general | solution.py:34
  566.1 9.2 fusion.6
  576.0 51.2 %all-reduce.29.cloned.1.call-done = f32[1024,768]{1,0:T(8,128)} async-done(((f32[1024,768]{1,0:T(8,128)}), f32[1024,768]{1,0:T(8,128)}) %all-reduce.29.cloned.1.call-update) | async-done | bytes 3145744 | tf_op jit(solution)/shard_map/psum | solution.py:244
  631.4 67.4 %all-reduce.33.cloned.1.call-done = (bf16[1024,768]{1,0:T(8,128)(2,1)}, bf16[1024,768]{1,0:T(8,128)(2,1)}) async-done(((bf16[1024,768]{1,0:T(8,128)(2,1)}, bf16[1024,768]{1,0:T(8,128)(2,1)}), (bf16[1024,768]{1,0:T(8,128)(2,1)}, bf16[1024,768]{1,0:T(8,128)(2,1)})) %all-reduce.33.cloned.1.call-update) | async-done | bytes 3145744 | tf_op jit(solution)/shard_map/psum | solution.py:175
  698.8 7.5 convert_reduce_fusion.6
  710.6 7.7 multiply_reduce_fusion
  718.4 16.0 %multiply_convert_fusion.1 = (bf16[4,3,256,1024]{3,2,1,0:T(8,128)(2,1)S(1)}, bf16[4,3,256,1024]{3,2,1,0:T(8,128)(2,1)}) fusion(f32[4,3,256,1024]{3,2,1,0:T(8,128)} %get-tuple-element.152, f32[4,3,256]{2,1,0:T(4,128)S(1)} %get-tuple-element.92, f32[4,3,256]{2,1,0:T(4,128)S(1)} %log_add_fusion.1, f32[4,3,256,1024]{3,2,1,0:T(8,128)} %get-tuple-element.150, ...), kind=kLoop, calls=%fused_computation.3 | loop fusion | flops 37748736 | bytes 62964736 | tf_op jit(solution)/shard_map/convert_element_type | solution.py:266
  747.6 8.0 fusion.4
  775.2 48.1 %reduce-scatter.13.cloned.1.call-done = f32[4,3,64,256]{3,2,1,0:T(8,128)} async-done(((f32[4,3,64,1024]{3,2,1,0:T(8,128)}), f32[4,3,64,256]{3,2,1,0:T(8,128)}) %reduce-scatter.13.cloned.1.call-update) | async-done | bytes 786448 | tf_op jit(solution)/shard_map/reduce_scatter | solution.py:279
  825.2 61.2 %reduce-scatter.17.cloned.1.call-done = f32[4,3,64,256]{3,2,1,0:T(8,128)} async-done(((f32[4,3,64,1024]{3,2,1,0:T(8,128)}), f32[4,3,64,256]{3,2,1,0:T(8,128)}) %reduce-scatter.17.cloned.1.call-update) | async-done | bytes 786448 | tf_op jit(solution)/shard_map/reduce_scatter | solution.py:279
  892.2 56.8 %reduce-scatter.19.cloned.1.call-done = f32[4,3,64,256]{3,2,1,0:T(8,128)} async-done(((f32[4,3,64,1024]{3,2,1,0:T(8,128)}), f32[4,3,64,256]{3,2,1,0:T(8,128)}) %reduce-scatter.19.cloned.1.call-update) | async-done | bytes 786448 | tf_op jit(solution)/shard_map/reduce_scatter | solution.py:280
  1005.6 72.9 %all-reduce.31.cloned.1.call-done = (f32[1024,768]{1,0:T(8,128)}, f32[1024,768]{1,0:T(8,128)}) async-done(((f32[1024,768]{1,0:T(8,128)}, f32[1024,768]{1,0:T(8,128)}), (f32[1024,768]{1,0:T(8,128)}, f32[1024,768]{1,0:T(8,128)})) %all-reduce.31.cloned.1.call-update) | async-done | bytes 6291472 | tf_op jit(solution)/shard_map/psum | solution.py:295
  1083.3 27.3 %all-reduce.12 = (f32[768]{0:T(1024)S(1)}, f32[768]{0:T(1024)S(1)}, f32[768]{0:T(1024)S(1)}, f32[768]{0:T(1024)S(1)}, f32[768]{0:T(1024)S(1)}, /*index=5*/f32[76...) all-reduce(f32[768]{0:T(1024)S(1)} %add.420, ...), channel_id=24, replica_groups=mesh['dp'=2,'ctx'=4,'tp'=4] {'dp','ctx'}, use_global_device_ids=true, to_apply=%region_47.48.clone | all-reduce | flops 5760 | bytes 46080
  1123.5 40.4 %reduce-scatter.29.cloned.1.call-done = f32[96,768]{1,0:T(8,128)} async-done(((f32[768,768]{1,0:T(8,128)}), f32[96,768]{1,0:T(8,128)}) %reduce-scatter.29.cloned.1.call-update) | async-done | bytes 294928 | tf_op jit(solution)/shard_map/reduce_scatter | solution.py:102
  1163.9 73.4 %reduce-scatter.31.cloned.1.call-done = f32[96,768]{1,0:T(8,128)} async-done(((f32[768,768]{1,0:T(8,128)}), f32[96,768]{1,0:T(8,128)}) %reduce-scatter.31.cloned.1.call-update) | async-done | bytes 294928
  1237.3 66.7 %reduce-scatter.25.cloned.1.call-done = f32[96,192]{1,0:T(8,128)} async-done(((f32[768,192]{1,0:T(8,128)}), f32[96,192]{1,0:T(8,128)}) %reduce-scatter.25.cloned.1.call-update) | async-done | bytes 73744 | tf_op jit(solution)/shard_map/reduce_scatter | solution.py:100
  1303.9 66.1 %reduce-scatter.23.cloned.1.call-done = f32[96,192]{1,0:T(8,128)} async-done(((f32[768,192]{1,0:T(8,128)}), f32[96,192]{1,0:T(8,128)}) %reduce-scatter.23.cloned.1.call-update) | async-done | bytes 73744 | tf_op jit(solution)/shard_map/reduce_scatter | solution.py:99
  (422 shorter events, 218.6 us)
Async XLA Ops:
  8.0 180.3 %all-gather.9.cloned.1.call-start = ((), (), s32[]{:S(2)}) async-start(), calls=%async_computation.11 | async-start | bytes 1966080 | tf_op jit(solution)/shard_map/all_gather | solution.py:149
  41.1 144.5 %copy-start.88 = (f32[768]{0:T(1024)}, f32[768]{0:T(1024)S(1)}, u32[]{:S(2)}) copy-start(f32[768]{0:T(1024)S(1)} %convert_element_type.259) | copy-start | bytes 9220
  41.1 301.9 %copy-start.48 = (f32[768]{0:T(1024)}, f32[768]{0:T(1024)S(1)}, u32[]{:S(2)}) copy-start(f32[768]{0:T(1024)S(1)} %convert_element_type.258) | copy-start | bytes 9220
  44.1 141.5 %copy-start.55 = (f32[4,256]{1,0:T(4,128)}, f32[4,256]{1,0:T(4,128)S(1)}, u32[]{:S(2)}) copy-start(f32[4,256]{1,0:T(4,128)S(1)} %get-tuple-element.140) | copy-start | bytes 12292
  44.1 298.9 %copy-start.59 = (f32[4,256]{1,0:T(4,128)}, f32[4,256]{1,0:T(4,128)S(1)}, u32[]{:S(2)}) copy-start(f32[4,256]{1,0:T(4,128)S(1)} %get-tuple-element.164) | copy-start | bytes 12292
  45.9 139.7 %copy-start.78 = (f32[4,256]{1,0:T(4,128)}, f32[4,256]{1,0:T(4,128)S(1)}, u32[]{:S(2)}) copy-start(f32[4,256]{1,0:T(4,128)S(1)} %get-tuple-element.142) | copy-start | bytes 12292
  77.8 118.6 %all-gather.17.cloned.1.call-start = ((), (), s32[]{:S(2)}) async-start(), calls=%async_computation.16 | async-start | bytes 1966080 | tf_op jit(solution)/shard_map/all_gather | solution.py:149
  78.4 264.6 %copy-start.82 = (f32[4,256]{1,0:T(4,128)}, f32[4,256]{1,0:T(4,128)S(1)}, u32[]{:S(2)}) copy-start(f32[4,256]{1,0:T(4,128)S(1)} %get-tuple-element.138) | copy-start | bytes 12292
  80.2 138.0 %all-gather.7.cloned.1.call-start = ((), (), s32[]{:S(2)}) async-start(), calls=%async_computation.10 | async-start | bytes 1966080 | tf_op jit(solution)/shard_map/all_gather | solution.py:150
  113.8 229.2 %copy-start.16 = (bf16[768,192]{0,1:T(8,128)(2,1)}, bf16[768,192]{0,1:T(8,128)(2,1)S(1)}, u32[]{:S(2)}) copy-start(bf16[768,192]{0,1:T(8,128)(2,1)S(1)} %copy.62) | copy-start | bytes 884740
  115.6 203.8 %all-reduce.23.cloned.1.call-start = ((), (), s32[]{:S(2)}) async-start(), calls=%async_computation.12 | async-start | bytes 6291456 | tf_op jit(solution)/shard_map/psum | solution.py:165
  228.1 96.6 %all-gather.11.cloned.1.call-start = ((), (), s32[]{:S(2)}) async-start(), calls=%async_computation.13 | async-start | bytes 1327104 | tf_op jit(solution)/shard_map/all_gather | solution.py:68
  228.6 104.5 %all-gather.13.cloned.1.call-start = ((), (), s32[]{:S(2)}) async-start(), calls=%async_computation.14 | async-start | bytes 1327104 | tf_op jit(solution)/shard_map/all_gather | solution.py:69
  229.2 183.7 %all-reduce.27.cloned.1.call-start = ((), (), s32[]{:S(2)}) async-start(), calls=%async_computation.18 | async-start | bytes 6291456 | tf_op jit(solution)/shard_map/psum | solution.py:244
  229.5 302.9 %copy-start.53 = (f32[768]{0:T(1024)}, f32[768]{0:T(1024)S(1)}, u32[]{:S(2)}) copy-start(f32[768]{0:T(1024)S(1)} %convert_element_type.272) | copy-start | bytes 9220
  229.5 103.7 %copy-start.93 = (f32[768]{0:T(1024)}, f32[768]{0:T(1024)S(1)}, u32[]{:S(2)}) copy-start(f32[768]{0:T(1024)S(1)} %convert_element_type.274) | copy-start | bytes 9220
  343.0 107.8 %all-gather.15.cloned.1.call-start = ((), (), s32[]{:S(2)}) async-start(), calls=%async_computation.15 | async-start | bytes 1966080 | tf_op jit(solution)/shard_map/all_gather | solution.py:150
  346.8 182.1 %all-reduce.25.cloned.1.call-start = ((), (), s32[]{:S(2)}) async-start(), calls=%async_computation.17 | async-start | bytes 6291456 | tf_op jit(solution)/shard_map/psum | solution.py:165
  460.7 166.6 %all-reduce.29.cloned.1.call-start = ((), (), s32[]{:S(2)}) async-start(), calls=%async_computation.21 | async-start | bytes 6291456 | tf_op jit(solution)/shard_map/psum | solution.py:244
  558.5 140.3 %all-reduce.33.cloned.1.call-start = ((), (), s32[]{:S(2)}) async-start(), calls=%async_computation.31 | async-start | bytes 6291456 | tf_op jit(solution)/shard_map/psum | solution.py:175
  566.1 206.6 %reduce-scatter.15.cloned.1.call-start = ((), (), s32[]{:S(2)}) async-start(), calls=%async_computation.20 | async-start | bytes 3932160 | tf_op jit(solution)/shard_map/reduce_scatter | solution.py:280
  575.3 247.9 %reduce-scatter.13.cloned.1.call-start = ((), (), s32[]{:S(2)}) async-start(), calls=%async_computation.19 | async-start | bytes 3932160 | tf_op jit(solution)/shard_map/reduce_scatter | solution.py:279
  739.9 146.4 %reduce-scatter.17.cloned.1.call-start = ((), (), s32[]{:S(2)}) async-start(), calls=%async_computation.22 | async-start | bytes 3932160 | tf_op jit(solution)/shard_map/reduce_scatter | solution.py:279
  746.7 202.3 %reduce-scatter.19.cloned.1.call-start = ((), (), s32[]{:S(2)}) async-start(), calls=%async_computation.23 | async-start | bytes 3932160 | tf_op jit(solution)/shard_map/reduce_scatter | solution.py:280
  755.6 322.8 %all-reduce.31.cloned.1.call-start = ((), (), s32[]{:S(2)}) async-start(), calls=%async_computation.30 | async-start | bytes 12582912 | tf_op jit(solution)/shard_map/psum | solution.py:295
  770.4 117.2 %copy-start.19 = (bf16[768,192]{0,1:T(8,128)(2,1)S(1)}, bf16[768,192]{0,1:T(8,128)(2,1)}, u32[]{:S(2)}) copy-start(bf16[768,192]{0,1:T(8,128)(2,1)} %copy-done.18) | copy-start | bytes 884740
  958.0 165.6 %reduce-scatter.27.cloned.1.call-start = ((), (), s32[]{:S(2)}) async-start(), calls=%async_computation.27 | async-start | bytes 884736 | tf_op jit(solution)/shard_map/reduce_scatter | solution.py:101
  963.3 160.2 %reduce-scatter.21.cloned.1.call-start = ((), (), s32[]{:S(2)}) async-start(), calls=%async_computation.24 | async-start | bytes 884736 | tf_op jit(solution)/shard_map/reduce_scatter | solution.py:98
  967.4 196.5 %reduce-scatter.29.cloned.1.call-start = ((), (), s32[]{:S(2)}) async-start(), calls=%async_computation.28 | async-start | bytes 2654208 | tf_op jit(solution)/shard_map/reduce_scatter | solution.py:102
  974.4 262.9 %reduce-scatter.31.cloned.1.call-start = ((), (), s32[]{:S(2)}) async-start(), calls=%async_computation.29 | async-start | bytes 2654208
  984.1 319.8 %reduce-scatter.25.cloned.1.call-start = ((), (), s32[]{:S(2)}) async-start(), calls=%async_computation.26 | async-start | bytes 884736 | tf_op jit(solution)/shard_map/reduce_scatter | solution.py:100
  988.1 381.9 %reduce-scatter.23.cloned.1.call-start = ((), (), s32[]{:S(2)}) async-start(), calls=%async_computation.25 | async-start | bytes 884736 | tf_op jit(solution)/shard_map/reduce_scatter | solution.py:99
  (111 other events, 671.2 us)
Sparse Core Ops, SparseCore 0:
  77.9 55.2 all-gather.8
  134.7 41.9 all-gather.16
  178.8 39.2 all-gather.6
  228.2 91.2 all-reduce.22
  343.1 69.8 all-reduce.26
  414.4 36.3 all-gather.14
  460.8 68.0 all-reduce.24
  558.7 68.5 all-reduce.28
  630.2 68.5 all-reduce.32
  701.0 59.5 reduce-scatter.14
  762.9 60.3 reduce-scatter.12
  826.0 60.3 reduce-scatter.16
  888.6 60.3 reduce-scatter.18
  958.1 120.3 all-reduce.30
Sparse Core Ops, SparseCore 1:
  230.6 60.9 all-gather.10
  293.6 39.5 all-gather.12
  963.4 61.5 reduce-scatter.26
  1028.8 62.3 reduce-scatter.20
  1095.2 68.6 reduce-scatter.28
  1168.0 69.2 reduce-scatter.30
  1241.0 62.9 reduce-scatter.24
  1307.7 62.3 reduce-scatter.22
where the time goes:
time: 1390 us; the launch traced here: 1380 us
  waiting for transfers between devices  854 us (61%)
  matrix products  201 us (14%)
  blocking collectives  178 us (13%)
  other arithmetic  80.4 us (6%)
  local copies, waits for them, and re-layouts  43.5 us (3%)
  between operations  18.4 us (1%)
    psum x2, waiting for transfers between devices, forward_pass(): lax.psum(heads_to_rows(mixed_heads, output_heads_w).reshape(row_count, mo...  156 us
    psum x2, waiting for transfers between devices, backward_pass(): normed_two_grad = lax.psum(times_transposed(up_grad_rows, full_up), 'tp')  117 us
    reduce_scatter x2, waiting for transfers between devices, backward_pass(): lax.psum_scatter(key_terms, 'ctx', scatter_dimension=3, tiled=True)  109 us
    unnamed x23, waiting for transfers between devices  74.7 us
    psum x1, waiting for transfers between devices, backward_pass(): lax.psum(normed_part.reshape(row_count, model_width), 'tp')  72.9 us
    psum x1, waiting for transfers between devices, forward_pass(): lax.psum(times_transposed(activated, full_down).astype(jnp.bfloat16), 'tp')  67.4 us
    reduce_scatter x1, waiting for transfers between devices, reduce_grads(): lax.psum_scatter(grads_local[2], ('dp', 'ctx'), scatter_dimension=0, tile...  66.7 us
    reduce_scatter x1, waiting for transfers between devices, reduce_grads(): lax.psum_scatter(grads_local[1], ('dp', 'ctx'), scatter_dimension=0, tile...  66.1 us
  transfers between devices with their start and end apart: 22, of which 16 were waited for; matrix products, arithmetic and copies ran while one was open for 17% of the time, Pallas kernels for 0%

commit v1 on v0

v1 whole, which is shorter than its diff:
```python
import functools

import jax
import jax.numpy as jnp
from jax import lax
from jax.experimental import pallas as pl
from jax.experimental.pallas import tpu as pltpu
from jax.sharding import PartitionSpec as P

HEAD_DIM = 64
MESH = pl.DeviceIdType.MESH
F32 = jnp.float32
BF16 = jnp.bfloat16
VMEM_LIMIT = 66 * 1000 * 1000

epsilon = 1e-05
root_half = 0.7071067811865476
density_scale = 0.3989422804014327


def remote(src, dst, send_sem, recv_sem, device):
    return pltpu.make_async_remote_copy(
        src_ref=src,
        dst_ref=dst,
        send_sem=send_sem,
        recv_sem=recv_sem,
        device_id=device,
        device_id_type=MESH,
    )


def nn_dot(left, right):
    return lax.dot_general(left, right, (((1,), (0,)), ((), ())), preferred_element_type=F32)


def nt_dot(left, right):
    return lax.dot_general(left, right, (((1,), (1,)), ((), ())), preferred_element_type=F32)


def tn_dot(left, right):
    return lax.dot_general(left, right, (((0,), (0,)), ((), ())), preferred_element_type=F32)


def normalize(values):
    centred = values - jnp.mean(values, axis=-1, keepdims=True)
    spread = lax.rsqrt(jnp.mean(centred * centred, axis=-1, keepdims=True) + epsilon)
    return centred * spread, spread


def norm_back(grad_scaled, scaled, spread):
    inner = grad_scaled - jnp.mean(grad_scaled, axis=-1, keepdims=True)
    inner = inner - scaled * jnp.mean(grad_scaled * scaled, axis=-1, keepdims=True)
    return inner * spread


class Place:
    def __init__(self, sizes):
        self.n_dp, self.n_ctx, self.n_tp = sizes
        self.n_pair = self.n_tp // 2
        self.dp = lax.axis_index("dp")
        self.ctx = lax.axis_index("ctx")
        self.tp = lax.axis_index("tp")
        self.pair = self.tp // 2
        self.side = self.tp % 2

    def other_dp(self, k):
        d = (self.dp + k) % self.n_dp
        return d, (d, self.ctx, self.tp)

    def other_ctx(self, k):
        z = (self.ctx + k) % self.n_ctx
        return z, (self.dp, z, self.tp)

    def other_pair(self, k):
        p = (self.pair + k) % self.n_pair
        return p, (self.dp, self.ctx, 2 * p + self.side)

    def partner(self):
        return (self.dp, self.ctx, 2 * self.pair + 1 - self.side)

    def barrier(self, far):
        sem = pltpu.get_barrier_semaphore()
        count = 1
        pl.semaphore_signal(sem, inc=1, device_id=self.partner(), device_id_type=MESH)
        if far:
            for size, other in (
                (self.n_dp, self.other_dp),
                (self.n_ctx, self.other_ctx),
                (self.n_pair, self.other_pair),
            ):
                for k in range(1, size):
                    pl.semaphore_signal(sem, inc=1, device_id=other(k)[1], device_id_type=MESH)
                    count += 1
        pl.semaphore_wait(sem, count)


class Sends:
    def __init__(self, sems):
        self.sems = sems
        self.started = []

    def go(self, src, dst, recv_sem, device):
        copy = remote(src, dst, self.sems.at[len(self.started)], recv_sem, device)
        copy.start()
        self.started.append(copy)

    def finish(self):
        for copy in self.started:
            copy.wait_send()


def gather_body(sizes, half, *refs):
    here = Place(sizes)
    n_dp, n_ctx, n_pair = here.n_dp, here.n_ctx, here.n_pair
    d, z, p, c = here.dp, here.ctx, here.pair, here.side
    tokens, out_grad = refs[0:2]
    shards = refs[2:8]
    vec, bias = refs[8:10]
    tok_own, og_own = refs[10:12]
    full = refs[12:18]
    vec_all, bias_all = refs[18:20]
    own_sem, send_sem, rows_sem, line_sem, group_sem, vline_sem, vgroup_sem, bias_sem = refs[20:28]
    own_row = d * n_ctx + z
    mine = p * n_ctx + z
    rows = pl.ds(pl.multiple_of(c * half, half), half)

    here.barrier(True)
    sends = Sends(send_sem)
    own = [
        pltpu.make_async_copy(tokens.at[mine, rows], tok_own.at[z], own_sem.at[0]),
        pltpu.make_async_copy(out_grad.at[mine, rows], og_own.at[z], own_sem.at[1]),
        pltpu.make_async_copy(vec, vec_all.at[own_row], own_sem.at[2]),
        pltpu.make_async_copy(bias, bias_all.at[p], own_sem.at[3]),
    ]
    for a in range(6):
        own.append(pltpu.make_async_copy(shards[a], full[a].at[p, own_row], own_sem.at[4 + a]))
    for copy in own:
        copy.start()

    def send_rows(index, source, target):
        for k in range(1, n_ctx):
            zz, device = here.other_ctx(k)
            sends.go(
                source.at[p * n_ctx + zz, rows], target.at[z], rows_sem.at[index, z], device
            )

    def send_line(a):
        for k in range(1, n_ctx):
            zz, device = here.other_ctx(k)
            sends.go(shards[a], full[a].at[p, own_row], line_sem.at[a, z], device)

    send_rows(0, tokens, tok_own)
    for k in range(1, n_ctx):
        zz, device = here.other_ctx(k)
        sends.go(vec, vec_all.at[own_row], vline_sem.at[z], device)
    for k in range(1, n_pair):
        pp, device = here.other_pair(k)
        sends.go(bias, bias_all.at[p], bias_sem.at[p], device)
    for a in range(6):
        send_line(a)
    send_rows(1, out_grad, og_own)

    for copy in own:
        copy.wait()

    def group(a, pp, dd):
        return full[a].at[pp, pl.ds(dd * n_ctx, n_ctx)]

    def wait_line(a):
        for k in range(1, n_ctx):
            zz, device = here.other_ctx(k)
            slot = full[a].at[p, d * n_ctx + zz]
            remote(slot, slot, send_sem.at[0], line_sem.at[a, zz], device).wait_recv()

    def send_pair(a, dd):
        for k in range(1, n_pair):
            pp, device = here.other_pair(k)
            sends.go(group(a, p, dd), group(a, p, dd), group_sem.at[a, p, dd], device)

    def send_dp(a, pp):
        for k in range(1, n_dp):
            dd, device = here.other_dp(k)
            sends.go(group(a, pp, d), group(a, pp, d), group_sem.at[a, pp, d], device)

    def wait_group(a, pp, dd):
        slot = group(a, pp, dd)
        remote(slot, slot, send_sem.at[0], group_sem.at[a, pp, dd], here.partner()).wait_recv()

    for a in range(6):
        wait_line(a)
        send_dp(a, p)
        send_pair(a, d)
    for k in range(1, n_ctx):
        zz, device = here.other_ctx(k)
        slot = vec_all.at[d * n_ctx + zz]
        remote(slot, slot, send_sem.at[0], vline_sem.at[zz], device).wait_recv()
    for k in range(1, n_dp):
        dd, device = here.other_dp(k)
        slot = vec_all.at[pl.ds(d * n_ctx, n_ctx)]
        sends.go(slot, slot, vgroup_sem.at[d], device)
    pair_first = (True, True, True, True, False, True)
    for a in range(6):
        if pair_first[a]:
            for k in range(1, n_pair):
                pp = here.other_pair(k)[0]
                wait_group(a, pp, d)
                send_dp(a, pp)
        else:
            for k in range(1, n_dp):
                dd = here.other_dp(k)[0]
                wait_group(a, p, dd)
                send_pair(a, dd)
    for a in range(6):
        for k in range(1, n_dp):
            dd = here.other_dp(k)[0]
            if pair_first[a]:
                wait_group(a, p, dd)
            for j in range(1, n_pair):
                wait_group(a, here.other_pair(j)[0], dd)
        if not pair_first[a]:
            for j in range(1, n_pair):
                wait_group(a, here.other_pair(j)[0], d)
    for k in range(1, n_dp):
        dd, device = here.other_dp(k)
        slot = vec_all.at[pl.ds(dd * n_ctx, n_ctx)]
        remote(slot, slot, send_sem.at[0], vgroup_sem.at[dd], device).wait_recv()
    for k in range(1, n_pair):
        pp, device = here.other_pair(k)
        slot = bias_all.at[pp]
        remote(slot, slot, send_sem.at[0], bias_sem.at[pp], device).wait_recv()
    for index, target in ((0, tok_own), (1, og_own)):
        for k in range(1, n_ctx):
            zz, device = here.other_ctx(k)
            slot = target.at[zz]
            remote(slot, slot, send_sem.at[0], rows_sem.at[index, zz], device).wait_recv()
    sends.finish()


def gather_call(sizes, tokens, out_grad, shards, vec, bias):
    n_dp, n_ctx, n_tp = sizes
    n_pair = n_tp // 2
    seqs, block, width = tokens.shape
    half = block // 2
    any_spec = pl.BlockSpec(memory_space=pl.ANY)
    vmem_spec = pl.BlockSpec(memory_space=pltpu.VMEM)
    own = jax.ShapeDtypeStruct((n_ctx, half, width), BF16)
    out_shape = [own, own]
    out_shape += [jax.ShapeDtypeStruct((n_pair, n_dp * n_ctx) + s.shape, BF16) for s in shards]
    out_shape += [
        jax.ShapeDtypeStruct((n_dp * n_ctx,) + vec.shape, F32),
        jax.ShapeDtypeStruct((n_pair,) + bias.shape, F32),
    ]
    n_sends = (
        2 * (n_ctx - 1)
        + (n_ctx - 1)
        + (n_pair - 1)
        + 6 * (n_ctx - 1)
        + (n_dp - 1)
        + 6 * ((n_dp - 1) + (n_pair - 1) + (n_dp - 1) * (n_pair - 1))
    )
    dma = pltpu.SemaphoreType.DMA
    return pl.pallas_call(
        functools.partial(gather_body, sizes, half),
        out_shape=out_shape,
        in_specs=[any_spec] * 10,
        out_specs=[vmem_spec] * 10,
        scratch_shapes=[
            dma((10,)),
            dma((n_sends,)),
            dma((2, n_ctx)),
            dma((6, n_ctx)),
            dma((6, n_pair, n_dp)),
            dma((n_ctx,)),
            dma((n_dp,)),
            dma((n_pair,)),
        ],
        compiler_params=pltpu.CompilerParams(
            collective_id=0, has_side_effects=True, vmem_limit_bytes=VMEM_LIMIT
        ),
    )(tokens, out_grad, *shards, vec, bias)


def compute_body(sizes, *refs):
    here = Place(sizes)
    n_ctx, n_pair = here.n_ctx, here.n_pair
    c = here.side
    (tok, og, gq, gk, gv, go, gu, gd, vecs, bias) = refs[:10]
    (lo, tg, dwq, dwk, dwv, dwo, dwu, dwd, small) = refs[10:19]
    (
        xn1, wqkv, wo, qs, ks, vs, o32, mixed, hid, xn2, ogf, act, ug, bg, dm,
        dka, dva, dqkv, tra, trb, part, ssend, srecv, p_first, send_sem, recv_sem,
    ) = refs[19 : 19 + 23] + (refs[42 : 42 + n_ctx],) + refs[42 + n_ctx :]
    half, width = tok.shape[1], tok.shape[2]
    block = 2 * half
    cols = gq.shape[2]
    hw = n_pair * cols
    fw = gu.shape[2]
    lanes = 2 * HEAD_DIM
    n_twos = hw // lanes
    partner = here.partner()
    scale = HEAD_DIM ** -0.5
    first_head = lax.broadcasted_iota(jnp.int32, (1, lanes), 1) < HEAD_DIM
    zero16 = jnp.zeros((), BF16)

    def own_rows(b):
        return pl.ds(pl.multiple_of(b * block + c * half, half), half)

    def far_rows(b):
        return pl.ds(pl.multiple_of(b * block + (1 - c) * half, half), half)

    def block_rows(b):
        return pl.ds(pl.multiple_of(b * block, block), block)

    def exchange(stage, b, src, dst):
        return remote(src, dst, send_sem.at[stage, b], recv_sem.at[stage, b], partner)

    def rows_copy(stage, b, ref):
        return exchange(stage, b, ref.at[own_rows(b)], ref.at[own_rows(b)])

    def rows_arrive(stage, b, ref):
        exchange(stage, b, ref.at[far_rows(b)], ref.at[far_rows(b)]).wait_recv()

    def part_copy(stage, slot, b):
        return exchange(stage, b, ssend.at[slot, b], srecv.at[slot, b])

    here.barrier(False)

    gain_one, shift_one, out_shift = vecs[0:1, :], vecs[1:2, :], vecs[2:3, :]
    gain_two, shift_two, down_shift = vecs[3:4, :], vecs[4:5, :], vecs[5:6, :]

    @pl.loop(0, n_ctx)
    def _(b):
        exchange(0, b, og.at[b], ogf.at[own_rows(b)]).start()
        ogf[own_rows(b), :] = og[b]
        scaled, _ = normalize(tok[b].astype(F32))
        xn1[own_rows(b), :] = (scaled * gain_one + shift_one).astype(BF16)
        rows_copy(1, b, xn1).start()

    for i in range(n_pair):
        at = slice(i * cols, (i + 1) * cols)
        wqkv[:, i * cols : (i + 1) * cols] = gq[i]
        wqkv[:, hw + i * cols : hw + (i + 1) * cols] = gk[i]
        wqkv[:, 2 * hw + i * cols : 2 * hw + (i + 1) * cols] = gv[i]
        wo[:, at] = go[i]
    q_shift = bias[0, 0:1, :hw]
    v_shift = bias[0, 1:2, :hw]
    for i in range(1, n_pair):
        q_shift = q_shift + bias[i, 0:1, :hw]
        v_shift = v_shift + bias[i, 1:2, :hw]

    @pl.loop(0, n_ctx)
    def _(b):
        rows_arrive(1, b, xn1)
        product = nn_dot(xn1[block_rows(b), :], wqkv[...])
        qs[block_rows(b), :] = (product[:, :hw] + q_shift).astype(BF16) * jnp.asarray(scale, BF16)
        ks[block_rows(b), :] = product[:, hw : 2 * hw].astype(BF16)
        vs[block_rows(b), :] = (product[:, 2 * hw :] + v_shift).astype(BF16)

    for b in range(n_ctx):
        reach = (b + 1) * block
        here_rows = slice(b * block, (b + 1) * block)

        @pl.loop(0, n_twos)
        def _(j):
            at = pl.ds(pl.multiple_of(j * lanes, lanes), lanes)
            queries, keys, values = qs[here_rows, at], ks[:reach, at], vs[:reach, at]
            pieces = []
            for e in range(2):
                head = first_head if e == 0 else jnp.logical_not(first_head)
                scores = nt_dot(jnp.where(head, queries, zero16), keys)
                powers = jnp.exp(scores - jnp.max(scores, axis=-1, keepdims=True))
                inverse = 1.0 / jnp.sum(powers, axis=-1, keepdims=True)
                probs = (powers * inverse).astype(BF16)
                p_first[b][2 * j + e] = probs
                pieces.append(nn_dot(probs, values))
            out = jnp.where(first_head, pieces[0], pieces[1])
            o32[here_rows, at] = out
            mixed[here_rows, at] = out.astype(BF16)

        ssend[0, b] = nt_dot(mixed[far_rows(b), :], wo[...]).astype(BF16)
        part_copy(2, 0, b).start()
        hid[b] = nt_dot(mixed[own_rows(b), :], wo[...])

    @pl.loop(0, n_ctx)
    def _(b):
        part_copy(2, 0, b).wait()
        hidden = tok[b].astype(F32) + (hid[b] + srecv[0, b].astype(F32)) + out_shift
        hid[b] = hidden
        scaled, _ = normalize(hidden)
        xn2[own_rows(b), :] = (scaled * gain_two + shift_two).astype(BF16)
        rows_copy(3, b, xn2).start()

    small[...] = jnp.zeros_like(small)

    @pl.loop(0, n_ctx)
    def _(b):
        rows_arrive(0, b, ogf)
        rows_arrive(3, b, xn2)
        normed = xn2[block_rows(b), :]
        grads = ogf[block_rows(b), :]
        for i in range(n_pair):
            upward = nn_dot(normed, gu[i]) + bias[i, 2:3, :]
            big_phi = 0.5 + 0.5 * lax.erf(upward * root_half)
            act[i, block_rows(b), :] = (upward * big_phi).astype(BF16)
            slope = big_phi + upward * density_scale * jnp.exp(-0.5 * upward * upward)
            rows_grad = (nn_dot(grads, gd[i]) * slope).astype(BF16)
            ug[i, block_rows(b), :] = rows_grad
            small[8 + i : 9 + i, :] += jnp.sum(rows_grad.astype(F32), axis=0, keepdims=True)

        def through(ref, weight, rows):
            total = nt_dot(ref[0, rows, :], weight[0])
            for i in range(1, n_pair):
                total = total + nt_dot(ref[i, rows, :], weight[i])
            return total

        ssend[1, b] = through(act, gd, far_rows(b)).astype(BF16)
        part_copy(4, 1, b).start()
        ssend[0, b] = through(ug, gu, far_rows(b)).astype(BF16)
        part_copy(5, 0, b).start()
        part[0, b] = through(act, gd, own_rows(b))
        part[1, b] = through(ug, gu, own_rows(b))

    def transposed(ref, out):
        for b in range(n_ctx):
            out[:, b * block : (b + 1) * block] = ref[b * block : (b + 1) * block, :].T

    @pl.loop(0, n_ctx)
    def _(b):
        part_copy(4, 1, b).wait()
        lo[b] = (hid[b] + (part[0, b] + srecv[1, b].astype(F32)) + down_shift).astype(BF16)
        part_copy(5, 0, b).wait()
        grad_two = part[1, b] + srecv[0, b].astype(F32)
        scaled, spread = normalize(hid[b])
        own_grad = og[b].astype(F32)
        hidden_grad = own_grad + norm_back(grad_two * gain_two, scaled, spread)
        hid[b] = hidden_grad
        branch = hidden_grad.astype(BF16)
        bg[own_rows(b), :] = branch
        rows_copy(6, b, bg).start()
        small[2:3, :] += jnp.sum(branch.astype(F32), axis=0, keepdims=True)
        small[3:4, :] += jnp.sum(grad_two * scaled, axis=0, keepdims=True)
        small[4:5, :] += jnp.sum(grad_two, axis=0, keepdims=True)
        small[5:6, :] += jnp.sum(own_grad, axis=0, keepdims=True)

    transposed(xn2, tra)
    transposed(ogf, trb)
    step = 256

    @pl.loop(0, width // step)
    def _(r):
        rows = pl.ds(pl.multiple_of(r * step, step), step)
        for i in range(n_pair):
            dwu[i, rows, :] = nn_dot(tra[rows, :], ug[i]).astype(BF16)
            dwd[i, rows, :] = nn_dot(trb[rows, :], act[i]).astype(BF16)

    @pl.loop(0, n_ctx)
    def _(b):
        rows_arrive(6, b, bg)
        dm[block_rows(b), :] = nn_dot(bg[block_rows(b), :], wo[...]).astype(BF16)

    transposed(bg, trb)

    @pl.loop(0, width // step)
    def _(r):
        rows = pl.ds(pl.multiple_of(r * step, step), step)
        product = nn_dot(trb[rows, :], mixed[...])
        for i in range(n_pair):
            dwo[i, rows, :] = product[:, i * cols : (i + 1) * cols].astype(BF16)

    for b in reversed(range(n_ctx)):
        reach = (b + 1) * block
        here_rows = slice(b * block, (b + 1) * block)

        @pl.loop(0, n_twos)
        def _(j):
            at = pl.ds(pl.multiple_of(j * lanes, lanes), lanes)
            queries, keys, values = qs[here_rows, at], ks[:reach, at], vs[:reach, at]
            mix_grad, mix = dm[here_rows, at], o32[here_rows, at]
            towards = mix_grad.astype(F32) * mix
            query_parts, key_sum, value_sum = [], None, None
            for e in range(2):
                head = first_head if e == 0 else jnp.logical_not(first_head)
                grad_head = jnp.where(head, mix_grad, zero16)
                prob_grad = nt_dot(grad_head, values)
                centre = jnp.sum(jnp.where(head, towards, 0.0), axis=-1, keepdims=True)
                probs = p_first[b][2 * j + e]
                score_grad = (probs.astype(F32) * (prob_grad - centre)).astype(BF16)
                query_parts.append(nn_dot(score_grad, keys))
                key_term = tn_dot(score_grad, jnp.where(head, queries, zero16))
                value_term = tn_dot(probs, grad_head)
                key_sum = key_term if key_sum is None else key_sum + key_term
                value_sum = value_term if value_sum is None else value_sum + value_term
            query_grad = jnp.where(first_head, query_parts[0], query_parts[1]) * scale
            dqkv[here_rows, at] = query_grad.astype(BF16)
            if b == n_ctx - 1:
                dka[:, at] = key_sum
                dva[:, at] = value_sum
            else:
                dka[:reach, at] += key_sum
                dva[:reach, at] += value_sum

    @pl.loop(0, n_ctx)
    def _(b):
        dqkv[block_rows(b), hw : 2 * hw] = dka[block_rows(b), :].astype(BF16)
        dqkv[block_rows(b), 2 * hw :] = dva[block_rows(b), :].astype(BF16)
        small[6:7, :hw] += jnp.sum(dqkv[block_rows(b), :hw].astype(F32), axis=0, keepdims=True)
        small[7:8, :hw] += jnp.sum(dqkv[block_rows(b), 2 * hw :].astype(F32), axis=0, keepdims=True)
        ssend[1, b] = nt_dot(dqkv[far_rows(b), :], wqkv[...]).astype(BF16)
        part_copy(7, 1, b).start()
        part[0, b] = nt_dot(dqkv[own_rows(b), :], wqkv[...])

    transposed(xn1, tra)

    @pl.loop(0, width // step)
    def _(r):
        rows = pl.ds(pl.multiple_of(r * step, step), step)
        product = nn_dot(tra[rows, :], dqkv[...])
        for i in range(n_pair):
            dwq[i, rows, :] = product[:, i * cols : (i + 1) * cols].astype(BF16)
            dwk[i, rows, :] = product[:, hw + i * cols : hw + (i + 1) * cols].astype(BF16)
            dwv[i, rows, :] = product[:, 2 * hw + i * cols : 2 * hw + (i + 1) * cols].astype(BF16)

    @pl.loop(0, n_ctx)
    def _(b):
        part_copy(7, 1, b).wait()
        grad_one = part[0, b] + srecv[1, b].astype(F32)
        scaled, spread = normalize(tok[b].astype(F32))
        tg[b] = (hid[b] + norm_back(grad_one * gain_one, scaled, spread)).astype(BF16)
        small[0:1, :] += jnp.sum(grad_one * scaled, axis=0, keepdims=True)
        small[1:2, :] += jnp.sum(grad_one, axis=0, keepdims=True)
        exchange(0, b, og.at[b], ogf.at[own_rows(b)]).wait_send()
        rows_copy(1, b, xn1).wait_send()
        rows_copy(3, b, xn2).wait_send()
        rows_copy(6, b, bg).wait_send()


def compute_call(sizes, tok, og, weights, vecs, bias):
    n_dp, n_ctx, n_tp = sizes
    n_pair = n_tp // 2
    half, width = tok.shape[1:]
    block = 2 * half
    length = n_ctx * block
    cols = weights[0].shape[2]
    hw = n_pair * cols
    fw = weights[4].shape[2]
    heads = hw // HEAD_DIM
    vmem_spec = pl.BlockSpec(memory_space=pltpu.VMEM)
    shape = jax.ShapeDtypeStruct
    out_shape = [
        shape(tok.shape, BF16),
        shape(tok.shape, BF16),
    ]
    out_shape += [shape(w.shape, BF16) for w in weights]
    out_shape += [shape((16, width), F32)]
    vm = pltpu.VMEM
    scratch = [
        vm((length, width), BF16),
        vm((width, 3 * hw), BF16),
        vm((width, hw), BF16),
        vm((length, hw), BF16),
        vm((length, hw), BF16),
        vm((length, hw), BF16),
        vm((length, hw), F32),
        vm((length, hw), BF16),
        vm((n_ctx, half, width), F32),
        vm((length, width), BF16),
        vm((length, width), BF16),
        vm((n_pair, length, fw), BF16),
        vm((n_pair, length, fw), BF16),
        vm((length, width), BF16),
        vm((length, hw), BF16),
        vm((length, hw), F32),
        vm((length, hw), F32),
        vm((length, 3 * hw), BF16),
        vm((width, length), BF16),
        vm((width, length), BF16),
        vm((2, n_ctx, half, width), F32),
        vm((2, n_ctx, half, width), BF16),
        vm((2, n_ctx, half, width), BF16),
    ]
    scratch += [vm((heads, block, (b + 1) * block), BF16) for b in range(n_ctx)]
    scratch += [pltpu.SemaphoreType.DMA((8, n_ctx)), pltpu.SemaphoreType.DMA((8, n_ctx))]
    return pl.pallas_call(
        functools.partial(compute_body, sizes),
        out_shape=out_shape,
        in_specs=[vmem_spec] * 10,
        out_specs=[vmem_spec] * 9,
        scratch_shapes=scratch,
        compiler_params=pltpu.CompilerParams(
            collective_id=1, has_side_effects=True, vmem_limit_bytes=VMEM_LIMIT
        ),
    )(tok, og, *weights, vecs, bias)


def scatter_body(sizes, half, *refs):
    here = Place(sizes)
    n_dp, n_ctx, n_pair = here.n_dp, here.n_ctx, here.n_pair
    d, z, p, c = here.dp, here.ctx, here.pair, here.side
    rows_in = refs[0:2]
    grads = refs[2:8]
    small = refs[8]
    rows_out = refs[9:11]
    owned = refs[11:17]
    small_out = refs[17]
    it = iter(refs[18:])
    dp_land = [next(it) for _ in range(6)]
    dp_sum = [next(it) for _ in range(6)]
    keep = [next(it) for _ in range(6)]
    pair_land = [next(it) for _ in range(6)]
    pair_sum = [next(it) for _ in range(6)]
    ctx_land = [next(it) for _ in range(6)]
    side_land, small_b, ctx_small, small_c, pair_small, small_d, dp_small = [next(it) for _ in range(7)]
    own_sem, send_sem, line_sem, far_sem, side_sem, dp_sem, pair_sem, ctx_sem, small_sem = it
    mine = p * n_ctx + z
    rows = pl.ds(pl.multiple_of(c * half, half), half)

    here.barrier(True)
    sends = Sends(send_sem)

    for a in range(6):
        for k in range(1, n_dp):
            dd, device = here.other_dp(k)
            sends.go(
                grads[a].at[:, pl.ds(dd * n_ctx, n_ctx)],
                dp_land[a].at[k - 1],
                dp_sem.at[a, k - 1],
                device,
            )
    own = []
    for i in range(2):
        for k in range(1, n_ctx):
            zz, device = here.other_ctx(k)
            sends.go(rows_in[i].at[zz], rows_out[i].at[mine, rows], line_sem.at[i, z], device)
        own.append(pltpu.make_async_copy(rows_in[i].at[z], rows_out[i].at[mine, rows], own_sem.at[i]))
        own[-1].start()
    sends.go(small.at[pl.ds(0, 8)], side_land, small_sem.at[0, 0], here.partner())

    def small_arrive(stage, k, land):
        remote(land, land, send_sem.at[0], small_sem.at[stage, k - 1], here.partner()).wait_recv()

    for i in range(2):
        own[i].wait()
        for k in range(1, n_ctx):
            zz, device = here.other_ctx(k)
            slot = rows_out[i].at[p * n_ctx + zz, rows]
            remote(slot, slot, send_sem.at[0], line_sem.at[i, zz], device).wait_recv()
        for k in range(1, n_pair):
            pp, device = here.other_pair(k)
            slot = rows_out[i].at[pl.ds(p * n_ctx, n_ctx), rows]
            sends.go(slot, slot, far_sem.at[i, p], device)

    small_arrive(0, 1, side_land)
    small_b[0:8, :] = small[0:8, :] + side_land[...]
    small_b[8:16, :] = small[8:16, :]
    small_b[6:8, :] = small[6:8, :]
    for k in range(1, n_ctx):
        zz, device = here.other_ctx(k)
        sends.go(small_b, ctx_small.at[k - 1], small_sem.at[1, k - 1], device)

    for a in range(6):
        for k in range(1, n_dp):
            remote(
                dp_land[a].at[k - 1], dp_land[a].at[k - 1], send_sem.at[0], dp_sem.at[a, k - 1],
                here.partner(),
            ).wait_recv()
        for i in range(n_pair):
            total = grads[a][i, pl.ds(d * n_ctx, n_ctx)].astype(F32)
            for k in range(1, n_dp):
                total = total + dp_land[a][k - 1, i].astype(F32)
            dp_sum[a][i] = total.astype(BF16)
        for k in range(1, n_pair):
            pp, device = here.other_pair(k)
            sends.go(dp_sum[a].at[pp], pair_land[a].at[k - 1], pair_sem.at[a, k - 1], device)

    total = small_b[...]
    for k in range(1, n_ctx):
        small_arrive(1, k, ctx_small.at[k - 1])
        total = total + ctx_small[k - 1]
    small_c[...] = total
    for k in range(1, n_pair):
        pp, device = here.other_pair(k)
        sends.go(small_c, pair_small.at[k - 1], small_sem.at[2, k - 1], device)

    for a in range(6):
        for k in range(1, n_pair):
            remote(
                pair_land[a].at[k - 1], pair_land[a].at[k - 1], send_sem.at[0], pair_sem.at[a, k - 1],
                here.partner(),
            ).wait_recv()
        total = dp_sum[a][p].astype(F32)
        for k in range(1, n_pair):
            total = total + pair_land[a][k - 1].astype(F32)
        keep[a][...] = total
        pair_sum[a][...] = total.astype(BF16)
        for k in range(1, n_ctx):
            zz, device = here.other_ctx(k)
            sends.go(pair_sum[a].at[zz], ctx_land[a].at[k - 1], ctx_sem.at[a, k - 1], device)

    total = small_c[...]
    for k in range(1, n_pair):
        small_arrive(2, k, pair_small.at[k - 1])
        total = total + pair_small[k - 1]
    small_d[...] = total
    for k in range(1, n_dp):
        dd, device = here.other_dp(k)
        sends.go(small_d, dp_small.at[k - 1], small_sem.at[3, k - 1], device)

    for i in range(2):
        for k in range(1, n_pair):
            pp, device = here.other_pair(k)
            slot = rows_out[i].at[pl.ds(pp * n_ctx, n_ctx), rows]
            remote(slot, slot, send_sem.at[0], far_sem.at[i, pp], device).wait_recv()
        slot = rows_out[i].at[:, rows]
        sends.go(slot, slot, side_sem.at[i], here.partner())

    for a in range(6):
        total = keep[a][z]
        for k in range(1, n_ctx):
            remote(
                ctx_land[a].at[k - 1], ctx_land[a].at[k - 1], send_sem.at[0], ctx_sem.at[a, k - 1],
                here.partner(),
            ).wait_recv()
            total = total + ctx_land[a][k - 1].astype(F32)
        owned[a][...] = total

    total = small_d[...]
    for k in range(1, n_dp):
        small_arrive(3, k, dp_small.at[k - 1])
        total = total + dp_small[k - 1]
    small_out[...] = total
    other = pl.ds(pl.multiple_of((1 - c) * half, half), half)
    for i in range(2):
        slot = rows_out[i].at[:, other]
        remote(slot, slot, send_sem.at[0], side_sem.at[i], here.partner()).wait_recv()
    sends.finish()


def scatter_call(sizes, seqs, lo, tg, grads, small):
    n_dp, n_ctx, n_tp = sizes
    n_pair = n_tp // 2
    half, width = lo.shape[1:]
    vmem_spec = pl.BlockSpec(memory_space=pltpu.VMEM)
    shape = jax.ShapeDtypeStruct
    vm = pltpu.VMEM
    tail = [g.shape[2:] for g in grads]
    out_shape = [shape((seqs, 2 * half, width), BF16)] * 2
    out_shape += [shape(t, F32) for t in tail]
    out_shape += [shape(small.shape, F32)]
    scratch = [vm((n_dp - 1, n_pair, n_ctx) + t, BF16) for t in tail]
    scratch += [vm((n_pair, n_ctx) + t, BF16) for t in tail]
    scratch += [vm((n_ctx,) + t, F32) for t in tail]
    scratch += [vm((n_pair - 1, n_ctx) + t, BF16) for t in tail]
    scratch += [vm((n_ctx,) + t, BF16) for t in tail]
    scratch += [vm((n_ctx - 1,) + t, BF16) for t in tail]
    scratch += [
        vm((8, width), F32),
        vm((16, width), F32),
        vm((n_ctx - 1, 16, width), F32),
        vm((16, width), F32),
        vm((n_pair - 1, 16, width), F32),
        vm((16, width), F32),
        vm((n_dp - 1, 16, width), F32),
    ]
    n_sends = (
        6 * ((n_dp - 1) + (n_pair - 1) + (n_ctx - 1))
        + 2 * ((n_ctx - 1) + (n_pair - 1) + 1)
        + 1 + (n_ctx - 1) + (n_pair - 1) + (n_dp - 1)
    )
    dma = pltpu.SemaphoreType.DMA
    most = max(n_dp, n_ctx, n_pair)
    scratch += [
        dma((2,)),
        dma((n_sends,)),
        dma((2, n_ctx)),
        dma((2, n_pair)),
        dma((2,)),
        dma((6, n_dp - 1)),
        dma((6, n_pair - 1)),
        dma((6, n_ctx - 1)),
        dma((4, most)),
    ]
    return pl.pallas_call(
        functools.partial(scatter_body, sizes, half),
        out_shape=out_shape,
        in_specs=[vmem_spec] * 9,
        out_specs=[vmem_spec] * 9,
        scratch_shapes=scratch,
        compiler_params=pltpu.CompilerParams(
            collective_id=2, has_side_effects=True, vmem_limit_bytes=VMEM_LIMIT
        ),
    )(lo, tg, *grads, small)


def per_device(
    tokens,
    out_grad,
    query_weight,
    key_weight,
    value_weight,
    output_weight,
    up_weight,
    down_weight,
    norm1_gain,
    norm1_bias,
    output_bias,
    norm2_gain,
    norm2_bias,
    down_bias,
    query_bias,
    value_bias,
    up_bias,
):
    sizes = (lax.axis_size("dp"), lax.axis_size("ctx"), lax.axis_size("tp"))
    n_dp, n_ctx, n_tp = sizes
    n_pair = n_tp // 2
    seqs, block, width = tokens.shape
    assert seqs == n_ctx * n_pair
    share = norm1_gain.shape[0]
    cols = query_bias.shape[0]
    pair = lax.axis_index("tp") // 2
    row = lax.axis_index("dp") * n_ctx + lax.axis_index("ctx")

    six = jnp.stack(
        [norm1_gain, norm1_bias, output_bias, norm2_gain, norm2_bias, down_bias]
    ).astype(F32)
    vec = jnp.pad(six, ((0, 2), (0, 128 - share)))
    columns = jnp.arange(width) // cols == pair
    narrow = [jnp.where(columns, jnp.tile(b.astype(F32), width // cols), 0.0) for b in (query_bias, value_bias)]
    bias = jnp.pad(jnp.stack(narrow + [up_bias.astype(F32)]), ((0, 5), (0, 0)))

    shards = (query_weight, key_weight, value_weight, output_weight, up_weight, down_weight)
    gathered = gather_call(sizes, tokens, out_grad, shards, vec, bias)
    tok, og = gathered[0:2]
    weights = [w.reshape(n_pair, width, w.shape[3]) for w in gathered[2:8]]
    vecs = gathered[8][:, :, :share].transpose(1, 0, 2).reshape(8, width)
    results = compute_call(sizes, tok, og, weights, vecs, gathered[9])
    lo, tg = results[0:2]
    grads = [
        g.reshape(n_pair, n_dp * n_ctx, s.shape[0], s.shape[1]) for g, s in zip(results[2:8], shards)
    ]
    final = scatter_call(sizes, seqs, lo, tg, grads, results[8])
    layer_out, tokens_grad = final[0], final[1].astype(F32)
    small = final[8]
    owned = [lax.dynamic_slice_in_dim(small[i], row * share, share) for i in range(6)]
    shifts = [lax.dynamic_slice_in_dim(small[6 + i], pair * cols, cols) for i in range(2)]
    up_total = lax.dynamic_index_in_dim(small[8 : 8 + n_pair], pair, 0, keepdims=False)
    return (layer_out, tokens_grad, *final[2:8], *owned, *shifts, up_total)


def solution(mesh):
    rows_spec = P("dp", "ctx", None)
    weight_spec = P(("dp", "ctx"), "tp")
    vector_spec = P(("dp", "ctx"))
    column_spec = P("tp")
    common = (rows_spec,) * 2 + (weight_spec,) * 6 + (vector_spec,) * 6 + (column_spec,) * 3
    return jax.shard_map(
        per_device, mesh=mesh, in_specs=common, out_specs=common, check_vma=False
    )
```

time: 1390 us -> 375 us (0.27)
  waiting for transfers between devices: 854 us -> 0 us
  Pallas kernels: 0 us -> 350 us
  matrix products: 201 us -> 0 us
  blocking collectives: 178 us -> 0 us
  other arithmetic: 80.4 us -> 6.54 us
  local copies, waits for them, and re-layouts: 43.5 us -> 15.5 us
  between operations: 18.4 us -> 0.77 us
    psum x6 -> x0, waiting for transfers between devices: 414 us -> none  [the longest x2 156 us: forward_pass(): lax.psum(heads_to_rows(mixed_heads, output_heads_w).reshape(row_count, mo...]
    pallas_call x0 -> x3, Pallas kernels: none -> 350 us  [the longest x1 138 us: scatter_call(): pl.pallas_call(functools.partial(scatter_body, sizes, half), out_shape=ou...]
    reduce_scatter x9 -> x0, waiting for transfers between devices: 339 us -> none  [the longest x2 109 us: backward_pass(): lax.psum_scatter(key_terms, 'ctx', scatter_dimension=3, tiled=True)]
    dot_general x48 -> x0, matrix products: 201 us -> none  [the longest x4 30.3 us: plain_product(): return jnp.dot(left_side, right_side, preferred_element_type=jnp.float32)]
    all_gather x4 -> x0, blocking collectives: 125 us -> none  [the longest x1 32.4 us: gather_forward(): lax.all_gather(shards[2], ('dp', 'ctx'), axis=0, tiled=True)]
    unnamed x23 -> x0, waiting for transfers between devices: 74.7 us -> none
    unnamed x2 -> x0, blocking collectives: 53.2 us -> none
    reduce_sum x14 -> x0, other arithmetic: 40.7 us -> none  [the longest x2 10.8 us: backward_pass(): out_shift_grad = jnp.sum(branch_grad.astype(jnp.float32), axis=0)]
  transfers between devices with their start and end apart: 22 -> 0, of which waited for: 16 -> 0; matrix products, arithmetic and copies ran while one was open for 17% -> 0% of each run, Pallas kernels for 0% -> 0%
where the time goes in v1:
time: 375 us; the launch traced here: 373 us
  Pallas kernels  350 us (93%)
  local copies, waits for them, and re-layouts  15.5 us (4%)
  other arithmetic  6.54 us (2%)
    pallas_call x1, Pallas kernels, scatter_call(): pl.pallas_call(functools.partial(scatter_body, sizes, half), out_shape=ou...  138 us
    pallas_call x1, Pallas kernels, gather_call(): pl.pallas_call(functools.partial(gather_body, sizes, half), out_shape=out...  124 us
    pallas_call x1, Pallas kernels, compute_call(): pl.pallas_call(functools.partial(compute_body, sizes), out_shape=out_shap...  88.6 us

profile of v1, /device:TPU:25, one launch (start us, length us, event | category | flops | bytes accessed | tf_op | source)
XLA Modules:
  0.0 372.8 jit_solution(6776301040236057280)
XLA Ops:
  0.7 0.7 tile.20
  1.3 0.1 tile.21
  1.4 0.7 tile.8
  2.1 0.1 tile.9
  2.2 0.7 reshape.154
  2.9 0.6 select_maximum_fusion.refs_9_
  3.5 0.8 stack.38
  4.3 0.6 pad_convert_fusion.refs_8_
  4.8 123.7 %shard_map.296 = (bf16[4,128,768]{2,1,0:T(8,128)(2,1)}, bf16[4,128,768]{2,1,0:T(8,128)(2,1)}, bf16[2,8,96,192]{3,2,1,0:T(8,128)(2,1)}, bf16[2,8,96,192]{3,2,1,0:...) custom-call(bf16[8,256,768]{2,1,0:T(8,128)(2,1)} %refs_0_.1, ...), custom_call_target="tpu_custom_call" | custom-call | tf_op jit(solution)/shard_map/pallas_call | solution.py:262
  128.6 0.8 slice_bitcast_fusion
  129.3 0.7 reshape.147.refs_8_
  130.0 88.6 %shard_map.297 = (bf16[4,128,768]{2,1,0:T(8,128)(2,1)}, bf16[4,128,768]{2,1,0:T(8,128)(2,1)}, bf16[2,768,192]{2,1,0:T(8,128)(2,1)}, bf16[2,768,192]{2,1,0:T(8,12...) custom-call(bf16[4,128,768]{2,1,0:T(8,128)(2,1)} %get-tuple-element., ...), custom_call_target="tpu_custom_call" | custom-call | tf_op jit(solution)/shard_map/pallas_call | solution.py:583
  218.6 137.7 %shard_map.298 = (bf16[8,256,768]{2,1,0:T(8,128)(2,1)}, bf16[8,256,768]{2,1,0:T(8,128)(2,1)}, f32[96,192]{1,0:T(8,128)}, f32[96,192]{1,0:T(8,128)}, f32[96,192]{...) custom-call(bf16[4,128,768]{2,1,0:T(8,128)(2,1)} %get-tuple-element.55.refs_0_, ...), custom_call_target="tpu_custom_call" | custom-call | tf_op jit(solution)/shard_map/pallas_call | solution.py:782
  356.3 5.3 %convert_element_type.17 = f32[8,256,768]{2,1,0:T(8,128)} convert(bf16[8,256,768]{2,1,0:T(8,128)(2,1)} %get-tuple-element.65) | non-fusion elementwise | flops 1572864 | bytes 9437184 | tf_op jit(solution)/shard_map/convert_element_type | solution.py:842
  361.7 0.6 constant_dynamic-slice_fusion.1
  362.3 0.6 constant_dynamic-slice_fusion
  363.0 0.6 dynamic-slice_reduce_fusion
  363.6 0.6 fusion
  364.2 0.6 fusion.1
  364.7 0.6 fusion.2
  365.3 0.6 fusion.3
  365.9 0.6 fusion.4
  366.5 0.6 fusion.5
  367.1 1.7 copy.42
  368.8 0.0 copy-done.6
  368.8 0.6 copy.43
  369.4 0.6 copy.44
  370.1 0.6 copy.45
  370.7 0.6 copy.46
  371.3 0.0 copy-done.2
  371.3 0.7 copy.47
  372.1 0.7 copy.48
  (18 shorter events, 0.1 us)
Async XLA Ops:
  356.3 5.3 %copy-start.7 = (f32[16,768]{1,0:T(8,128)S(1)}, f32[16,768]{1,0:T(8,128)}, u32[]{:S(2)}) copy-start(f32[16,768]{1,0:T(8,128)} %get-tuple-element.72) | copy-start | bytes 147460
  356.3 10.7 %copy-start = (bf16[8,256,768]{2,1,0:T(8,128)(2,1)S(1)}, bf16[8,256,768]{2,1,0:T(8,128)(2,1)}, u32[]{:S(2)}) copy-start(bf16[8,256,768]{2,1,0:T(8,128)(2,1)} %get-tuple-element.100) | copy-start | bytes 9437188
  367.1 1.7 copy-start.6
  367.1 2.4 copy-start.5
  367.1 3.0 copy-start.4
  367.1 3.6 copy-start.3
  367.1 4.3 %copy-start.2 = (f32[96,768]{1,0:T(8,128)S(1)}, f32[96,768]{1,0:T(8,128)}, u32[]{:S(2)}) copy-start(f32[96,768]{1,0:T(8,128)} %get-tuple-element.106) | copy-start | bytes 884740
  367.1 5.0 %copy-start.1 = (f32[96,768]{1,0:T(8,128)S(1)}, f32[96,768]{1,0:T(8,128)}, u32[]{:S(2)}) copy-start(f32[96,768]{1,0:T(8,128)} %get-tuple-element.107) | copy-start | bytes 884740

commit v2 on v1

--- a/solution.py
+++ b/solution.py
@@ -791,6 +791,737 @@
     )(lo, tg, *grads, small)
 
 
+def fused_body(sizes, dims, *refs):
+    here = Place(sizes)
+    n_dp, n_ctx, n_pair = here.n_dp, here.n_ctx, here.n_pair
+    d, z, p, c = here.dp, here.ctx, here.pair, here.side
+    half, width, share, cols, fw = dims
+    block = 2 * half
+    hw = n_pair * cols
+    lanes = 2 * HEAD_DIM
+    n_twos = hw // lanes
+    n_rows = n_dp * n_ctx
+    two = n_ctx // 2
+    it = iter(refs)
+
+    def take(n):
+        return [next(it) for _ in range(n)]
+
+    tokens, out_grad, pack = take(3)
+    shards = take(3)
+    rows_out = take(2)
+    owned = take(3)
+    small_out = next(it)
+    full = take(3)
+    pack_all, vecs, cold = take(3)
+    tok, og, lo, tg = take(4)
+    (
+        xn1, wqkv, wo, qs, ks, vs, o32, mixed, hid, xn2, ogf, act, ug, bg, dm, dqkv, tra, trb,
+        wide, ssend, srecv, dwd, small,
+    ) = take(23)
+    p_first = take(n_ctx)
+    dp_one, pair_one, pair_two, dp_two, ctx_land = take(3), take(3), take(3), take(3), take(3)
+    side_land, small_b, ctx_small, small_c, pair_small, small_d, dp_small = take(7)
+    (
+        own_sem, put_sem, rows_sem, line_sem, pair_sem, dp_sem, diag_dp_sem, diag_pair_sem, swap_send,
+        swap_recv, scatter_sem, ctx_sem, out_line, out_pair, out_side, small_sem,
+    ) = take(16)
+    partner = here.partner()
+    own_row = d * n_ctx + z
+    mine = p * n_ctx + z
+    scale = HEAD_DIM ** -0.5
+    first_head = lax.broadcasted_iota(jnp.int32, (1, lanes), 1) < HEAD_DIM
+    zero16 = jnp.zeros((), BF16)
+    side_rows = pl.ds(pl.multiple_of(c * half, half), half)
+    sends = Sends(put_sem)
+
+    def arrive(slot, sem):
+        remote(slot, slot, put_sem.at[0], sem, partner).wait_recv()
+
+    def shard_rows(r, count=1):
+        return pl.ds(pl.multiple_of(r * share, 16), count * share)
+
+    def slot(a, pp, dd, zz, count=1):
+        return full[a].at[pp, shard_rows(dd * n_ctx + zz, count)]
+
+    gather_own = [pltpu.make_async_copy(shards[a], slot(a, p, d, z), own_sem.at[a]) for a in range(3)]
+
+    def gather_start(a):
+        gather_own[a].start()
+        for k in range(1, n_ctx):
+            zz, device = here.other_ctx(k)
+            sends.go(shards[a], slot(a, p, d, z), line_sem.at[a, z], device)
+
+    def gather_hop(a):
+        gather_own[a].wait()
+        for k in range(1, n_ctx):
+            zz = here.other_ctx(k)[0]
+            arrive(slot(a, p, d, zz), line_sem.at[a, zz])
+        group = slot(a, p, d, 0, n_ctx)
+        for k in range(1, n_pair):
+            sends.go(group, group, pair_sem.at[a, p], here.other_pair(k)[1])
+        for k in range(1, n_dp):
+            sends.go(group, group, dp_sem.at[a, d], here.other_dp(k)[1])
+
+    def gather_turn(a):
+        for k in range(1, n_pair):
+            pp = here.other_pair(k)[0]
+            arrive(slot(a, pp, d, 0, n_ctx), pair_sem.at[a, pp])
+            first = slot(a, pp, d, 0, two)
+            for j in range(1, n_dp):
+                sends.go(first, first, diag_dp_sem.at[a, pp, d], here.other_dp(j)[1])
+        for k in range(1, n_dp):
+            dd = here.other_dp(k)[0]
+            arrive(slot(a, p, dd, 0, n_ctx), dp_sem.at[a, dd])
+            second = slot(a, p, dd, two, n_ctx - two)
+            for j in range(1, n_pair):
+                sends.go(second, second, diag_pair_sem.at[a, p, dd], here.other_pair(j)[1])
+
+    def gather_end(a):
+        for k in range(1, n_pair):
+            pp = here.other_pair(k)[0]
+            for j in range(1, n_dp):
+                dd = here.other_dp(j)[0]
+                arrive(slot(a, pp, dd, 0, two), diag_dp_sem.at[a, pp, dd])
+                arrive(slot(a, pp, dd, two, n_ctx - two), diag_pair_sem.at[a, pp, dd])
+
+    def pack_start():
+        pack_own.start()
+        for k in range(1, n_ctx):
+            sends.go(pack, pack_all.at[p, own_row], line_sem.at[3, z], here.other_ctx(k)[1])
+
+    def pack_hop():
+        pack_own.wait()
+        for k in range(1, n_ctx):
+            zz = here.other_ctx(k)[0]
+            arrive(pack_all.at[p, d * n_ctx + zz], line_sem.at[3, zz])
+        group = pack_all.at[p, pl.ds(d * n_ctx, n_ctx)]
+        for k in range(1, n_pair):
+            sends.go(group, group, pair_sem.at[3, p], here.other_pair(k)[1])
+        for k in range(1, n_dp):
+            sends.go(group, group, dp_sem.at[3, d], here.other_dp(k)[1])
+
+    def pack_end():
+        for k in range(1, n_pair):
+            pp = here.other_pair(k)[0]
+            arrive(pack_all.at[pp, pl.ds(d * n_ctx, n_ctx)], pair_sem.at[3, pp])
+        for k in range(1, n_dp):
+            dd = here.other_dp(k)[0]
+            arrive(pack_all.at[p, pl.ds(dd * n_ctx, n_ctx)], dp_sem.at[3, dd])
+
+    pack_own = pltpu.make_async_copy(pack, pack_all.at[p, own_row], own_sem.at[3])
+
+    rows_own = [
+        pltpu.make_async_copy(source.at[mine, side_rows], target.at[z], own_sem.at[4 + i])
+        for i, (source, target) in enumerate(((tokens, tok), (out_grad, og)))
+    ]
+
+    def rows_start(i, source, target):
+        rows_own[i].start()
+        for k in range(1, n_ctx):
+            zz, device = here.other_ctx(k)
+            sends.go(source.at[p * n_ctx + zz, side_rows], target.at[z], rows_sem.at[i, z], device)
+
+    def grad_rows(ref, pp, dd, second):
+        return ref.at[pp, shard_rows(dd * n_ctx + (two if second else 0), two)]
+
+    def scatter_start(a, ref):
+        for k in range(1, n_dp):
+            dd, device = here.other_dp(k)
+            for i in range(n_pair):
+                sends.go(grad_rows(ref, i, dd, False), dp_one[a].at[k - 1, i], scatter_sem.at[a, 0, k - 1, i], device)
+        for k in range(1, n_pair):
+            pp, device = here.other_pair(k)
+            for i in range(n_dp):
+                sends.go(grad_rows(ref, pp, i, True), pair_one[a].at[k - 1, i], scatter_sem.at[a, 1, k - 1, i], device)
+
+    def add_into(target, parts):
+        total = target[...].astype(F32)
+        for part in parts:
+            total = total + part[...].astype(F32)
+        target[...] = total.astype(BF16)
+
+    def scatter_turn(a, ref):
+        for i in range(n_pair):
+            for k in range(1, n_dp):
+                arrive(dp_one[a].at[k - 1, i], scatter_sem.at[a, 0, k - 1, i])
+            add_into(grad_rows(ref, i, d, False), [dp_one[a].at[k - 1, i] for k in range(1, n_dp)])
+        for k in range(1, n_pair):
+            pp, device = here.other_pair(k)
+            sends.go(grad_rows(ref, pp, d, False), pair_two[a].at[k - 1], scatter_sem.at[a, 2, k - 1, 0], device)
+        for i in range(n_dp):
+            for k in range(1, n_pair):
+                arrive(pair_one[a].at[k - 1, i], scatter_sem.at[a, 1, k - 1, i])
+            add_into(grad_rows(ref, p, i, True), [pair_one[a].at[k - 1, i] for k in range(1, n_pair)])
+        for k in range(1, n_dp):
+            dd, device = here.other_dp(k)
+            sends.go(grad_rows(ref, p, dd, True), dp_two[a].at[k - 1], scatter_sem.at[a, 3, k - 1, 0], device)
+
+    def scatter_line(a, ref):
+        for k in range(1, n_pair):
+            arrive(pair_two[a].at[k - 1], scatter_sem.at[a, 2, k - 1, 0])
+        add_into(grad_rows(ref, p, d, False), [pair_two[a].at[k - 1] for k in range(1, n_pair)])
+        for k in range(1, n_dp):
+            arrive(dp_two[a].at[k - 1], scatter_sem.at[a, 3, k - 1, 0])
+        add_into(grad_rows(ref, p, d, True), [dp_two[a].at[k - 1] for k in range(1, n_dp)])
+        for k in range(1, n_ctx):
+            zz, device = here.other_ctx(k)
+            sends.go(ref.at[p, shard_rows(d * n_ctx + zz)], ctx_land[a].at[k - 1], ctx_sem.at[a, k - 1], device)
+
+    def scatter_end(a, ref):
+        total = ref[p, shard_rows(own_row), :].astype(F32)
+        for k in range(1, n_ctx):
+            arrive(ctx_land[a].at[k - 1], ctx_sem.at[a, k - 1])
+            total = total + ctx_land[a][k - 1].astype(F32)
+        owned[a][...] = total
+
+    def out_slot(i, s, rows):
+        return rows_out[i].at[s, rows]
+
+    def out_start(i, source):
+        for k in range(1, n_ctx):
+            zz, device = here.other_ctx(k)
+            sends.go(source.at[zz], out_slot(i, mine, side_rows), out_line.at[i, z], device)
+        copy = pltpu.make_async_copy(source.at[z], out_slot(i, mine, side_rows), own_sem.at[6 + i])
+        copy.start()
+        return copy
+
+    def out_pass(i, s):
+        piece = out_slot(i, s, side_rows)
+        for j in range(1, n_pair):
+            sends.go(piece, piece, out_pair.at[i, s], here.other_pair(j)[1])
+        sends.go(piece, piece, out_side.at[i, s], partner)
+
+    def out_hop(i, copy):
+        copy.wait()
+        out_pass(i, mine)
+        for k in range(1, n_ctx):
+            zz = here.other_ctx(k)[0]
+            s = p * n_ctx + zz
+            arrive(out_slot(i, s, side_rows), out_line.at[i, zz])
+            out_pass(i, s)
+
+    def out_cross(i):
+        for j in range(1, n_pair):
+            pp = here.other_pair(j)[0]
+            for k in range(n_ctx):
+                s = pp * n_ctx + (z + k) % n_ctx
+                piece = out_slot(i, s, side_rows)
+                arrive(piece, out_pair.at[i, s])
+                sends.go(piece, piece, out_side.at[i, s], partner)
+
+    far_side = pl.ds(pl.multiple_of((1 - c) * half, half), half)
+
+    def out_end(i):
+        for s in range(n_pair * n_ctx):
+            arrive(out_slot(i, s, far_side), out_side.at[i, s])
+
+    def own_rows(b):
+        return pl.ds(pl.multiple_of(b * block + c * half, half), half)
+
+    def far_rows(b):
+        return pl.ds(pl.multiple_of(b * block + (1 - c) * half, half), half)
+
+    def block_rows(b):
+        return pl.ds(pl.multiple_of(b * block, block), block)
+
+    def swap(stage, b, src, dst):
+        return remote(src, dst, swap_send.at[stage, b], swap_recv.at[stage, b], partner)
+
+    def rows_copy(stage, b, ref):
+        return swap(stage, b, ref.at[own_rows(b)], ref.at[own_rows(b)])
+
+    def rows_arrive(stage, b, ref):
+        swap(stage, b, ref.at[far_rows(b)], ref.at[far_rows(b)]).wait_recv()
+
+    def part_copy(stage, place, b):
+        return swap(stage, b, ssend.at[place, b], srecv.at[place, b])
+
+    def part_store(i, b, value):
+        wide[i, pl.ds(pl.multiple_of(b * block, block), half), :] = value[:, :hw]
+        wide[i, pl.ds(pl.multiple_of(b * block + half, half), half), :] = value[:, hw:]
+
+    def part_load(i, b):
+        left = wide[i, pl.ds(pl.multiple_of(b * block, block), half), :]
+        right = wide[i, pl.ds(pl.multiple_of(b * block + half, half), half), :]
+        return jnp.concatenate([left, right], axis=1)
+
+    here.barrier(True)
+    gather_start(0)
+    pack_start()
+    rows_start(0, tokens, tok)
+    gather_start(1)
+    gather_start(2)
+    rows_start(1, out_grad, og)
+
+    small[...] = jnp.zeros_like(small)
+    gather_hop(0)
+    pack_hop()
+    pack_end()
+    for r in range(n_rows):
+        own_part = pack_all[p, r]
+        vecs[0:8, r * share : (r + 1) * share] = own_part[0:8, :share]
+    for i in range(n_pair):
+        piece = pack_all[i, d * n_ctx]
+        for line in range(2):
+            for w in range(0, cols, 128):
+                n = min(128, cols - w)
+                row = 6 + 2 * line + w // 128
+                cold[line : line + 1, i * cols + w : i * cols + w + n] = piece[row : row + 1, :n]
+        for w in range(0, fw, 128):
+            row = 10 + w // 128
+            cold[2 + i : 3 + i, w : w + 128] = piece[row : row + 1, :]
+    gain_one, shift_one, out_shift = vecs[0:1, :], vecs[1:2, :], vecs[2:3, :]
+    gain_two, shift_two, down_shift = vecs[3:4, :], vecs[4:5, :], vecs[5:6, :]
+
+    rows_own[0].wait()
+    for k in range(n_ctx):
+        b = (z + k) % n_ctx
+        if k > 0:
+            arrive(tok.at[b], rows_sem.at[0, b])
+        scaled, _ = normalize(tok[b].astype(F32))
+        xn1[own_rows(b), :] = (scaled * gain_one + shift_one).astype(BF16)
+        rows_copy(1, b, xn1).start()
+
+    gather_turn(0)
+    gather_end(0)
+    for i in range(n_pair):
+        for a, base in enumerate((0, hw, 2 * hw)):
+            wqkv[:, base + i * cols : base + (i + 1) * cols] = full[0][i, :, a * cols : (a + 1) * cols]
+        wo[:, i * cols : (i + 1) * cols] = full[0][i, :, 3 * cols : 4 * cols]
+    gather_hop(1)
+    q_shift, v_shift = cold[0:1, :hw], cold[1:2, :hw]
+
+    @pl.loop(0, n_ctx)
+    def _(b):
+        rows_arrive(1, b, xn1)
+        product = nn_dot(xn1[block_rows(b), :], wqkv[...])
+        qs[block_rows(b), :] = (product[:, :hw] + q_shift).astype(BF16) * jnp.asarray(scale, BF16)
+        ks[block_rows(b), :] = product[:, hw : 2 * hw].astype(BF16)
+        vs[block_rows(b), :] = (product[:, 2 * hw :] + v_shift).astype(BF16)
+
+    gather_hop(2)
+
+    for b in range(n_ctx):
+        reach = (b + 1) * block
+        here_rows = slice(b * block, (b + 1) * block)
+
+        @pl.loop(0, n_twos)
+        def _(j):
+            at = pl.ds(pl.multiple_of(j * lanes, lanes), lanes)
+            queries, keys, values = qs[here_rows, at], ks[:reach, at], vs[:reach, at]
+            pieces = []
+            for e in range(2):
+                head = first_head if e == 0 else jnp.logical_not(first_head)
+                scores = nt_dot(jnp.where(head, queries, zero16), keys)
+                powers = jnp.exp(scores - jnp.max(scores, axis=-1, keepdims=True))
+                inverse = 1.0 / jnp.sum(powers, axis=-1, keepdims=True)
+                probs = (powers * inverse).astype(BF16)
+                p_first[b][2 * j + e] = probs
+                pieces.append(nn_dot(probs, values))
+            out = jnp.where(first_head, pieces[0], pieces[1])
+            o32[here_rows, at] = out
+            mixed[here_rows, at] = out.astype(BF16)
+
+        ssend[0, b] = nt_dot(mixed[far_rows(b), :], wo[...]).astype(BF16)
+        part_copy(2, 0, b).start()
+        hid[b] = nt_dot(mixed[own_rows(b), :], wo[...])
+        if b == 2:
+            gather_turn(1)
+
+    gather_end(1)
+    gather_turn(2)
+
+    @pl.loop(0, n_ctx)
+    def _(b):
+        part_copy(2, 0, b).wait()
+        hidden = tok[b].astype(F32) + (hid[b] + srecv[0, b].astype(F32)) + out_shift
+        hid[b] = hidden
+        scaled, _ = normalize(hidden)
+        xn2[own_rows(b), :] = (scaled * gain_two + shift_two).astype(BF16)
+        rows_copy(3, b, xn2).start()
+
+    rows_own[1].wait()
+    for k in range(n_ctx):
+        b = (z + k) % n_ctx
+        if k > 0:
+            arrive(og.at[b], rows_sem.at[1, b])
+        ogf[own_rows(b), :] = og[b]
+        swap(0, b, og.at[b], ogf.at[own_rows(b)]).start()
+
+    @pl.loop(0, n_ctx)
+    def _(b):
+        rows_arrive(3, b, xn2)
+        normed = xn2[block_rows(b), :]
+        for i in range(n_pair):
+            upward = nn_dot(normed, full[1][i]) + cold[2 + i : 3 + i, :fw]
+            big_phi = 0.5 + 0.5 * lax.erf(upward * root_half)
+            act[i, block_rows(b), :] = (upward * big_phi).astype(BF16)
+            slope = big_phi + upward * density_scale * jnp.exp(-0.5 * upward * upward)
+            ug[i, block_rows(b), :] = slope.astype(BF16)
+        rows_arrive(0, b, ogf)
+
+    step = 256
+
+    def transposed(ref, out):
+        for b in range(n_ctx):
+            out[:, b * block : (b + 1) * block] = ref[b * block : (b + 1) * block, :].T
+
+    transposed(ogf, trb)
+
+    @pl.loop(0, width // step)
+    def _(r):
+        rows = pl.ds(pl.multiple_of(r * step, step), step)
+        for i in range(n_pair):
+            dwd[i, rows, :] = nn_dot(trb[rows, :], act[i]).astype(BF16)
+
+    gathered = len(sends.started)
+    scatter_start(2, dwd)
+    gather_end(2)
+
+    def through(ref, weight, rows):
+        total = nt_dot(ref[0, rows, :], weight[0])
+        for i in range(1, n_pair):
+            total = total + nt_dot(ref[i, rows, :], weight[i])
+        return total
+
+    @pl.loop(0, n_ctx)
+    def _(b):
+        grads = ogf[block_rows(b), :]
+        for i in range(n_pair):
+            slope = ug[i, block_rows(b), :].astype(F32)
+            rows_grad = (nn_dot(grads, full[2][i]) * slope).astype(BF16)
+            ug[i, block_rows(b), :] = rows_grad
+            small[8 + i : 9 + i, :] += jnp.sum(rows_grad.astype(F32), axis=0, keepdims=True)
+        ssend[0, b] = through(ug, full[1], far_rows(b)).astype(BF16)
+        part_copy(5, 0, b).start()
+        ssend[1, b] = through(act, full[2], far_rows(b)).astype(BF16)
+        part_copy(4, 1, b).start()
+        part_store(1, b, through(ug, full[1], own_rows(b)))
+        part_store(0, b, through(act, full[2], own_rows(b)))
+
+    transposed(xn2, tra)
+    for copy in sends.started[:gathered]:
+        copy.wait_send()
+
+    @pl.loop(0, width // step)
+    def _(r):
+        rows = pl.ds(pl.multiple_of(r * step, step), step)
+        for i in range(n_pair):
+            full[1][i, rows, :] = nn_dot(tra[rows, :], ug[i]).astype(BF16)
+
+    scatter_start(1, full[1])
+
+    @pl.loop(0, n_ctx)
+    def _(b):
+        part_copy(5, 0, b).wait()
+        grad_two = part_load(1, b) + srecv[0, b].astype(F32)
+        part_copy(4, 1, b).wait()
+        lo[b] = (hid[b] + (part_load(0, b) + srecv[1, b].astype(F32)) + down_shift).astype(BF16)
+        scaled, spread = normalize(hid[b])
+        own_grad = og[b].astype(F32)
+        hidden_grad = own_grad + norm_back(grad_two * gain_two, scaled, spread)
+        hid[b] = hidden_grad
+        branch = hidden_grad.astype(BF16)
+        bg[own_rows(b), :] = branch
+        rows_copy(6, b, bg).start()
+        small[2:3, :] += jnp.sum(branch.astype(F32), axis=0, keepdims=True)
+        small[3:4, :] += jnp.sum(grad_two * scaled, axis=0, keepdims=True)
+        small[4:5, :] += jnp.sum(grad_two, axis=0, keepdims=True)
+        small[5:6, :] += jnp.sum(own_grad, axis=0, keepdims=True)
+
+    lo_copy = out_start(0, lo)
+
+    @pl.loop(0, n_ctx)
+    def _(b):
+        rows_arrive(6, b, bg)
+        dm[block_rows(b), :] = nn_dot(bg[block_rows(b), :], wo[...]).astype(BF16)
+
+    transposed(bg, trb)
+
+    @pl.loop(0, width // step)
+    def _(r):
+        rows = pl.ds(pl.multiple_of(r * step, step), step)
+        product = nn_dot(trb[rows, :], mixed[...])
+        for i in range(n_pair):
+            full[0][i, rows, 3 * cols : 4 * cols] = product[:, i * cols : (i + 1) * cols].astype(BF16)
+
+    scatter_turn(2, dwd)
+
+    for b in reversed(range(n_ctx)):
+        reach = (b + 1) * block
+        here_rows = slice(b * block, (b + 1) * block)
+
+        @pl.loop(0, n_twos)
+        def _(j):
+            at = pl.ds(pl.multiple_of(j * lanes, lanes), lanes)
+            queries, keys, values = qs[here_rows, at], ks[:reach, at], vs[:reach, at]
+            mix_grad, mix = dm[here_rows, at], o32[here_rows, at]
+            towards = mix_grad.astype(F32) * mix
+            query_parts, key_sum, value_sum = [], None, None
+            for e in range(2):
+                head = first_head if e == 0 else jnp.logical_not(first_head)
+                grad_head = jnp.where(head, mix_grad, zero16)
+                prob_grad = nt_dot(grad_head, values)
+                centre = jnp.sum(jnp.where(head, towards, 0.0), axis=-1, keepdims=True)
+                probs = p_first[b][2 * j + e]
+                score_grad = (probs.astype(F32) * (prob_grad - centre)).astype(BF16)
+                query_parts.append(nn_dot(score_grad, keys))
+                key_term = tn_dot(score_grad, jnp.where(head, queries, zero16))
+                value_term = tn_dot(probs, grad_head)
+                key_sum = key_term if key_sum is None else key_sum + key_term
+                value_sum = value_term if value_sum is None else value_sum + value_term
+            query_grad = jnp.where(first_head, query_parts[0], query_parts[1]) * scale
+            dqkv[here_rows, at] = query_grad.astype(BF16)
+            if b == n_ctx - 1:
+                wide[0, :, at] = key_sum
+                wide[1, :, at] = value_sum
+            else:
+                wide[0, :reach, at] += key_sum
+                wide[1, :reach, at] += value_sum
+
+        if b == n_ctx - 1:
+            scatter_turn(1, full[1])
+            out_hop(0, lo_copy)
+        if b == n_ctx - 2:
+            scatter_line(2, dwd)
+            out_cross(0)
+
+    scatter_line(1, full[1])
+
+    @pl.loop(0, n_ctx)
+    def _(b):
+        dqkv[block_rows(b), hw : 2 * hw] = wide[0, block_rows(b), :].astype(BF16)
+        dqkv[block_rows(b), 2 * hw :] = wide[1, block_rows(b), :].astype(BF16)
+        small[6:7, :hw] += jnp.sum(dqkv[block_rows(b), :hw].astype(F32), axis=0, keepdims=True)
+        small[7:8, :hw] += jnp.sum(dqkv[block_rows(b), 2 * hw :].astype(F32), axis=0, keepdims=True)
+        ssend[1, b] = nt_dot(dqkv[far_rows(b), :], wqkv[...]).astype(BF16)
+        part_copy(7, 1, b).start()
+
+    transposed(xn1, tra)
+
+    @pl.loop(0, width // step)
+    def _(r):
+        rows = pl.ds(pl.multiple_of(r * step, step), step)
+        product = nn_dot(tra[rows, :], dqkv[...])
+        for i in range(n_pair):
+            for a in range(3):
+                full[0][i, rows, a * cols : (a + 1) * cols] = product[
+                    :, a * hw + i * cols : a * hw + (i + 1) * cols
+                ].astype(BF16)
+
+    scatter_start(0, full[0])
+
+    @pl.loop(0, n_ctx)
+    def _(b):
+        own_part = nt_dot(dqkv[own_rows(b), :], wqkv[...])
+        part_copy(7, 1, b).wait()
+        grad_one = own_part + srecv[1, b].astype(F32)
+        scaled, spread = normalize(tok[b].astype(F32))
+        tg[b] = (hid[b] + norm_back(grad_one * gain_one, scaled, spread)).astype(BF16)
+        small[0:1, :] += jnp.sum(grad_one * scaled, axis=0, keepdims=True)
+        small[1:2, :] += jnp.sum(grad_one, axis=0, keepdims=True)
+        swap(0, b, og.at[b], ogf.at[own_rows(b)]).wait_send()
+        rows_copy(1, b, xn1).wait_send()
+        rows_copy(3, b, xn2).wait_send()
+        rows_copy(6, b, bg).wait_send()
+
+    tg_copy = out_start(1, tg)
+    sends.go(small.at[pl.ds(0, 8)], side_land, small_sem.at[0, 0], partner)
+    scatter_turn(0, full[0])
+    arrive(side_land, small_sem.at[0, 0])
+    small_b[0:6, :] = small[0:6, :] + side_land[0:6, :]
+    small_b[6:16, :] = small[6:16, :]
+    for k in range(1, n_ctx):
+        sends.go(small_b, ctx_small.at[k - 1], small_sem.at[1, k - 1], here.other_ctx(k)[1])
+    scatter_end(1, full[1])
+    scatter_end(2, dwd)
+    out_end(0)
+    scatter_line(0, full[0])
+    total = small_b[...]
+    for k in range(1, n_ctx):
+        arrive(ctx_small.at[k - 1], small_sem.at[1, k - 1])
+        total = total + ctx_small[k - 1]
+    small_c[...] = total
+    for k in range(1, n_pair):
+        sends.go(small_c, pair_small.at[k - 1], small_sem.at[2, k - 1], here.other_pair(k)[1])
+    out_hop(1, tg_copy)
+    total = small_c[...]
+    for k in range(1, n_pair):
+        arrive(pair_small.at[k - 1], small_sem.at[2, k - 1])
+        total = total + pair_small[k - 1]
+    small_d[...] = total
+    for k in range(1, n_dp):
+        sends.go(small_d, dp_small.at[k - 1], small_sem.at[3, k - 1], here.other_dp(k)[1])
+    out_cross(1)
+    scatter_end(0, full[0])
+    total = small_d[...]
+    for k in range(1, n_dp):
+        arrive(dp_small.at[k - 1], small_sem.at[3, k - 1])
+        total = total + dp_small[k - 1]
+    small_out[...] = total
+    out_end(1)
+    for copy in sends.started[gathered:]:
+        copy.wait_send()
+
+
+def fused_call(sizes, tokens, out_grad, pack, shards, cols):
+    n_dp, n_ctx, n_tp = sizes
+    n_pair = n_tp // 2
+    seqs, block, width = tokens.shape
+    half = block // 2
+    length = n_ctx * block
+    share = shards[0].shape[0]
+    fw = shards[1].shape[1]
+    hw = n_pair * cols
+    heads = hw // HEAD_DIM
+    two = n_ctx // 2
+    any_spec = pl.BlockSpec(memory_space=pl.ANY)
+    vmem_spec = pl.BlockSpec(memory_space=pltpu.VMEM)
+    shape = jax.ShapeDtypeStruct
+    vm = pltpu.VMEM
+    dma = pltpu.SemaphoreType.DMA
+    out_shape = [shape(tokens.shape, BF16)] * 2
+    out_shape += [shape(s.shape, F32) for s in shards]
+    out_shape += [shape((16, width), F32)]
+    scratch = [vm((n_pair, width, s.shape[1]), BF16) for s in shards]
+    scratch += [
+        vm((n_pair, n_dp * n_ctx) + pack.shape, F32),
+        vm((8, width), F32),
+        vm((8, width), F32),
+    ]
+    scratch += [vm((n_ctx, half, width), BF16)] * 4
+    scratch += [
+        vm((length, width), BF16),
+        vm((width, 3 * hw), BF16),
+        vm((width, hw), BF16),
+        vm((length, hw), BF16),
+        vm((length, hw), BF16),
+        vm((length, hw), BF16),
+        vm((length, hw), F32),
+        vm((length, hw), BF16),
+        vm((n_ctx, half, width), F32),
+        vm((length, width), BF16),
+        vm((length, width), BF16),
+        vm((n_pair, length, fw), BF16),
+        vm((n_pair, length, fw), BF16),
+        vm((length, width), BF16),
+        vm((length, hw), BF16),
+        vm((length, 3 * hw), BF16),
+        vm((width, length), BF16),
+        vm((width, length), BF16),
+        vm((2, length, hw), F32),
+        vm((2, n_ctx, half, width), BF16),
+        vm((2, n_ctx, half, width), BF16),
+        vm((n_pair, width, fw), BF16),
+        vm((16, width), F32),
+    ]
+    scratch += [vm((heads, block, (b + 1) * block), BF16) for b in range(n_ctx)]
+    wide = [s.shape[1] for s in shards]
+    scratch += [vm((n_dp - 1, n_pair, two * share, w), BF16) for w in wide]
+    scratch += [vm((n_pair - 1, n_dp, two * share, w), BF16) for w in wide]
+    scratch += [vm((n_pair - 1, two * share, w), BF16) for w in wide]
+    scratch += [vm((n_dp - 1, two * share, w), BF16) for w in wide]
+    scratch += [vm((n_ctx - 1, share, w), BF16) for w in wide]
+    scratch += [
+        vm((8, width), F32),
+        vm((16, width), F32),
+        vm((n_ctx - 1, 16, width), F32),
+        vm((16, width), F32),
+        vm((n_pair - 1, 16, width), F32),
+        vm((16, width), F32),
+        vm((n_dp - 1, 16, width), F32),
+    ]
+    most = max(n_dp, n_ctx, n_pair)
+    scratch += [
+        dma((8,)),
+        dma((200,)),
+        dma((2, n_ctx)),
+        dma((4, n_ctx)),
+        dma((4, n_pair)),
+        dma((4, n_dp)),
+        dma((3, n_pair, n_dp)),
+        dma((3, n_pair, n_dp)),
+        dma((8, n_ctx)),
+        dma((8, n_ctx)),
+        dma((3, 4, most, most)),
+        dma((3, n_ctx)),
+        dma((2, n_ctx)),
+        dma((2, seqs)),
+        dma((2, seqs)),
+        dma((4, most)),
+    ]
+    return pl.pallas_call(
+        functools.partial(fused_body, sizes, (half, width, share, cols, fw)),
+        out_shape=out_shape,
+        in_specs=[any_spec] * 6,
+        out_specs=[any_spec] * 2 + [vmem_spec] * 4,
+        scratch_shapes=scratch,
+        compiler_params=pltpu.CompilerParams(
+            collective_id=3, has_side_effects=True, vmem_limit_bytes=67043328
+        ),
+    )(tokens, out_grad, pack, *shards)
+
+
+def finish_body(n_ctx, share, cols, *refs):
+    lo_in, tg_in, attn, up, down, small = refs[:6]
+    lo, tg, dq, dk, dv, do, du, dd = refs[6:14]
+    vectors = refs[14:20]
+    shifts = refs[20:22]
+    up_shift = refs[22]
+    lo[...] = lo_in[...]
+    tg[...] = tg_in[...].astype(F32)
+    row = lax.axis_index("dp") * n_ctx + lax.axis_index("ctx")
+    pair = lax.axis_index("tp") // 2
+    width = small.shape[1]
+
+    @pl.when(pl.program_id(0) == 0)
+    def _():
+        for i, ref in enumerate((dq, dk, dv, do)):
+            ref[...] = attn[:, i * cols : (i + 1) * cols]
+        du[...] = up[...]
+        dd[...] = down[...]
+        turned = pltpu.roll(small[0:8, :], (width - row * share) % width, 1)
+        for i, ref in enumerate(vectors):
+            ref[...] = turned[i : i + 1, :share]
+        turned = pltpu.roll(small[0:8, :], (width - pair * cols) % width, 1)
+        for i, ref in enumerate(shifts):
+            ref[...] = turned[6 + i : 7 + i, :cols]
+        up_shift[...] = small[pl.ds(8 + pair, 1), :]
+
+
+def finish_call(sizes, cols, lo, tg, attn, up, down, small):
+    n_dp, n_ctx, n_tp = sizes
+    seqs, block, width = lo.shape
+    share = attn.shape[0]
+    shape = jax.ShapeDtypeStruct
+    rows = pl.BlockSpec((1, block, width), lambda i: (i, 0, 0))
+
+    def whole(s):
+        return pl.BlockSpec(s, lambda i: (0, 0))
+
+    out_tail = [(share, cols)] * 4 + [up.shape] * 2 + [(1, share)] * 6 + [(1, cols)] * 2 + [(1, up.shape[1])]
+    return pl.pallas_call(
+        functools.partial(finish_body, n_ctx, share, cols),
+        grid=(seqs,),
+        out_shape=[shape(lo.shape, BF16), shape(lo.shape, F32)] + [shape(s, F32) for s in out_tail],
+        in_specs=[rows, rows] + [whole(x.shape) for x in (attn, up, down, small)],
+        out_specs=[rows, rows] + [whole(s) for s in out_tail],
+    )(lo, tg, attn, up, down, small)
+
+
+def fused_layer(sizes, tokens, out_grad, shards, vectors, column_biases):
+    cols = shards[0].shape[1]
+    share = shards[0].shape[0]
+    attn = jnp.concatenate(shards[:4], axis=1)
+    pieces = [jnp.pad(v.astype(F32), (0, 128 - share)) for v in vectors]
+    pieces += [jnp.pad(b.astype(F32), (0, (-b.shape[0]) % 128)) for b in column_biases]
+    pack = jnp.concatenate(pieces).reshape(-1, 128)
+    results = fused_call(sizes, tokens, out_grad, pack, (attn, shards[4], shards[5]), cols)
+    final = finish_call(sizes, cols, *results)
+    return (*final[:8], *[v.reshape(v.shape[1]) for v in final[8:]])
+
+
 def per_device(
     tokens,
     out_grad,
@@ -819,16 +1550,19 @@
     cols = query_bias.shape[0]
     pair = lax.axis_index("tp") // 2
     row = lax.axis_index("dp") * n_ctx + lax.axis_index("ctx")
-
-    six = jnp.stack(
-        [norm1_gain, norm1_bias, output_bias, norm2_gain, norm2_bias, down_bias]
-    ).astype(F32)
+    shards = (query_weight, key_weight, value_weight, output_weight, up_weight, down_weight)
+    vectors = (norm1_gain, norm1_bias, output_bias, norm2_gain, norm2_bias, down_bias)
+    if share % 16 == 0 and n_ctx % 2 == 0:
+        return fused_layer(
+            sizes, tokens, out_grad, shards, vectors, (query_bias, value_bias, up_bias)
+        )
+
+    six = jnp.stack(vectors).astype(F32)
     vec = jnp.pad(six, ((0, 2), (0, 128 - share)))
     columns = jnp.arange(width) // cols == pair
     narrow = [jnp.where(columns, jnp.tile(b.astype(F32), width // cols), 0.0) for b in (query_bias, value_bias)]
     bias = jnp.pad(jnp.stack(narrow + [up_bias.astype(F32)]), ((0, 5), (0, 0)))
 
-    shards = (query_weight, key_weight, value_weight, output_weight, up_weight, down_weight)
     gathered = gather_call(sizes, tokens, out_grad, shards, vec, bias)
     tok, og = gathered[0:2]
     weights = [w.reshape(n_pair, width, w.shape[3]) for w in gathered[2:8]]

time: 375 us -> 267 us (0.71)
  Pallas kernels: 350 us -> 255 us
  local copies, waits for them, and re-layouts: 15.5 us -> 7.73 us
    pallas_call x3 -> x2, Pallas kernels: 350 us -> 255 us  [the longest x1 246 us: fused_call(): pl.pallas_call(functools.partial(fused_body, sizes, (half, width, share,...]
    dynamic_slice x9 -> x0, local copies, waits for them, and re-layouts: 5.37 us -> none  [the longest x6 3.49 us: per_device(): lax.dynamic_slice_in_dim(small[i], row * share, share)]
    convert_element_type x1 -> x0, other arithmetic: 5.31 us -> none  [per_device(): layer_out, tokens_grad = (final[0], final[1].astype(F32))]
    pad x0 -> x8, local copies, waits for them, and re-layouts: none -> 5.28 us  [the longest x6 3.96 us: fused_layer(): pieces = [jnp.pad(v.astype(F32), (0, 128 - share)) for v in vectors]]
    unnamed x23 -> x8, local copies, waits for them, and re-layouts: 5.69 us -> 1.61 us
where the time goes in v2:
time: 267 us
  Pallas kernels  255 us (96%)
  local copies, waits for them, and re-layouts  7.73 us (3%)
  other arithmetic  3.52 us (1%)
    pallas_call x1, Pallas kernels, fused_call(): pl.pallas_call(functools.partial(fused_body, sizes, (half, width, share,...  246 us
    pallas_call x1, Pallas kernels, finish_call(): pl.pallas_call(functools.partial(finish_body, n_ctx, share, cols), grid=(...  9.1 us

profile of v2, /device:TPU:25, one launch (start us, length us, event | category | flops | bytes accessed | tf_op | source)
XLA Modules:
  0.0 266.8 jit_solution(13103115155474567891)
XLA Ops:
  0.7 0.7 pad.34
  1.3 0.7 pad.35
  2.0 0.7 pad.36
  2.6 0.7 pad.37
  3.3 0.7 pad.38
  4.0 0.7 pad.39
  4.6 0.7 pad.40
  5.3 0.7 pad.41
  5.9 0.2 dynamic-update-slice
  6.1 0.2 dynamic-update-slice.1
  6.3 0.2 dynamic-update-slice.2
  6.5 0.2 dynamic-update-slice.3
  6.7 0.2 dynamic-update-slice.4
  6.9 0.2 dynamic-update-slice.5
  7.1 0.2 dynamic-update-slice.6
  7.4 0.2 dynamic-update-slice.7
  7.5 0.8 dynamic-update-slice.8
  8.4 0.6 bitcast_convert_fusion.refs_2_
  9.0 1.6 pad_maximum_fusion.refs_3_
  10.6 245.8 %shard_map.296 = (bf16[8,256,768]{2,1,0:T(8,128)(2,1)}, bf16[8,256,768]{2,1,0:T(8,128)(2,1)}, f32[96,768]{1,0:T(8,128)}, f32[96,768]{1,0:T(8,128)}, f32[96,768]{1,0:T(8,128)}, /*index=5*/f32[16,768]{1,0:T(8,128)}) custom-call(bf16[8,256,768]{2,1,0:T(8,128)(2,1)} %refs_0_.1, bf16[8,256,768]{2,1,0:T(8,128)(2,1)} %refs_1_.1, ...), custom_call_target="tpu_custom_call" | custom-call | tf_op jit(solution)/shard_map/pallas_call | solution.py:1454
  256.4 9.1 %shard_map.297 = (bf16[8,256,768]{2,1,0:T(8,128)(2,1)}, f32[8,256,768]{2,1,0:T(8,128)}, f32[96,192]{1,0:T(8,128)}, f32[96,192]{1,0:T(8,128)}, f32[96,192]{1,0:T(...) custom-call(bf16[8,256,768]{2,1,0:T(8,128)(2,1)} %get-tuple-element., ...), custom_call_target="tpu_custom_call" | custom-call | tf_op jit(solution)/shard_map/pallas_call | solution.py:1504
  265.5 1.3 reduce
  (1 shorter events, 0.0 us)

commit v3 on v2

--- a/solution.py
+++ b/solution.py
@@ -807,8 +807,10 @@
     def take(n):
         return [next(it) for _ in range(n)]
 
-    tokens, out_grad, pack = take(3)
-    shards = take(3)
+    tokens, out_grad = take(2)
+    narrow_shards = take(4)
+    shards = [None] + take(2)
+    vectors, column_biases = take(6), take(3)
     rows_out = take(2)
     owned = take(3)
     small_out = next(it)
@@ -817,15 +819,15 @@
     tok, og, lo, tg = take(4)
     (
         xn1, wqkv, wo, qs, ks, vs, o32, mixed, hid, xn2, ogf, act, ug, bg, dm, dqkv, tra, trb,
-        wide, ssend, srecv, dwd, small,
-    ) = take(23)
+        wide, whole, ssend, srecv, dwd, small,
+    ) = take(24)
     p_first = take(n_ctx)
-    dp_one, pair_one, pair_two, dp_two, ctx_land = take(3), take(3), take(3), take(3), take(3)
+    first_land, second_land, ctx_land = take(3), take(3), take(3)
     side_land, small_b, ctx_small, small_c, pair_small, small_d, dp_small = take(7)
     (
         own_sem, put_sem, rows_sem, line_sem, pair_sem, dp_sem, diag_dp_sem, diag_pair_sem, swap_send,
-        swap_recv, scatter_sem, ctx_sem, out_line, out_pair, out_side, small_sem,
-    ) = take(16)
+        swap_recv, first_sem, second_sem, ctx_sem, out_line, out_pair, out_side, small_sem,
+    ) = take(17)
     partner = here.partner()
     own_row = d * n_ctx + z
     mine = p * n_ctx + z
@@ -833,27 +835,43 @@
     first_head = lax.broadcasted_iota(jnp.int32, (1, lanes), 1) < HEAD_DIM
     zero16 = jnp.zeros((), BF16)
     side_rows = pl.ds(pl.multiple_of(c * half, half), half)
+    far_side = pl.ds(pl.multiple_of((1 - c) * half, half), half)
     sends = Sends(put_sem)
 
     def arrive(slot, sem):
         remote(slot, slot, put_sem.at[0], sem, partner).wait_recv()
 
+    def far_first():
+        upper = z // two
+        order = []
+        for i in range(n_ctx - 1):
+            down = n_ctx - 1 - i
+            down = down - (z - down + n_ctx) // n_ctx
+            up = i + (i - z + n_ctx) // n_ctx
+            zz = upper * up + (1 - upper) * down
+            order.append((zz, (d, zz, here.tp)))
+        return order
+
+    line_order = far_first()
+
     def shard_rows(r, count=1):
         return pl.ds(pl.multiple_of(r * share, 16), count * share)
 
     def slot(a, pp, dd, zz, count=1):
         return full[a].at[pp, shard_rows(dd * n_ctx + zz, count)]
 
-    gather_own = [pltpu.make_async_copy(shards[a], slot(a, p, d, z), own_sem.at[a]) for a in range(3)]
+    gather_own = [None] + [
+        pltpu.make_async_copy(shards[a], slot(a, p, d, z), own_sem.at[a]) for a in (1, 2)
+    ]
 
     def gather_start(a):
-        gather_own[a].start()
-        for k in range(1, n_ctx):
-            zz, device = here.other_ctx(k)
-            sends.go(shards[a], slot(a, p, d, z), line_sem.at[a, z], device)
+        source = slot(a, p, d, z) if a == 0 else shards[a]
+        for zz, device in line_order:
+            sends.go(source, slot(a, p, d, z), line_sem.at[a, z], device)
 
     def gather_hop(a):
-        gather_own[a].wait()
+        if a > 0:
+            gather_own[a].wait()
         for k in range(1, n_ctx):
             zz = here.other_ctx(k)[0]
             arrive(slot(a, p, d, zz), line_sem.at[a, zz])
@@ -886,12 +904,11 @@
                 arrive(slot(a, pp, dd, two, n_ctx - two), diag_pair_sem.at[a, pp, dd])
 
     def pack_start():
-        pack_own.start()
-        for k in range(1, n_ctx):
-            sends.go(pack, pack_all.at[p, own_row], line_sem.at[3, z], here.other_ctx(k)[1])
+        own = pack_all.at[p, own_row]
+        for zz, device in line_order:
+            sends.go(own, own, line_sem.at[3, z], device)
 
     def pack_hop():
-        pack_own.wait()
         for k in range(1, n_ctx):
             zz = here.other_ctx(k)[0]
             arrive(pack_all.at[p, d * n_ctx + zz], line_sem.at[3, zz])
@@ -909,31 +926,33 @@
             dd = here.other_dp(k)[0]
             arrive(pack_all.at[p, pl.ds(dd * n_ctx, n_ctx)], dp_sem.at[3, dd])
 
-    pack_own = pltpu.make_async_copy(pack, pack_all.at[p, own_row], own_sem.at[3])
-
     rows_own = [
         pltpu.make_async_copy(source.at[mine, side_rows], target.at[z], own_sem.at[4 + i])
         for i, (source, target) in enumerate(((tokens, tok), (out_grad, og)))
     ]
 
     def rows_start(i, source, target):
-        rows_own[i].start()
-        for k in range(1, n_ctx):
-            zz, device = here.other_ctx(k)
+        for zz, device in line_order:
             sends.go(source.at[p * n_ctx + zz, side_rows], target.at[z], rows_sem.at[i, z], device)
 
-    def grad_rows(ref, pp, dd, second):
-        return ref.at[pp, shard_rows(dd * n_ctx + (two if second else 0), two)]
-
-    def scatter_start(a, ref):
-        for k in range(1, n_dp):
-            dd, device = here.other_dp(k)
-            for i in range(n_pair):
-                sends.go(grad_rows(ref, i, dd, False), dp_one[a].at[k - 1, i], scatter_sem.at[a, 0, k - 1, i], device)
-        for k in range(1, n_pair):
-            pp, device = here.other_pair(k)
-            for i in range(n_dp):
-                sends.go(grad_rows(ref, pp, i, True), pair_one[a].at[k - 1, i], scatter_sem.at[a, 1, k - 1, i], device)
+    def grad_slot(ref, pp, dd, k):
+        return ref.at[pp, shard_rows(dd * n_ctx + (z + k) % n_ctx)]
+
+    def pair_leads(a, k):
+        return a == 2 and k % 2 == 1
+
+    def scatter_start(a, ref, ks):
+        for k in ks:
+            if pair_leads(a, k):
+                for j in range(1, n_pair):
+                    pp, device = here.other_pair(j)
+                    for i in range(n_dp):
+                        sends.go(grad_slot(ref, pp, i, k), first_land[a].at[j - 1, i, k], first_sem.at[a, j - 1, i, k], device)
+            else:
+                for j in range(1, n_dp):
+                    dd, device = here.other_dp(j)
+                    for i in range(n_pair):
+                        sends.go(grad_slot(ref, i, dd, k), first_land[a].at[j - 1, i, k], first_sem.at[a, j - 1, i, k], device)
 
     def add_into(target, parts):
         total = target[...].astype(F32)
@@ -941,32 +960,30 @@
             total = total + part[...].astype(F32)
         target[...] = total.astype(BF16)
 
-    def scatter_turn(a, ref):
-        for i in range(n_pair):
-            for k in range(1, n_dp):
-                arrive(dp_one[a].at[k - 1, i], scatter_sem.at[a, 0, k - 1, i])
-            add_into(grad_rows(ref, i, d, False), [dp_one[a].at[k - 1, i] for k in range(1, n_dp)])
-        for k in range(1, n_pair):
-            pp, device = here.other_pair(k)
-            sends.go(grad_rows(ref, pp, d, False), pair_two[a].at[k - 1], scatter_sem.at[a, 2, k - 1, 0], device)
-        for i in range(n_dp):
-            for k in range(1, n_pair):
-                arrive(pair_one[a].at[k - 1, i], scatter_sem.at[a, 1, k - 1, i])
-            add_into(grad_rows(ref, p, i, True), [pair_one[a].at[k - 1, i] for k in range(1, n_pair)])
-        for k in range(1, n_dp):
-            dd, device = here.other_dp(k)
-            sends.go(grad_rows(ref, p, dd, True), dp_two[a].at[k - 1], scatter_sem.at[a, 3, k - 1, 0], device)
-
-    def scatter_line(a, ref):
-        for k in range(1, n_pair):
-            arrive(pair_two[a].at[k - 1], scatter_sem.at[a, 2, k - 1, 0])
-        add_into(grad_rows(ref, p, d, False), [pair_two[a].at[k - 1] for k in range(1, n_pair)])
-        for k in range(1, n_dp):
-            arrive(dp_two[a].at[k - 1], scatter_sem.at[a, 3, k - 1, 0])
-        add_into(grad_rows(ref, p, d, True), [dp_two[a].at[k - 1] for k in range(1, n_dp)])
-        for k in range(1, n_ctx):
-            zz, device = here.other_ctx(k)
-            sends.go(ref.at[p, shard_rows(d * n_ctx + zz)], ctx_land[a].at[k - 1], ctx_sem.at[a, k - 1], device)
+    def scatter_turn(a, ref, ks):
+        for k in ks:
+            leads = pair_leads(a, k)
+            n_lead, n_next = (n_pair, n_dp) if leads else (n_dp, n_pair)
+            for i in range(n_next):
+                parts = [first_land[a].at[j - 1, i, k] for j in range(1, n_lead)]
+                for j in range(1, n_lead):
+                    arrive(parts[j - 1], first_sem.at[a, j - 1, i, k])
+                target = grad_slot(ref, p, i, k) if leads else grad_slot(ref, i, d, k)
+                add_into(target, parts)
+            for j in range(1, n_next):
+                other, device = here.other_dp(j) if leads else here.other_pair(j)
+                source = grad_slot(ref, p, other, k) if leads else grad_slot(ref, other, d, k)
+                sends.go(source, second_land[a].at[j - 1, k], second_sem.at[a, j - 1, k], device)
+
+    def scatter_line(a, ref, ks):
+        for k in ks:
+            n_next = n_dp if pair_leads(a, k) else n_pair
+            parts = [second_land[a].at[j - 1, k] for j in range(1, n_next)]
+            for j in range(1, n_next):
+                arrive(parts[j - 1], second_sem.at[a, j - 1, k])
+            add_into(grad_slot(ref, p, d, k), parts)
+            if k > 0:
+                sends.go(grad_slot(ref, p, d, k), ctx_land[a].at[k - 1], ctx_sem.at[a, k - 1], here.other_ctx(k)[1])
 
     def scatter_end(a, ref):
         total = ref[p, shard_rows(own_row), :].astype(F32)
@@ -975,31 +992,31 @@
             total = total + ctx_land[a][k - 1].astype(F32)
         owned[a][...] = total
 
+    near = list(range(1, n_ctx)) + [0]
+    early, late = near[:two], near[two:]
+
     def out_slot(i, s, rows):
         return rows_out[i].at[s, rows]
 
     def out_start(i, source):
-        for k in range(1, n_ctx):
-            zz, device = here.other_ctx(k)
+        for zz, device in line_order:
             sends.go(source.at[zz], out_slot(i, mine, side_rows), out_line.at[i, z], device)
         copy = pltpu.make_async_copy(source.at[z], out_slot(i, mine, side_rows), own_sem.at[6 + i])
         copy.start()
         return copy
 
-    def out_pass(i, s):
+    def out_pass(i, s, source):
         piece = out_slot(i, s, side_rows)
         for j in range(1, n_pair):
-            sends.go(piece, piece, out_pair.at[i, s], here.other_pair(j)[1])
-        sends.go(piece, piece, out_side.at[i, s], partner)
-
-    def out_hop(i, copy):
-        copy.wait()
-        out_pass(i, mine)
+            sends.go(source, piece, out_pair.at[i, s], here.other_pair(j)[1])
+        sends.go(source, piece, out_side.at[i, s], partner)
+
+    def out_hop(i):
         for k in range(1, n_ctx):
-            zz = here.other_ctx(k)[0]
-            s = p * n_ctx + zz
-            arrive(out_slot(i, s, side_rows), out_line.at[i, zz])
-            out_pass(i, s)
+            s = p * n_ctx + here.other_ctx(k)[0]
+            piece = out_slot(i, s, side_rows)
+            arrive(piece, out_line.at[i, here.other_ctx(k)[0]])
+            out_pass(i, s, piece)
 
     def out_cross(i):
         for j in range(1, n_pair):
@@ -1010,8 +1027,6 @@
                 arrive(piece, out_pair.at[i, s])
                 sends.go(piece, piece, out_side.at[i, s], partner)
 
-    far_side = pl.ds(pl.multiple_of((1 - c) * half, half), half)
-
     def out_end(i):
         for s in range(n_pair * n_ctx):
             arrive(out_slot(i, s, far_side), out_side.at[i, s])
@@ -1046,16 +1061,31 @@
         right = wide[i, pl.ds(pl.multiple_of(b * block + half, half), half), :]
         return jnp.concatenate([left, right], axis=1)
 
+    rows_own[0].start()
+    rows_own[1].start()
+    gather_own[1].start()
+    gather_own[2].start()
+    for a in range(4):
+        full[0][p, shard_rows(own_row), a * cols : (a + 1) * cols] = narrow_shards[a][...]
+    own_pack = pack_all.at[p, own_row]
+    own_pack[...] = jnp.zeros(own_pack.shape, F32)
+    for i in range(6):
+        own_pack[i : i + 1, :share] = vectors[i][...].astype(F32)
+    row = 6
+    for ref in column_biases:
+        n = ref.shape[1]
+        for w in range(0, n, 128):
+            m = min(128, n - w)
+            own_pack[row : row + 1, :m] = ref[:, w : w + m].astype(F32)
+            row += 1
+    small[...] = jnp.zeros_like(small)
     here.barrier(True)
+    pack_start()
     gather_start(0)
-    pack_start()
+    gather_start(1)
     rows_start(0, tokens, tok)
-    gather_start(1)
     gather_start(2)
     rows_start(1, out_grad, og)
-
-    small[...] = jnp.zeros_like(small)
-    gather_hop(0)
     pack_hop()
     pack_end()
     for r in range(n_rows):
@@ -1074,22 +1104,25 @@
     gain_one, shift_one, out_shift = vecs[0:1, :], vecs[1:2, :], vecs[2:3, :]
     gain_two, shift_two, down_shift = vecs[3:4, :], vecs[4:5, :], vecs[5:6, :]
 
-    rows_own[0].wait()
-    for k in range(n_ctx):
-        b = (z + k) % n_ctx
-        if k > 0:
-            arrive(tok.at[b], rows_sem.at[0, b])
+    def norm_one(b):
         scaled, _ = normalize(tok[b].astype(F32))
         xn1[own_rows(b), :] = (scaled * gain_one + shift_one).astype(BF16)
         rows_copy(1, b, xn1).start()
 
+    rows_own[0].wait()
+    norm_one(z)
+    gather_hop(0)
     gather_turn(0)
+    gather_hop(1)
+    for k in range(1, n_ctx):
+        b = here.other_ctx(k)[0]
+        arrive(tok.at[b], rows_sem.at[0, b])
+        norm_one(b)
     gather_end(0)
     for i in range(n_pair):
         for a, base in enumerate((0, hw, 2 * hw)):
             wqkv[:, base + i * cols : base + (i + 1) * cols] = full[0][i, :, a * cols : (a + 1) * cols]
         wo[:, i * cols : (i + 1) * cols] = full[0][i, :, 3 * cols : 4 * cols]
-    gather_hop(1)
     q_shift, v_shift = cold[0:1, :hw], cold[1:2, :hw]
 
     @pl.loop(0, n_ctx)
@@ -1099,8 +1132,6 @@
         qs[block_rows(b), :] = (product[:, :hw] + q_shift).astype(BF16) * jnp.asarray(scale, BF16)
         ks[block_rows(b), :] = product[:, hw : 2 * hw].astype(BF16)
         vs[block_rows(b), :] = (product[:, 2 * hw :] + v_shift).astype(BF16)
-
-    gather_hop(2)
 
     for b in range(n_ctx):
         reach = (b + 1) * block
@@ -1123,14 +1154,14 @@
             o32[here_rows, at] = out
             mixed[here_rows, at] = out.astype(BF16)
 
-        ssend[0, b] = nt_dot(mixed[far_rows(b), :], wo[...]).astype(BF16)
+        whole[b % 2] = nt_dot(mixed[here_rows, :], wo[...])
+        ssend[0, b] = whole[b % 2, far_side, :].astype(BF16)
         part_copy(2, 0, b).start()
-        hid[b] = nt_dot(mixed[own_rows(b), :], wo[...])
-        if b == 2:
+        hid[b] = whole[b % 2, side_rows, :]
+        if b == 0:
             gather_turn(1)
-
-    gather_end(1)
-    gather_turn(2)
+        if b == 1:
+            gather_hop(2)
 
     @pl.loop(0, n_ctx)
     def _(b):
@@ -1141,13 +1172,7 @@
         xn2[own_rows(b), :] = (scaled * gain_two + shift_two).astype(BF16)
         rows_copy(3, b, xn2).start()
 
-    rows_own[1].wait()
-    for k in range(n_ctx):
-        b = (z + k) % n_ctx
-        if k > 0:
-            arrive(og.at[b], rows_sem.at[1, b])
-        ogf[own_rows(b), :] = og[b]
-        swap(0, b, og.at[b], ogf.at[own_rows(b)]).start()
+    gather_end(1)
 
     @pl.loop(0, n_ctx)
     def _(b):
@@ -1159,6 +1184,15 @@
             act[i, block_rows(b), :] = (upward * big_phi).astype(BF16)
             slope = big_phi + upward * density_scale * jnp.exp(-0.5 * upward * upward)
             ug[i, block_rows(b), :] = slope.astype(BF16)
+
+    rows_own[1].wait()
+    for k in range(n_ctx):
+        b = (z + k) % n_ctx
+        if k > 0:
+            arrive(og.at[b], rows_sem.at[1, b])
+        swap(0, b, og.at[b], ogf.at[own_rows(b)]).start()
+        ogf[own_rows(b), :] = og[b]
+    for b in range(n_ctx):
         rows_arrive(0, b, ogf)
 
     step = 256
@@ -1168,6 +1202,8 @@
             out[:, b * block : (b + 1) * block] = ref[b * block : (b + 1) * block, :].T
 
     transposed(ogf, trb)
+    gather_turn(2)
+    gathered = len(sends.started)
 
     @pl.loop(0, width // step)
     def _(r):
@@ -1175,8 +1211,7 @@
         for i in range(n_pair):
             dwd[i, rows, :] = nn_dot(trb[rows, :], act[i]).astype(BF16)
 
-    gathered = len(sends.started)
-    scatter_start(2, dwd)
+    scatter_start(2, dwd, near)
     gather_end(2)
 
     def through(ref, weight, rows):
@@ -1193,14 +1228,17 @@
             rows_grad = (nn_dot(grads, full[2][i]) * slope).astype(BF16)
             ug[i, block_rows(b), :] = rows_grad
             small[8 + i : 9 + i, :] += jnp.sum(rows_grad.astype(F32), axis=0, keepdims=True)
-        ssend[0, b] = through(ug, full[1], far_rows(b)).astype(BF16)
+        whole[0] = through(ug, full[1], block_rows(b))
+        ssend[0, b] = whole[0, far_side, :].astype(BF16)
         part_copy(5, 0, b).start()
-        ssend[1, b] = through(act, full[2], far_rows(b)).astype(BF16)
+        part_store(1, b, whole[0, side_rows, :])
+        whole[1] = through(act, full[2], block_rows(b))
+        ssend[1, b] = whole[1, far_side, :].astype(BF16)
         part_copy(4, 1, b).start()
-        part_store(1, b, through(ug, full[1], own_rows(b)))
-        part_store(0, b, through(act, full[2], own_rows(b)))
+        part_store(0, b, whole[1, side_rows, :])
 
     transposed(xn2, tra)
+    scatter_turn(2, dwd, near)
     for copy in sends.started[:gathered]:
         copy.wait_send()
 
@@ -1210,7 +1248,7 @@
         for i in range(n_pair):
             full[1][i, rows, :] = nn_dot(tra[rows, :], ug[i]).astype(BF16)
 
-    scatter_start(1, full[1])
+    scatter_start(1, full[1], near)
 
     @pl.loop(0, n_ctx)
     def _(b):
@@ -1231,6 +1269,7 @@
         small[5:6, :] += jnp.sum(own_grad, axis=0, keepdims=True)
 
     lo_copy = out_start(0, lo)
+    out_pass(0, mine, lo.at[z])
 
     @pl.loop(0, n_ctx)
     def _(b):
@@ -1245,8 +1284,6 @@
         product = nn_dot(trb[rows, :], mixed[...])
         for i in range(n_pair):
             full[0][i, rows, 3 * cols : 4 * cols] = product[:, i * cols : (i + 1) * cols].astype(BF16)
-
-    scatter_turn(2, dwd)
 
     for b in reversed(range(n_ctx)):
         reach = (b + 1) * block
@@ -1280,14 +1317,12 @@
                 wide[0, :reach, at] += key_sum
                 wide[1, :reach, at] += value_sum
 
-        if b == n_ctx - 1:
-            scatter_turn(1, full[1])
-            out_hop(0, lo_copy)
-        if b == n_ctx - 2:
-            scatter_line(2, dwd)
-            out_cross(0)
-
-    scatter_line(1, full[1])
+        if b == 3:
+            scatter_line(2, dwd, near)
+        if b == 1:
+            scatter_turn(1, full[1], early)
+        if b == 0:
+            out_hop(0)
 
     @pl.loop(0, n_ctx)
     def _(b):
@@ -1295,8 +1330,10 @@
         dqkv[block_rows(b), 2 * hw :] = wide[1, block_rows(b), :].astype(BF16)
         small[6:7, :hw] += jnp.sum(dqkv[block_rows(b), :hw].astype(F32), axis=0, keepdims=True)
         small[7:8, :hw] += jnp.sum(dqkv[block_rows(b), 2 * hw :].astype(F32), axis=0, keepdims=True)
-        ssend[1, b] = nt_dot(dqkv[far_rows(b), :], wqkv[...]).astype(BF16)
+        whole[0] = nt_dot(dqkv[block_rows(b), :], wqkv[...])
+        ssend[1, b] = whole[0, far_side, :].astype(BF16)
         part_copy(7, 1, b).start()
+        part_store(0, b, whole[0, side_rows, :])
 
     transposed(xn1, tra)
 
@@ -1310,69 +1347,81 @@
                     :, a * hw + i * cols : a * hw + (i + 1) * cols
                 ].astype(BF16)
 
-    scatter_start(0, full[0])
+    scatter_start(0, full[0], near)
 
     @pl.loop(0, n_ctx)
     def _(b):
-        own_part = nt_dot(dqkv[own_rows(b), :], wqkv[...])
         part_copy(7, 1, b).wait()
-        grad_one = own_part + srecv[1, b].astype(F32)
+        grad_one = part_load(0, b) + srecv[1, b].astype(F32)
         scaled, spread = normalize(tok[b].astype(F32))
         tg[b] = (hid[b] + norm_back(grad_one * gain_one, scaled, spread)).astype(BF16)
         small[0:1, :] += jnp.sum(grad_one * scaled, axis=0, keepdims=True)
         small[1:2, :] += jnp.sum(grad_one, axis=0, keepdims=True)
+
+    sends.go(small.at[pl.ds(0, 8)], side_land, small_sem.at[0, 0], partner)
+    tg_copy = out_start(1, tg)
+    out_pass(1, mine, tg.at[z])
+    scatter_turn(1, full[1], late)
+    arrive(side_land, small_sem.at[0, 0])
+    small_b[0:6, :] = small[0:6, :] + side_land[0:6, :]
+    small_b[6:16, :] = small[6:16, :]
+    for k in range(1, n_pair):
+        sends.go(small_b, pair_small.at[k - 1], small_sem.at[2, k - 1], here.other_pair(k)[1])
+    out_cross(0)
+    scatter_line(1, full[1], early)
+    scatter_turn(0, full[0], early)
+    out_hop(1)
+    scatter_line(1, full[1], late)
+    scatter_turn(0, full[0], late)
+    total = small_b[...]
+    for k in range(1, n_pair):
+        arrive(pair_small.at[k - 1], small_sem.at[2, k - 1])
+        total = total + pair_small[k - 1]
+    small_c[...] = total
+    for k in range(1, n_dp):
+        sends.go(small_c, dp_small.at[k - 1], small_sem.at[3, k - 1], here.other_dp(k)[1])
+    scatter_line(0, full[0], near)
+    scatter_end(2, dwd)
+    scatter_end(1, full[1])
+    out_end(0)
+    total = small_c[...]
+    for k in range(1, n_dp):
+        arrive(dp_small.at[k - 1], small_sem.at[3, k - 1])
+        total = total + dp_small[k - 1]
+    small_d[...] = total
+    for k in range(1, n_ctx):
+        sends.go(small_d, ctx_small.at[k - 1], small_sem.at[1, k - 1], here.other_ctx(k)[1])
+    out_cross(1)
+    scatter_end(0, full[0])
+    total = small_d[...]
+    for k in range(1, n_ctx):
+        arrive(ctx_small.at[k - 1], small_sem.at[1, k - 1])
+        total = total + ctx_small[k - 1]
+    small_out[...] = total
+    out_end(1)
+    lo_copy.wait()
+    tg_copy.wait()
+
+    @pl.loop(0, n_ctx)
+    def _(b):
         swap(0, b, og.at[b], ogf.at[own_rows(b)]).wait_send()
         rows_copy(1, b, xn1).wait_send()
         rows_copy(3, b, xn2).wait_send()
         rows_copy(6, b, bg).wait_send()
 
-    tg_copy = out_start(1, tg)
-    sends.go(small.at[pl.ds(0, 8)], side_land, small_sem.at[0, 0], partner)
-    scatter_turn(0, full[0])
-    arrive(side_land, small_sem.at[0, 0])
-    small_b[0:6, :] = small[0:6, :] + side_land[0:6, :]
-    small_b[6:16, :] = small[6:16, :]
-    for k in range(1, n_ctx):
-        sends.go(small_b, ctx_small.at[k - 1], small_sem.at[1, k - 1], here.other_ctx(k)[1])
-    scatter_end(1, full[1])
-    scatter_end(2, dwd)
-    out_end(0)
-    scatter_line(0, full[0])
-    total = small_b[...]
-    for k in range(1, n_ctx):
-        arrive(ctx_small.at[k - 1], small_sem.at[1, k - 1])
-        total = total + ctx_small[k - 1]
-    small_c[...] = total
-    for k in range(1, n_pair):
-        sends.go(small_c, pair_small.at[k - 1], small_sem.at[2, k - 1], here.other_pair(k)[1])
-    out_hop(1, tg_copy)
-    total = small_c[...]
-    for k in range(1, n_pair):
-        arrive(pair_small.at[k - 1], small_sem.at[2, k - 1])
-        total = total + pair_small[k - 1]
-    small_d[...] = total
-    for k in range(1, n_dp):
-        sends.go(small_d, dp_small.at[k - 1], small_sem.at[3, k - 1], here.other_dp(k)[1])
-    out_cross(1)
-    scatter_end(0, full[0])
-    total = small_d[...]
-    for k in range(1, n_dp):
-        arrive(dp_small.at[k - 1], small_sem.at[3, k - 1])
-        total = total + dp_small[k - 1]
-    small_out[...] = total
-    out_end(1)
     for copy in sends.started[gathered:]:
         copy.wait_send()
 
 
-def fused_call(sizes, tokens, out_grad, pack, shards, cols):
+def fused_call(sizes, tokens, out_grad, shards, vectors, column_biases):
     n_dp, n_ctx, n_tp = sizes
     n_pair = n_tp // 2
     seqs, block, width = tokens.shape
     half = block // 2
     length = n_ctx * block
-    share = shards[0].shape[0]
-    fw = shards[1].shape[1]
+    share, cols = shards[0].shape
+    fw = shards[4].shape[1]
+    widths = [4 * cols, fw, fw]
     hw = n_pair * cols
     heads = hw // HEAD_DIM
     two = n_ctx // 2
@@ -1382,11 +1431,11 @@
     vm = pltpu.VMEM
     dma = pltpu.SemaphoreType.DMA
     out_shape = [shape(tokens.shape, BF16)] * 2
-    out_shape += [shape(s.shape, F32) for s in shards]
+    out_shape += [shape((share, w), F32) for w in widths]
     out_shape += [shape((16, width), F32)]
-    scratch = [vm((n_pair, width, s.shape[1]), BF16) for s in shards]
+    scratch = [vm((n_pair, width, w), BF16) for w in widths]
     scratch += [
-        vm((n_pair, n_dp * n_ctx) + pack.shape, F32),
+        vm((n_pair, n_dp * n_ctx, 16, 128), F32),
         vm((8, width), F32),
         vm((8, width), F32),
     ]
@@ -1411,18 +1460,17 @@
         vm((width, length), BF16),
         vm((width, length), BF16),
         vm((2, length, hw), F32),
+        vm((2, block, width), F32),
         vm((2, n_ctx, half, width), BF16),
         vm((2, n_ctx, half, width), BF16),
         vm((n_pair, width, fw), BF16),
         vm((16, width), F32),
     ]
     scratch += [vm((heads, block, (b + 1) * block), BF16) for b in range(n_ctx)]
-    wide = [s.shape[1] for s in shards]
-    scratch += [vm((n_dp - 1, n_pair, two * share, w), BF16) for w in wide]
-    scratch += [vm((n_pair - 1, n_dp, two * share, w), BF16) for w in wide]
-    scratch += [vm((n_pair - 1, two * share, w), BF16) for w in wide]
-    scratch += [vm((n_dp - 1, two * share, w), BF16) for w in wide]
-    scratch += [vm((n_ctx - 1, share, w), BF16) for w in wide]
+    lead, after = max(n_dp, n_pair) - 1, max(n_dp, n_pair)
+    scratch += [vm((lead, after, n_ctx, share, w), BF16) for w in widths]
+    scratch += [vm((lead, n_ctx, share, w), BF16) for w in widths]
+    scratch += [vm((n_ctx - 1, share, w), BF16) for w in widths]
     scratch += [
         vm((8, width), F32),
         vm((16, width), F32),
@@ -1435,7 +1483,7 @@
     most = max(n_dp, n_ctx, n_pair)
     scratch += [
         dma((8,)),
-        dma((200,)),
+        dma((260,)),
         dma((2, n_ctx)),
         dma((4, n_ctx)),
         dma((4, n_pair)),
@@ -1444,7 +1492,8 @@
         dma((3, n_pair, n_dp)),
         dma((8, n_ctx)),
         dma((8, n_ctx)),
-        dma((3, 4, most, most)),
+        dma((3, lead, after, n_ctx)),
+        dma((3, lead, n_ctx)),
         dma((3, n_ctx)),
         dma((2, n_ctx)),
         dma((2, seqs)),
@@ -1454,13 +1503,13 @@
     return pl.pallas_call(
         functools.partial(fused_body, sizes, (half, width, share, cols, fw)),
         out_shape=out_shape,
-        in_specs=[any_spec] * 6,
+        in_specs=[any_spec] * 2 + [vmem_spec] * 4 + [any_spec] * 2 + [vmem_spec] * 9,
         out_specs=[any_spec] * 2 + [vmem_spec] * 4,
         scratch_shapes=scratch,
         compiler_params=pltpu.CompilerParams(
             collective_id=3, has_side_effects=True, vmem_limit_bytes=67043328
         ),
-    )(tokens, out_grad, pack, *shards)
+    )(tokens, out_grad, *shards, *vectors, *column_biases)
 
 
 def finish_body(n_ctx, share, cols, *refs):
@@ -1487,7 +1536,9 @@
         turned = pltpu.roll(small[0:8, :], (width - pair * cols) % width, 1)
         for i, ref in enumerate(shifts):
             ref[...] = turned[6 + i : 7 + i, :cols]
-        up_shift[...] = small[pl.ds(8 + pair, 1), :]
+        row_of = small[pl.ds(8 + pair, 1), :]
+        for i in range(up_shift.shape[0]):
+            up_shift[i : i + 1, :] = row_of[:, i * 128 : (i + 1) * 128]
 
 
 def finish_call(sizes, cols, lo, tg, attn, up, down, small):
@@ -1500,7 +1551,7 @@
     def whole(s):
         return pl.BlockSpec(s, lambda i: (0, 0))
 
-    out_tail = [(share, cols)] * 4 + [up.shape] * 2 + [(1, share)] * 6 + [(1, cols)] * 2 + [(1, up.shape[1])]
+    out_tail = [(share, cols)] * 4 + [up.shape] * 2 + [(1, share)] * 6 + [(1, cols)] * 2 + [(up.shape[1] // 128, 128)]
     return pl.pallas_call(
         functools.partial(finish_body, n_ctx, share, cols),
         grid=(seqs,),
@@ -1512,14 +1563,10 @@
 
 def fused_layer(sizes, tokens, out_grad, shards, vectors, column_biases):
     cols = shards[0].shape[1]
-    share = shards[0].shape[0]
-    attn = jnp.concatenate(shards[:4], axis=1)
-    pieces = [jnp.pad(v.astype(F32), (0, 128 - share)) for v in vectors]
-    pieces += [jnp.pad(b.astype(F32), (0, (-b.shape[0]) % 128)) for b in column_biases]
-    pack = jnp.concatenate(pieces).reshape(-1, 128)
-    results = fused_call(sizes, tokens, out_grad, pack, (attn, shards[4], shards[5]), cols)
+    lines = [v.reshape(1, -1) for v in (*vectors, *column_biases)]
+    results = fused_call(sizes, tokens, out_grad, shards, lines[:6], lines[6:])
     final = finish_call(sizes, cols, *results)
-    return (*final[:8], *[v.reshape(v.shape[1]) for v in final[8:]])
+    return (*final[:8], *[v.reshape(-1) for v in final[8:]])
 
 
 def per_device(

time: 267 us -> 222 us (0.83); the launches traced: 267 us -> 218 us
  Pallas kernels: 255 us -> 214 us
  local copies, waits for them, and re-layouts: 7.73 us -> 3.7 us
  other arithmetic: 3.52 us -> 0 us
    pallas_call x1, Pallas kernels: 246 us -> 205 us  [fused_call(): pl.pallas_call(functools.partial(fused_body, sizes, (half, width, share,...]
    pad x8 -> x0, local copies, waits for them, and re-layouts: 5.28 us -> none  [the longest x6 3.96 us: fused_layer(): pieces = [jnp.pad(v.astype(F32), (0, 128 - share)) for v in vectors]]
    reshape x0 -> x3, local copies, waits for them, and re-layouts: none -> 3.7 us  [fused_layer(): lines = [v.reshape(1, -1) for v in (*vectors, *column_biases)]]
where the time goes in v3:
time: 222 us; the launch traced here: 218 us
  Pallas kernels  214 us (96%)
  local copies, waits for them, and re-layouts  3.7 us (2%)
    pallas_call x1, Pallas kernels, fused_call(): pl.pallas_call(functools.partial(fused_body, sizes, (half, width, share,...  205 us
    pallas_call x1, Pallas kernels, finish_call(): pl.pallas_call(functools.partial(finish_body, n_ctx, share, cols), grid=(...  9.1 us

profile of v3, /device:TPU:25, one launch (start us, length us, event | category | flops | bytes accessed | tf_op | source)
XLA Modules:
  0.0 218.3 jit_solution(14774339792956461975)
XLA Ops:
  0.7 1.2 reshape.94.refs_14_
  1.9 1.2 reshape.95.refs_15_
  3.1 1.3 reshape.96.refs_16_
  4.4 204.7 %shard_map.296 = (bf16[8,256,768]{2,1,0:T(8,128)(2,1)}, bf16[8,256,768]{2,1,0:T(8,128)(2,1)}, f32[96,768]{1,0:T(8,128)}, f32[96,768]{1,0:T(8,128)}, f32[96,768]{1,0:T(8,128)}, /*index=5*/f32[16,768]{1,0:T(8,128)}) custom-call(bf16[8,256,768]{2,1,0:T(8,128)(2,1)} %refs_0_.1, bf16[8,256,768]{2,1,0:T(8,128)(2,1)} %refs_1_.1, bf16[96,192]{1,0:T(8,128)(2,1)} %refs_2_.1, ...), custom_call_target="tpu_custom_call" | custom-call | tf_op jit(solution)/shard_map/pallas_call | solution.py:1503
  209.1 9.1 %shard_map.297 = (bf16[8,256,768]{2,1,0:T(8,128)(2,1)}, f32[8,256,768]{2,1,0:T(8,128)}, f32[96,192]{1,0:T(8,128)}, f32[96,192]{1,0:T(8,128)}, f32[96,192]{1,0:T(...) custom-call(bf16[8,256,768]{2,1,0:T(8,128)(2,1)} %get-tuple-element., ...), custom_call_target="tpu_custom_call" | custom-call | tf_op jit(solution)/shard_map/pallas_call | solution.py:1555

commit v4 on v3

--- a/solution.py
+++ b/solution.py
@@ -827,7 +827,8 @@
     (
         own_sem, put_sem, rows_sem, line_sem, pair_sem, dp_sem, diag_dp_sem, diag_pair_sem, swap_send,
         swap_recv, first_sem, second_sem, ctx_sem, out_line, out_pair, out_side, small_sem,
-    ) = take(17)
+        side_sem,
+    ) = take(18)
     partner = here.partner()
     own_row = d * n_ctx + z
     mine = p * n_ctx + z
@@ -854,6 +855,12 @@
 
     line_order = far_first()
 
+    def flipped(h):
+        zz = z + h - 2 * h * ((z // h) % 2)
+        return zz, (d, zz, here.tp)
+
+    strides = [1 << i for i in range(n_ctx.bit_length() - 1)]
+
     def shard_rows(r, count=1):
         return pl.ds(pl.multiple_of(r * share, 16), count * share)
 
@@ -864,17 +871,31 @@
         pltpu.make_async_copy(shards[a], slot(a, p, d, z), own_sem.at[a]) for a in (1, 2)
     ]
 
+    def gather_give(a, h):
+        device = flipped(h)[1]
+        for i in range(n_ctx // (2 * h)):
+            zz = (z + 2 * h * i) % n_ctx
+            source = shards[a] if a > 0 and i == 0 else slot(a, p, d, zz)
+            sends.go(source, slot(a, p, d, zz), line_sem.at[a, zz], device)
+
+    def gather_take(a, h):
+        q = flipped(h)[0]
+        for i in range(n_ctx // (2 * h)):
+            zz = (q + 2 * h * i) % n_ctx
+            arrive(slot(a, p, d, zz), line_sem.at[a, zz])
+
     def gather_start(a):
-        source = slot(a, p, d, z) if a == 0 else shards[a]
-        for zz, device in line_order:
-            sends.go(source, slot(a, p, d, z), line_sem.at[a, z], device)
+        gather_give(a, strides[-1])
+
+    def gather_next(a):
+        for h in reversed(strides[:-1]):
+            gather_take(a, 2 * h)
+            gather_give(a, h)
 
     def gather_hop(a):
         if a > 0:
             gather_own[a].wait()
-        for k in range(1, n_ctx):
-            zz = here.other_ctx(k)[0]
-            arrive(slot(a, p, d, zz), line_sem.at[a, zz])
+        gather_take(a, 1)
         group = slot(a, p, d, 0, n_ctx)
         for k in range(1, n_pair):
             sends.go(group, group, pair_sem.at[a, p], here.other_pair(k)[1])
@@ -939,7 +960,7 @@
         return ref.at[pp, shard_rows(dd * n_ctx + (z + k) % n_ctx)]
 
     def pair_leads(a, k):
-        return a == 2 and k % 2 == 1
+        return k == 1 if a == 0 else near.index(k) % 2 == 0
 
     def scatter_start(a, ref, ks):
         for k in ks:
@@ -982,18 +1003,31 @@
             for j in range(1, n_next):
                 arrive(parts[j - 1], second_sem.at[a, j - 1, k])
             add_into(grad_slot(ref, p, d, k), parts)
-            if k > 0:
-                sends.go(grad_slot(ref, p, d, k), ctx_land[a].at[k - 1], ctx_sem.at[a, k - 1], here.other_ctx(k)[1])
+            if k % 2 == 1:
+                scatter_give(a, ref, 1, k)
+
+    def scatter_give(a, ref, h, k):
+        zz, device = flipped(h)
+        at = n_ctx - n_ctx // h + ((z + k - zz + n_ctx) % n_ctx) // (2 * h)
+        sends.go(grad_slot(ref, p, d, k), ctx_land[a].at[at], ctx_sem.at[a, at], device)
+
+    def scatter_across(a, ref):
+        for h in strides[1:]:
+            for i in range(n_ctx // h):
+                at = n_ctx - 2 * n_ctx // h + i
+                arrive(ctx_land[a].at[at], ctx_sem.at[a, at])
+                add_into(grad_slot(ref, p, d, i * h), [ctx_land[a].at[at]])
+            for k in range(h, n_ctx, 2 * h):
+                scatter_give(a, ref, h, k)
 
     def scatter_end(a, ref):
-        total = ref[p, shard_rows(own_row), :].astype(F32)
-        for k in range(1, n_ctx):
-            arrive(ctx_land[a].at[k - 1], ctx_sem.at[a, k - 1])
-            total = total + ctx_land[a][k - 1].astype(F32)
-        owned[a][...] = total
-
-    near = list(range(1, n_ctx)) + [0]
+        last = n_ctx - 2
+        arrive(ctx_land[a].at[last], ctx_sem.at[a, last])
+        owned[a][...] = ref[p, shard_rows(own_row), :].astype(F32) + ctx_land[a][last].astype(F32)
+
+    near = [k for h in strides for k in range(h, n_ctx, 2 * h)] + [0]
     early, late = near[:two], near[two:]
+    others = list(range(1, n_ctx))
 
     def out_slot(i, s, rows):
         return rows_out[i].at[s, rows]
@@ -1011,8 +1045,8 @@
             sends.go(source, piece, out_pair.at[i, s], here.other_pair(j)[1])
         sends.go(source, piece, out_side.at[i, s], partner)
 
-    def out_hop(i):
-        for k in range(1, n_ctx):
+    def out_hop(i, ks):
+        for k in ks:
             s = p * n_ctx + here.other_ctx(k)[0]
             piece = out_slot(i, s, side_rows)
             arrive(piece, out_line.at[i, here.other_ctx(k)[0]])
@@ -1082,10 +1116,8 @@
     here.barrier(True)
     pack_start()
     gather_start(0)
+    gather_next(0)
     gather_start(1)
-    rows_start(0, tokens, tok)
-    gather_start(2)
-    rows_start(1, out_grad, og)
     pack_hop()
     pack_end()
     for r in range(n_rows):
@@ -1112,6 +1144,11 @@
     rows_own[0].wait()
     norm_one(z)
     gather_hop(0)
+    gather_next(1)
+    pl.semaphore_signal(side_sem, inc=1, device_id=partner, device_id_type=MESH)
+    pl.semaphore_wait(side_sem, 1)
+    rows_start(0, tokens, tok)
+    gather_start(2)
     gather_turn(0)
     gather_hop(1)
     for k in range(1, n_ctx):
@@ -1132,6 +1169,8 @@
         qs[block_rows(b), :] = (product[:, :hw] + q_shift).astype(BF16) * jnp.asarray(scale, BF16)
         ks[block_rows(b), :] = product[:, hw : 2 * hw].astype(BF16)
         vs[block_rows(b), :] = (product[:, 2 * hw :] + v_shift).astype(BF16)
+
+    gather_next(2)
 
     for b in range(n_ctx):
         reach = (b + 1) * block
@@ -1158,9 +1197,10 @@
         ssend[0, b] = whole[b % 2, far_side, :].astype(BF16)
         part_copy(2, 0, b).start()
         hid[b] = whole[b % 2, side_rows, :]
-        if b == 0:
+        if b == 1:
             gather_turn(1)
-        if b == 1:
+            rows_start(1, out_grad, og)
+        if b == 2:
             gather_hop(2)
 
     @pl.loop(0, n_ctx)
@@ -1202,8 +1242,6 @@
             out[:, b * block : (b + 1) * block] = ref[b * block : (b + 1) * block, :].T
 
     transposed(ogf, trb)
-    gather_turn(2)
-    gathered = len(sends.started)
 
     @pl.loop(0, width // step)
     def _(r):
@@ -1211,7 +1249,20 @@
         for i in range(n_pair):
             dwd[i, rows, :] = nn_dot(trb[rows, :], act[i]).astype(BF16)
 
+    gather_turn(2)
+    gathered = len(sends.started)
     scatter_start(2, dwd, near)
+
+    def slope_back(i, b):
+        slope = ug[i, block_rows(b), :].astype(F32)
+        rows_grad = (nn_dot(ogf[block_rows(b), :], full[2][i]) * slope).astype(BF16)
+        ug[i, block_rows(b), :] = rows_grad
+        small[pl.ds(8 + i, 1), :] += jnp.sum(rows_grad.astype(F32), axis=0, keepdims=True)
+
+    @pl.loop(0, n_ctx)
+    def _(b):
+        slope_back(p, b)
+
     gather_end(2)
 
     def through(ref, weight, rows):
@@ -1220,14 +1271,9 @@
             total = total + nt_dot(ref[i, rows, :], weight[i])
         return total
 
-    @pl.loop(0, n_ctx)
-    def _(b):
-        grads = ogf[block_rows(b), :]
-        for i in range(n_pair):
-            slope = ug[i, block_rows(b), :].astype(F32)
-            rows_grad = (nn_dot(grads, full[2][i]) * slope).astype(BF16)
-            ug[i, block_rows(b), :] = rows_grad
-            small[8 + i : 9 + i, :] += jnp.sum(rows_grad.astype(F32), axis=0, keepdims=True)
+    def units_back(b):
+        for k in range(1, n_pair):
+            slope_back(here.other_pair(k)[0], b)
         whole[0] = through(ug, full[1], block_rows(b))
         ssend[0, b] = whole[0, far_side, :].astype(BF16)
         part_copy(5, 0, b).start()
@@ -1237,8 +1283,11 @@
         part_copy(4, 1, b).start()
         part_store(0, b, whole[1, side_rows, :])
 
+    pl.loop(0, two)(units_back)
+    scatter_turn(2, dwd, early)
+    pl.loop(two, n_ctx)(units_back)
     transposed(xn2, tra)
-    scatter_turn(2, dwd, near)
+    scatter_turn(2, dwd, late)
     for copy in sends.started[:gathered]:
         copy.wait_send()
 
@@ -1249,6 +1298,7 @@
             full[1][i, rows, :] = nn_dot(tra[rows, :], ug[i]).astype(BF16)
 
     scatter_start(1, full[1], near)
+    scatter_line(2, dwd, early)
 
     @pl.loop(0, n_ctx)
     def _(b):
@@ -1276,6 +1326,7 @@
         rows_arrive(6, b, bg)
         dm[block_rows(b), :] = nn_dot(bg[block_rows(b), :], wo[...]).astype(BF16)
 
+    scatter_line(2, dwd, late)
     transposed(bg, trb)
 
     @pl.loop(0, width // step)
@@ -1317,12 +1368,10 @@
                 wide[0, :reach, at] += key_sum
                 wide[1, :reach, at] += value_sum
 
-        if b == 3:
-            scatter_line(2, dwd, near)
         if b == 1:
-            scatter_turn(1, full[1], early)
+            scatter_turn(1, full[1], near)
         if b == 0:
-            out_hop(0)
+            out_hop(0, others)
 
     @pl.loop(0, n_ctx)
     def _(b):
@@ -1361,18 +1410,19 @@
     sends.go(small.at[pl.ds(0, 8)], side_land, small_sem.at[0, 0], partner)
     tg_copy = out_start(1, tg)
     out_pass(1, mine, tg.at[z])
-    scatter_turn(1, full[1], late)
+    scatter_line(1, full[1], near)
+    scatter_across(2, dwd)
     arrive(side_land, small_sem.at[0, 0])
     small_b[0:6, :] = small[0:6, :] + side_land[0:6, :]
     small_b[6:16, :] = small[6:16, :]
     for k in range(1, n_pair):
         sends.go(small_b, pair_small.at[k - 1], small_sem.at[2, k - 1], here.other_pair(k)[1])
+    scatter_turn(0, full[0], early)
     out_cross(0)
-    scatter_line(1, full[1], early)
-    scatter_turn(0, full[0], early)
-    out_hop(1)
-    scatter_line(1, full[1], late)
+    scatter_line(0, full[0], early)
     scatter_turn(0, full[0], late)
+    out_hop(1, others)
+    scatter_across(1, full[1])
     total = small_b[...]
     for k in range(1, n_pair):
         arrive(pair_small.at[k - 1], small_sem.at[2, k - 1])
@@ -1380,7 +1430,8 @@
     small_c[...] = total
     for k in range(1, n_dp):
         sends.go(small_c, dp_small.at[k - 1], small_sem.at[3, k - 1], here.other_dp(k)[1])
-    scatter_line(0, full[0], near)
+    scatter_line(0, full[0], late)
+    scatter_across(0, full[0])
     scatter_end(2, dwd)
     scatter_end(1, full[1])
     out_end(0)
@@ -1499,6 +1550,7 @@
         dma((2, seqs)),
         dma((2, seqs)),
         dma((4, most)),
+        pltpu.SemaphoreType.REGULAR,
     ]
     return pl.pallas_call(
         functools.partial(fused_body, sizes, (half, width, share, cols, fw)),

time: 222 us -> 200 us (0.901)
  Pallas kernels: 214 us -> 192 us
    pallas_call x1, Pallas kernels: 205 us -> 183 us  [fused_call(): pl.pallas_call(functools.partial(fused_body, sizes, (half, width, share,...]
where the time goes in v4:
time: 200 us; the launch traced here: 197 us
  Pallas kernels  192 us (96%)
  local copies, waits for them, and re-layouts  3.7 us (2%)
    pallas_call x1, Pallas kernels, fused_call(): pl.pallas_call(functools.partial(fused_body, sizes, (half, width, share,...  183 us
    pallas_call x1, Pallas kernels, finish_call(): pl.pallas_call(functools.partial(finish_body, n_ctx, share, cols), grid=(...  9.1 us

profile of v4, /device:TPU:25, one launch (start us, length us, event | category | flops | bytes accessed | tf_op | source)
XLA Modules:
  0.0 196.9 jit_solution(10184965980962125216)
XLA Ops:
  0.7 1.2 reshape.94.refs_14_
  1.9 1.2 reshape.95.refs_15_
  3.1 1.3 reshape.96.refs_16_
  4.4 183.3 %shard_map.296 = (bf16[8,256,768]{2,1,0:T(8,128)(2,1)}, bf16[8,256,768]{2,1,0:T(8,128)(2,1)}, f32[96,768]{1,0:T(8,128)}, f32[96,768]{1,0:T(8,128)}, f32[96,768]{1,0:T(8,128)}, /*index=5*/f32[16,768]{1,0:T(8,128)}) custom-call(bf16[8,256,768]{2,1,0:T(8,128)(2,1)} %refs_0_.1, bf16[8,256,768]{2,1,0:T(8,128)(2,1)} %refs_1_.1, bf16[96,192]{1,0:T(8,128)(2,1)} %refs_2_.1, ...), custom_call_target="tpu_custom_call" | custom-call | tf_op jit(solution)/shard_map/pallas_call | solution.py:1555
  187.6 9.1 %shard_map.297 = (bf16[8,256,768]{2,1,0:T(8,128)(2,1)}, f32[8,256,768]{2,1,0:T(8,128)}, f32[96,192]{1,0:T(8,128)}, f32[96,192]{1,0:T(8,128)}, f32[96,192]{1,0:T(...) custom-call(bf16[8,256,768]{2,1,0:T(8,128)(2,1)} %get-tuple-element., ...), custom_call_target="tpu_custom_call" | custom-call | tf_op jit(solution)/shard_map/pallas_call | solution.py:1607

commit v5 on v4

--- a/solution.py
+++ b/solution.py
@@ -812,7 +812,7 @@
     shards = [None] + take(2)
     vectors, column_biases = take(6), take(3)
     rows_out = take(2)
-    owned = take(3)
+    owned_out = take(3)
     small_out = next(it)
     full = take(3)
     pack_all, vecs, cold = take(3)
@@ -824,6 +824,8 @@
     p_first = take(n_ctx)
     first_land, second_land, ctx_land = take(3), take(3), take(3)
     side_land, small_b, ctx_small, small_c, pair_small, small_d, dp_small = take(7)
+    owned = take(3)
+    small_e = next(it)
     (
         own_sem, put_sem, rows_sem, line_sem, pair_sem, dp_sem, diag_dp_sem, diag_pair_sem, swap_send,
         swap_recv, first_sem, second_sem, ctx_sem, out_line, out_pair, out_side, small_sem,
@@ -960,7 +962,7 @@
         return ref.at[pp, shard_rows(dd * n_ctx + (z + k) % n_ctx)]
 
     def pair_leads(a, k):
-        return k == 1 if a == 0 else near.index(k) % 2 == 0
+        return a > 0 and near.index(k) % 2 == 0
 
     def scatter_start(a, ref, ks):
         for k in ks:
@@ -1024,6 +1026,7 @@
         last = n_ctx - 2
         arrive(ctx_land[a].at[last], ctx_sem.at[a, last])
         owned[a][...] = ref[p, shard_rows(own_row), :].astype(F32) + ctx_land[a][last].astype(F32)
+        pltpu.make_async_copy(owned[a], owned_out[a], own_sem.at[8 + a]).start()
 
     near = [k for h in strides for k in range(h, n_ctx, 2 * h)] + [0]
     early, late = near[:two], near[two:]
@@ -1107,10 +1110,11 @@
         own_pack[i : i + 1, :share] = vectors[i][...].astype(F32)
     row = 6
     for ref in column_biases:
-        n = ref.shape[1]
+        n = ref.shape[0]
+        line = ref[...].astype(F32).reshape(1, n)
         for w in range(0, n, 128):
             m = min(128, n - w)
-            own_pack[row : row + 1, :m] = ref[:, w : w + m].astype(F32)
+            own_pack[row : row + 1, :m] = line[:, w : w + m]
             row += 1
     small[...] = jnp.zeros_like(small)
     here.barrier(True)
@@ -1241,6 +1245,8 @@
         for b in range(n_ctx):
             out[:, b * block : (b + 1) * block] = ref[b * block : (b + 1) * block, :].T
 
+    gather_turn(2)
+    gathered = len(sends.started)
     transposed(ogf, trb)
 
     @pl.loop(0, width // step)
@@ -1249,8 +1255,6 @@
         for i in range(n_pair):
             dwd[i, rows, :] = nn_dot(trb[rows, :], act[i]).astype(BF16)
 
-    gather_turn(2)
-    gathered = len(sends.started)
     scatter_start(2, dwd, near)
 
     def slope_back(i, b):
@@ -1419,9 +1423,10 @@
         sends.go(small_b, pair_small.at[k - 1], small_sem.at[2, k - 1], here.other_pair(k)[1])
     scatter_turn(0, full[0], early)
     out_cross(0)
+    out_hop(1, others[:1])
     scatter_line(0, full[0], early)
     scatter_turn(0, full[0], late)
-    out_hop(1, others)
+    out_hop(1, others[1:])
     scatter_across(1, full[1])
     total = small_b[...]
     for k in range(1, n_pair):
@@ -1448,10 +1453,15 @@
     for k in range(1, n_ctx):
         arrive(ctx_small.at[k - 1], small_sem.at[1, k - 1])
         total = total + ctx_small[k - 1]
-    small_out[...] = total
+    small_e[...] = total
+    small_copy = pltpu.make_async_copy(small_e, small_out, own_sem.at[11])
+    small_copy.start()
     out_end(1)
     lo_copy.wait()
     tg_copy.wait()
+    small_copy.wait()
+    for a in range(3):
+        pltpu.make_async_copy(owned[a], owned_out[a], own_sem.at[8 + a]).wait()
 
     @pl.loop(0, n_ctx)
     def _(b):
@@ -1531,9 +1541,11 @@
         vm((16, width), F32),
         vm((n_dp - 1, 16, width), F32),
     ]
+    scratch += [vm((share, w), F32) for w in widths]
+    scratch += [vm((16, width), F32)]
     most = max(n_dp, n_ctx, n_pair)
     scratch += [
-        dma((8,)),
+        dma((12,)),
         dma((260,)),
         dma((2, n_ctx)),
         dma((4, n_ctx)),
@@ -1556,7 +1568,7 @@
         functools.partial(fused_body, sizes, (half, width, share, cols, fw)),
         out_shape=out_shape,
         in_specs=[any_spec] * 2 + [vmem_spec] * 4 + [any_spec] * 2 + [vmem_spec] * 9,
-        out_specs=[any_spec] * 2 + [vmem_spec] * 4,
+        out_specs=[any_spec] * 6,
         scratch_shapes=scratch,
         compiler_params=pltpu.CompilerParams(
             collective_id=3, has_side_effects=True, vmem_limit_bytes=67043328
@@ -1565,32 +1577,78 @@
 
 
 def finish_body(n_ctx, share, cols, *refs):
-    lo_in, tg_in, attn, up, down, small = refs[:6]
+    lo_in, tg_in, attn_in, up_in, down_in, small_in = refs[:6]
     lo, tg, dq, dk, dv, do, du, dd = refs[6:14]
     vectors = refs[14:20]
     shifts = refs[20:22]
     up_shift = refs[22]
-    lo[...] = lo_in[...]
-    tg[...] = tg_in[...].astype(F32)
+    lo_held, tg_held, tg_wide, attn, up, down, small = refs[23:30]
+    narrow = refs[30:34]
+    in_sem, out_sem, more_in, more_out = refs[34:]
     row = lax.axis_index("dp") * n_ctx + lax.axis_index("ctx")
     pair = lax.axis_index("tp") // 2
     width = small.shape[1]
-
-    @pl.when(pl.program_id(0) == 0)
-    def _():
-        for i, ref in enumerate((dq, dk, dv, do)):
-            ref[...] = attn[:, i * cols : (i + 1) * cols]
-        du[...] = up[...]
-        dd[...] = down[...]
-        turned = pltpu.roll(small[0:8, :], (width - row * share) % width, 1)
-        for i, ref in enumerate(vectors):
-            ref[...] = turned[i : i + 1, :share]
-        turned = pltpu.roll(small[0:8, :], (width - pair * cols) % width, 1)
-        for i, ref in enumerate(shifts):
-            ref[...] = turned[6 + i : 7 + i, :cols]
-        row_of = small[pl.ds(8 + pair, 1), :]
-        for i in range(up_shift.shape[0]):
-            up_shift[i : i + 1, :] = row_of[:, i * 128 : (i + 1) * 128]
+    seqs = lo_held.shape[0]
+    move = pltpu.make_async_copy
+
+    def rows_in(i, s):
+        source, held = ((tg_in, tg_held), (lo_in, lo_held))[i]
+        return move(source.at[s], held.at[s], in_sem.at[i, s])
+
+    def rows_out(i, s):
+        held, target = ((tg_wide, tg), (lo_held, lo))[i]
+        return move(held.at[s], target.at[s], out_sem.at[i, s])
+
+    takes = [
+        move(source, held, more_in.at[i])
+        for i, (source, held) in enumerate(((up_in, up), (down_in, down), (attn_in, attn), (small_in, small)))
+    ]
+    gives = [
+        move(held, target, more_out.at[i])
+        for i, (held, target) in enumerate(zip((up, down, *narrow), (du, dd, dq, dk, dv, do)))
+    ]
+
+    @pl.loop(0, seqs)
+    def _(s):
+        rows_in(0, s).start()
+        rows_in(1, s).start()
+
+    for copy in takes:
+        copy.start()
+
+    @pl.loop(0, seqs)
+    def _(s):
+        rows_in(0, s).wait()
+        tg_wide[s] = tg_held[s].astype(F32)
+        rows_out(0, s).start()
+        rows_in(1, s).wait()
+        rows_out(1, s).start()
+
+    for i in range(2):
+        takes[i].wait()
+        gives[i].start()
+    takes[2].wait()
+    for i, ref in enumerate(narrow):
+        ref[...] = attn[:, i * cols : (i + 1) * cols]
+        gives[2 + i].start()
+    takes[3].wait()
+    turned = pltpu.roll(small[0:8, :], (width - row * share) % width, 1)
+    for i, ref in enumerate(vectors):
+        ref[...] = turned[i : i + 1, :share]
+    turned = pltpu.roll(small[0:8, :], (width - pair * cols) % width, 1)
+    for i, ref in enumerate(shifts):
+        ref[...] = turned[6 + i : 7 + i, :cols]
+    row_of = small[pl.ds(8 + pair, 1), :]
+    for i in range(up_shift.shape[0]):
+        up_shift[i : i + 1, :] = row_of[:, i * 128 : (i + 1) * 128]
+
+    @pl.loop(0, seqs)
+    def _(s):
+        rows_out(0, s).wait()
+        rows_out(1, s).wait()
+
+    for copy in gives:
+        copy.wait()
 
 
 def finish_call(sizes, cols, lo, tg, attn, up, down, small):
@@ -1598,25 +1656,34 @@
     seqs, block, width = lo.shape
     share = attn.shape[0]
     shape = jax.ShapeDtypeStruct
-    rows = pl.BlockSpec((1, block, width), lambda i: (i, 0, 0))
-
-    def whole(s):
-        return pl.BlockSpec(s, lambda i: (0, 0))
-
+    any_spec = pl.BlockSpec(memory_space=pl.ANY)
+    vmem_spec = pl.BlockSpec(memory_space=pltpu.VMEM)
+    vm = pltpu.VMEM
+    dma = pltpu.SemaphoreType.DMA
     out_tail = [(share, cols)] * 4 + [up.shape] * 2 + [(1, share)] * 6 + [(1, cols)] * 2 + [(up.shape[1] // 128, 128)]
     return pl.pallas_call(
         functools.partial(finish_body, n_ctx, share, cols),
-        grid=(seqs,),
         out_shape=[shape(lo.shape, BF16), shape(lo.shape, F32)] + [shape(s, F32) for s in out_tail],
-        in_specs=[rows, rows] + [whole(x.shape) for x in (attn, up, down, small)],
-        out_specs=[rows, rows] + [whole(s) for s in out_tail],
+        in_specs=[any_spec] * 6,
+        out_specs=[any_spec] * 8 + [vmem_spec] * 9,
+        scratch_shapes=[
+            vm(lo.shape, BF16),
+            vm(lo.shape, BF16),
+            vm(lo.shape, F32),
+            vm(attn.shape, F32),
+            vm(up.shape, F32),
+            vm(down.shape, F32),
+            vm(small.shape, F32),
+        ]
+        + [vm((share, cols), F32)] * 4
+        + [dma((2, seqs)), dma((2, seqs)), dma((4,)), dma((6,))],
     )(lo, tg, attn, up, down, small)
 
 
 def fused_layer(sizes, tokens, out_grad, shards, vectors, column_biases):
     cols = shards[0].shape[1]
-    lines = [v.reshape(1, -1) for v in (*vectors, *column_biases)]
-    results = fused_call(sizes, tokens, out_grad, shards, lines[:6], lines[6:])
+    lines = [v.reshape(1, -1) for v in vectors]
+    results = fused_call(sizes, tokens, out_grad, shards, lines, column_biases)
     final = finish_call(sizes, cols, *results)
     return (*final[:8], *[v.reshape(-1) for v in final[8:]])
 
@@ -1651,7 +1718,7 @@
     row = lax.axis_index("dp") * n_ctx + lax.axis_index("ctx")
     shards = (query_weight, key_weight, value_weight, output_weight, up_weight, down_weight)
     vectors = (norm1_gain, norm1_bias, output_bias, norm2_gain, norm2_bias, down_bias)
-    if share % 16 == 0 and n_ctx % 2 == 0:
+    if share % 16 == 0 and n_ctx % 4 == 0 and n_ctx & (n_ctx - 1) == 0:
         return fused_layer(
             sizes, tokens, out_grad, shards, vectors, (query_bias, value_bias, up_bias)
         )

time: 200 us -> 190 us (0.950)
  Pallas kernels: 192 us -> 186 us
  local copies, waits for them, and re-layouts: 3.7 us -> 0 us
    pallas_call x1, Pallas kernels: 183 us -> 178 us  [fused_call(): pl.pallas_call(functools.partial(fused_body, sizes, (half, width, share,...]
    reshape x3 -> x0, local copies, waits for them, and re-layouts: 3.7 us -> none  [fused_layer(): lines = [v.reshape(1, -1) for v in (*vectors, *column_biases)]]
where the time goes in v5:
time: 190 us; the launch traced here: 186 us
  Pallas kernels  186 us (98%)
    pallas_call x1, Pallas kernels, fused_call(): pl.pallas_call(functools.partial(fused_body, sizes, (half, width, share,...  178 us
    pallas_call x1, Pallas kernels, finish_call(): pl.pallas_call(functools.partial(finish_body, n_ctx, share, cols), out_sh...  7.42 us

profile of v5, /device:TPU:25, one launch (start us, length us, event | category | flops | bytes accessed | tf_op | source)
XLA Modules:
  0.0 186.4 jit_solution(5097690692202430422)
XLA Ops:
  0.7 178.1 %shard_map.296 = (bf16[8,256,768]{2,1,0:T(8,128)(2,1)}, bf16[8,256,768]{2,1,0:T(8,128)(2,1)}, f32[96,768]{1,0:T(8,128)}, f32[96,768]{1,0:T(8,128)}, f32[96,768]{1,0:T(8,128)}, /*index=5*/f32[16,768]{1,0:T(8,128)}) custom-call(bf16[8,256,768]{2,1,0:T(8,128)(2,1)} %refs_0_.1, bf16[8,256,768]{2,1,0:T(8,128)(2,1)} %refs_1_.1, bf16[96,192]{1,0:T(8,128)(2,1)} %refs_2_.1, ...), custom_call_target="tpu_custom_call" | custom-call | tf_op jit(solution)/shard_map/pallas_call | solution.py:1567
  178.8 7.4 %shard_map.297 = (bf16[8,256,768]{2,1,0:T(8,128)(2,1)}, f32[8,256,768]{2,1,0:T(8,128)}, f32[96,192]{1,0:T(8,128)}, f32[96,192]{1,0:T(8,128)}, f32[96,192]{1,0:T(...) custom-call(bf16[8,256,768]{2,1,0:T(8,128)(2,1)} %get-tuple-element., ...), custom_call_target="tpu_custom_call" | custom-call | tf_op jit(solution)/shard_map/pallas_call | solution.py:1664

commit v6 on v5

--- a/solution.py
+++ b/solution.py
@@ -829,8 +829,8 @@
     (
         own_sem, put_sem, rows_sem, line_sem, pair_sem, dp_sem, diag_dp_sem, diag_pair_sem, swap_send,
         swap_recv, first_sem, second_sem, ctx_sem, out_line, out_pair, out_side, small_sem,
-        side_sem,
-    ) = take(18)
+        side_sem, cross_pair, cross_dp,
+    ) = take(20)
     partner = here.partner()
     own_row = d * n_ctx + z
     mine = p * n_ctx + z
@@ -886,6 +886,15 @@
             zz = (q + 2 * h * i) % n_ctx
             arrive(slot(a, p, d, zz), line_sem.at[a, zz])
 
+    def gather_cross(a, first):
+        for i in range(n_ctx // 2):
+            zz = (first + 2 * i) % n_ctx
+            piece = slot(a, p, d, zz)
+            for k in range(1, n_pair):
+                sends.go(piece, piece, cross_pair.at[a, p, zz], here.other_pair(k)[1])
+            for k in range(1, n_dp):
+                sends.go(piece, piece, cross_dp.at[a, d, zz], here.other_dp(k)[1])
+
     def gather_start(a):
         gather_give(a, strides[-1])
 
@@ -893,27 +902,26 @@
         for h in reversed(strides[:-1]):
             gather_take(a, 2 * h)
             gather_give(a, h)
-
-    def gather_hop(a):
         if a > 0:
             gather_own[a].wait()
+        gather_cross(a, z)
+
+    def gather_hop(a):
         gather_take(a, 1)
-        group = slot(a, p, d, 0, n_ctx)
-        for k in range(1, n_pair):
-            sends.go(group, group, pair_sem.at[a, p], here.other_pair(k)[1])
-        for k in range(1, n_dp):
-            sends.go(group, group, dp_sem.at[a, d], here.other_dp(k)[1])
+        gather_cross(a, flipped(1)[0])
 
     def gather_turn(a):
         for k in range(1, n_pair):
             pp = here.other_pair(k)[0]
-            arrive(slot(a, pp, d, 0, n_ctx), pair_sem.at[a, pp])
+            for zz in range(n_ctx):
+                arrive(slot(a, pp, d, zz), cross_pair.at[a, pp, zz])
             first = slot(a, pp, d, 0, two)
             for j in range(1, n_dp):
                 sends.go(first, first, diag_dp_sem.at[a, pp, d], here.other_dp(j)[1])
         for k in range(1, n_dp):
             dd = here.other_dp(k)[0]
-            arrive(slot(a, p, dd, 0, n_ctx), dp_sem.at[a, dd])
+            for zz in range(n_ctx):
+                arrive(slot(a, p, dd, zz), cross_dp.at[a, dd, zz])
             second = slot(a, p, dd, two, n_ctx - two)
             for j in range(1, n_pair):
                 sends.go(second, second, diag_pair_sem.at[a, p, dd], here.other_pair(j)[1])
@@ -1201,8 +1209,9 @@
         ssend[0, b] = whole[b % 2, far_side, :].astype(BF16)
         part_copy(2, 0, b).start()
         hid[b] = whole[b % 2, side_rows, :]
+        if b == 0:
+            gather_turn(1)
         if b == 1:
-            gather_turn(1)
             rows_start(1, out_grad, og)
         if b == 2:
             gather_hop(2)
@@ -1546,7 +1555,7 @@
     most = max(n_dp, n_ctx, n_pair)
     scratch += [
         dma((12,)),
-        dma((260,)),
+        dma((300,)),
         dma((2, n_ctx)),
         dma((4, n_ctx)),
         dma((4, n_pair)),
@@ -1563,6 +1572,8 @@
         dma((2, seqs)),
         dma((4, most)),
         pltpu.SemaphoreType.REGULAR,
+        dma((3, n_pair, n_ctx)),
+        dma((3, n_dp, n_ctx)),
     ]
     return pl.pallas_call(
         functools.partial(fused_body, sizes, (half, width, share, cols, fw)),

time: 190 us -> 189 us (level)
  no operation moved by 1% of the time
where the time goes in v6:
time: 189 us; the launch traced here: 187 us
  Pallas kernels  186 us (98%)
    pallas_call x1, Pallas kernels, fused_call(): pl.pallas_call(functools.partial(fused_body, sizes, (half, width, share,...  178 us
    pallas_call x1, Pallas kernels, finish_call(): pl.pallas_call(functools.partial(finish_body, n_ctx, share, cols), out_sh...  7.42 us

profile of v6, /device:TPU:25, one launch (start us, length us, event | category | flops | bytes accessed | tf_op | source)
XLA Modules:
  0.0 186.7 jit_solution(1897728677454954266)
XLA Ops:
  0.7 178.4 %shard_map.296 = (bf16[8,256,768]{2,1,0:T(8,128)(2,1)}, bf16[8,256,768]{2,1,0:T(8,128)(2,1)}, f32[96,768]{1,0:T(8,128)}, f32[96,768]{1,0:T(8,128)}, f32[96,768]{1,0:T(8,128)}, /*index=5*/f32[16,768]{1,0:T(8,128)}) custom-call(bf16[8,256,768]{2,1,0:T(8,128)(2,1)} %refs_0_.1, bf16[8,256,768]{2,1,0:T(8,128)(2,1)} %refs_1_.1, bf16[96,192]{1,0:T(8,128)(2,1)} %refs_2_.1, ...), custom_call_target="tpu_custom_call" | custom-call | tf_op jit(solution)/shard_map/pallas_call | solution.py:1578
  179.1 7.4 %shard_map.297 = (bf16[8,256,768]{2,1,0:T(8,128)(2,1)}, f32[8,256,768]{2,1,0:T(8,128)}, f32[96,192]{1,0:T(8,128)}, f32[96,192]{1,0:T(8,128)}, f32[96,192]{1,0:T(...) custom-call(bf16[8,256,768]{2,1,0:T(8,128)(2,1)} %get-tuple-element., ...), custom_call_target="tpu_custom_call" | custom-call | tf_op jit(solution)/shard_map/pallas_call | solution.py:1675

commit v7 on v6

--- a/solution.py
+++ b/solution.py
@@ -1446,9 +1446,6 @@
         sends.go(small_c, dp_small.at[k - 1], small_sem.at[3, k - 1], here.other_dp(k)[1])
     scatter_line(0, full[0], late)
     scatter_across(0, full[0])
-    scatter_end(2, dwd)
-    scatter_end(1, full[1])
-    out_end(0)
     total = small_c[...]
     for k in range(1, n_dp):
         arrive(dp_small.at[k - 1], small_sem.at[3, k - 1])
@@ -1457,6 +1454,9 @@
     for k in range(1, n_ctx):
         sends.go(small_d, ctx_small.at[k - 1], small_sem.at[1, k - 1], here.other_ctx(k)[1])
     out_cross(1)
+    scatter_end(2, dwd)
+    scatter_end(1, full[1])
+    out_end(0)
     scatter_end(0, full[0])
     total = small_d[...]
     for k in range(1, n_ctx):

time: 189 us -> 189 us (level)
  no operation moved by 1% of the time
where the time goes in v7:
time: 189 us; the launch traced here: 187 us
  Pallas kernels  186 us (98%)
    pallas_call x1, Pallas kernels, fused_call(): pl.pallas_call(functools.partial(fused_body, sizes, (half, width, share,...  178 us
    pallas_call x1, Pallas kernels, finish_call(): pl.pallas_call(functools.partial(finish_body, n_ctx, share, cols), out_sh...  7.42 us

profile of v7, /device:TPU:25, one launch (start us, length us, event | category | flops | bytes accessed | tf_op | source)
XLA Modules:
  0.0 186.7 jit_solution(15504703777234021776)
XLA Ops:
  0.7 178.4 %shard_map.296 = (bf16[8,256,768]{2,1,0:T(8,128)(2,1)}, bf16[8,256,768]{2,1,0:T(8,128)(2,1)}, f32[96,768]{1,0:T(8,128)}, f32[96,768]{1,0:T(8,128)}, f32[96,768]{1,0:T(8,128)}, /*index=5*/f32[16,768]{1,0:T(8,128)}) custom-call(bf16[8,256,768]{2,1,0:T(8,128)(2,1)} %refs_0_.1, bf16[8,256,768]{2,1,0:T(8,128)(2,1)} %refs_1_.1, bf16[96,192]{1,0:T(8,128)(2,1)} %refs_2_.1, ...), custom_call_target="tpu_custom_call" | custom-call | tf_op jit(solution)/shard_map/pallas_call | solution.py:1578
  179.1 7.4 %shard_map.297 = (bf16[8,256,768]{2,1,0:T(8,128)(2,1)}, f32[8,256,768]{2,1,0:T(8,128)}, f32[96,192]{1,0:T(8,128)}, f32[96,192]{1,0:T(8,128)}, f32[96,192]{1,0:T(...) custom-call(bf16[8,256,768]{2,1,0:T(8,128)(2,1)} %get-tuple-element., ...), custom_call_target="tpu_custom_call" | custom-call | tf_op jit(solution)/shard_map/pallas_call | solution.py:1675
